TPU v7x, 256 devices: a whole 4x4x8 slice. The times are simulated.
256 devices in a mesh: src: 32 (over z_hi, x, core), tgt: 8 (over y, z_lo).
Axes of the slice: x: 4, y: 4, z: 8 (z_hi: 4, z_lo: 2; z = z_hi * 2 + z_lo), core: 2. Of those that a mesh axis runs over, the one named last changes fastest.
Arguments:
- upstream: bfloat16 [256, 128, 324], P('src'), may hold values from -6 to 6
- centers: int32 [2, 256, 128], P(None, 'src'), may hold values from -4 to 259, as said below
- post_relu: bfloat16 [256, 128, 128], P('src'), as said below
- conv_input: bfloat16 [256, 128, 128], P(('src', 'tgt')), may hold values from -6 to 6
- target_feats: bfloat16 [64, 256, 256], P('tgt'), may hold values from -6 to 6
- out_weight: bfloat16 [128, 256], replicated, may hold values from -0.5 to 0.5
- conv_weight: bfloat16 [3, 3, 128, 128], replicated, may hold values from -0.1875 to 0.1875
Outputs:
- tgt_grad: bfloat16 [64, 256, 256], P('tgt', 'src')
- act_grad: bfloat16 [256, 128, 128], P(('src', 'tgt'))
- out_wgrad: float32 [128, 256], replicated
- conv_wgrad: float32 [3, 3, 128, 128], replicated
Inputs may be any that keep to these rules, and one draw needn't show every extreme that they name: centers[0] is a target row from -4 to 67 and centers[1] a target column from -4 to 259; windows may reach outside the target image. `post_relu`: entries are zero or positive.
All inputs are finite; a program needn't handle non-finite values.
Results may differ from a plain program's by a relative error of at most 0.0064.
Values may be sent and summed in bfloat16 or wider, within the bound.
No kernel may reach another device: no remote copies, remote signals or barrier semaphores. Data moves between devices by JAX's collectives and lax.ppermute only.
A program may use at most 64 MiB of HBM per device.

v0:
```python
import math

import jax
import jax.numpy as jnp
from jax import lax
from jax.sharding import PartitionSpec as P


def padded_2(array, sides, width):
    for axis, dim in sides:
        devices, length = (lax.axis_size(axis), array.shape[dim])
        up = [(i, (i + 1) % devices) for i in range(devices - 1)]
        down = [(j, i) for i, j in up]
        last = lax.slice_in_dim(array, length - width, length, axis=dim)
        first = lax.slice_in_dim(array, 0, width, axis=dim)
        before = lax.ppermute(last, axis, up)
        after = lax.ppermute(first, axis, down)
        array = jnp.concatenate([before, array, after], axis=dim)
    return array


def corr_block(center_rows, center_cols, grad_rows, row_start, row_total, col_total):
    source_total = grad_rows.shape[0]
    row_ids = row_start + jnp.arange(row_total, dtype=jnp.int32)
    col_ids = jnp.arange(col_total, dtype=jnp.int32)
    offsets = jnp.arange(9, dtype=jnp.int32)
    row_parts = []
    col_parts = []
    for level_no in range(4):
        level_step = 2**level_no
        row_off = (
            jnp.floor_divide(row_ids, level_step)[None, :]
            - jnp.floor_divide(center_rows, level_step)[:, None]
            + 4
        )
        col_off = (
            jnp.floor_divide(col_ids, level_step)[None, :]
            - jnp.floor_divide(center_cols, level_step)[:, None]
            + 4
        )
        row_hot = jnp.where(
            row_off[:, None, :] == offsets[None, :, None], 0.25**level_no, 0.0
        ).astype(jnp.float32)
        col_hot = jnp.where(col_off[:, None, :] == offsets[None, :, None], 1.0, 0.0).astype(
            jnp.float32
        )
        level_grads = (
            grad_rows[:, 81 * level_no : 81 * (level_no + 1)]
            .astype(jnp.float32)
            .reshape(source_total, 9, 9)
        )
        row_parts.append(row_hot)
        col_parts.append(jnp.einsum("sab,sbx->sax", level_grads, col_hot))
    row_table = jnp.concatenate(row_parts, axis=1)
    col_table = jnp.concatenate(col_parts, axis=1)
    return jnp.einsum("say,sax->syx", row_table, col_table).astype(jnp.bfloat16)


def hidden_grads(src_grad, relu_rows, out_weight):
    hidden = jnp.einsum("rwd,cd->rwc", src_grad, out_weight, preferred_element_type=jnp.float32)
    block_grad = jnp.where(relu_rows > 0, hidden, 0.0).astype(jnp.bfloat16)
    out_term = jnp.einsum("rwc,rwd->cd", relu_rows, src_grad, preferred_element_type=jnp.float32)
    return (block_grad, out_term)


def conv_back(grad_pad, inputs, kernel):
    row_total = inputs.shape[0]
    width_total = inputs.shape[1]
    padded = jnp.pad(grad_pad, ((0, 0), (1, 1), (0, 0)))
    act_sum = jnp.zeros(inputs.shape, jnp.float32)
    tap_grads = []
    for row_tap in range(3):
        for col_tap in range(3):
            window = padded[
                2 - row_tap : 2 - row_tap + row_total, 2 - col_tap : 2 - col_tap + width_total
            ]
            act_sum = act_sum + jnp.einsum(
                "rwo,io->rwi", window, kernel[row_tap, col_tap], preferred_element_type=jnp.float32
            )
            tap_grads.append(
                jnp.einsum("rwi,rwo->io", inputs, window, preferred_element_type=jnp.float32)
            )
    channels = inputs.shape[2]
    return (act_sum, jnp.stack(tap_grads).reshape(3, 3, channels, channels))


def body(upstream, centers, post_relu, conv_input, target_feats, out_weight, conv_weight):
    src_rows, src_width, lookups = upstream.shape
    tgt_rows, tgt_width, feat_width = target_feats.shape
    channels = post_relu.shape[2]
    src_devices = lax.axis_size("src")
    tgt_devices = lax.axis_size("tgt")
    row_first = lax.axis_index("tgt") * tgt_rows
    inv_root = 1.0 / math.sqrt(feat_width)
    source_total = src_rows * src_width
    flat_grads = upstream.reshape(source_total, lookups)
    flat_rows = centers[0].reshape(source_total)
    flat_cols = centers[1].reshape(source_total)
    block_size = math.gcd(256, source_total)

    def build_block(block_no):
        first_row = block_no * block_size
        return corr_block(
            lax.dynamic_slice_in_dim(flat_rows, first_row, block_size),
            lax.dynamic_slice_in_dim(flat_cols, first_row, block_size),
            lax.dynamic_slice_in_dim(flat_grads, first_row, block_size, 0),
            row_first,
            tgt_rows,
            tgt_width,
        )

    corr_grad = lax.map(build_block, jnp.arange(source_total // block_size, dtype=jnp.int32))
    corr_grad = corr_grad.reshape(source_total, tgt_rows, tgt_width)
    corr_flat = corr_grad.reshape(source_total, tgt_rows * tgt_width)
    src_feats = jnp.dot(
        post_relu.reshape(source_total, channels), out_weight, preferred_element_type=jnp.float32
    ).astype(jnp.bfloat16)
    flat_targets = target_feats.reshape(tgt_rows * tgt_width, feat_width)
    corr_piece = lax.slice_in_dim(
        corr_grad, 0, tgt_width // src_devices * lax.axis_size("src"), axis=2
    )
    target_share = lax.psum_scatter(
        jnp.einsum("syc,sd->cyd", corr_piece, src_feats, preferred_element_type=jnp.float32)
        * inv_root,
        "src",
        scatter_dimension=0,
        tiled=True,
    )
    tgt_grad = jnp.transpose(target_share, (1, 0, 2)).astype(jnp.bfloat16)
    tile_rows = src_rows // tgt_devices
    src_partial = jnp.dot(corr_flat, flat_targets, preferred_element_type=jnp.float32) * inv_root
    src_total = lax.psum(src_partial, "tgt")
    src_grad = src_total.reshape(src_rows, src_width, feat_width).astype(jnp.bfloat16)
    block_grad, out_term = hidden_grads(src_grad, post_relu, out_weight)
    grad_pad = padded_2(block_grad, (("src", 0),), 1)
    whole_input = lax.all_gather(conv_input, "tgt", axis=0, tiled=True)
    act_sum, conv_term = conv_back(grad_pad, whole_input, conv_weight)
    out_total, conv_total = lax.psum((out_term, conv_term), "src")
    act_grad = lax.dynamic_slice_in_dim(
        act_sum, lax.axis_index("tgt") * tile_rows, tile_rows, 0
    ).astype(jnp.bfloat16)
    row_count = float(src_rows * src_devices)
    return (tgt_grad, act_grad, out_total / row_count, conv_total / row_count)


def solution(mesh):
    placed = (
        P("src", None, None),
        P(None, "src", None),
        P("src", None, None),
        P(("src", "tgt"), None, None),
        P("tgt", None, None),
        P(),
        P(),
    )
    return jax.shard_map(
        body,
        mesh=mesh,
        in_specs=placed,
        out_specs=(P("tgt", "src", None), P(("src", "tgt"), None, None), P(), P()),
        check_vma=False,
    )
```

profile of v0, /device:TPU:8, one launch (start us, length us, event | category | flops | bytes accessed | tf_op | source)
XLA Modules:
  0.0 605.3 jit_solution(13785077860471548321)
XLA Ops:
  8.0 1.1 pad.23
  9.3 84.5 %while.13 = (s32[]{:T(128)}, bf16[4,256,8,256]{3,2,1,0:T(8,128)(2,1)}, s32[]{:T(128)}, s32[4]{0:T(128)S(1)}, s32[1024]{0:T(1024)S(1)}, /*index=5*/bf16[1024,324]...) while((s32[]{:T(128)}, ...), condition=%wide.region_1.2_spmd, body=%wide.region_0.1_spmd.sunk | while | flops 104745304 | bytes 30385264 | solution.py:112
  12.9 2.0 fusion.171
  15.1 1.0 copy.86
  16.1 2.1 fusion.172
  19.3 2.0 fusion.174
  24.7 5.7 fusion.175
  34.0 2.0 fusion.171
  37.2 2.1 fusion.172
  40.4 2.0 fusion.174
  45.9 5.7 fusion.175
  55.1 2.0 fusion.171
  58.3 2.1 fusion.172
  61.6 2.0 fusion.174
  67.0 5.7 fusion.175
  76.2 2.0 fusion.171
  79.4 2.1 fusion.172
  82.7 2.0 fusion.174
  88.1 5.7 fusion.175
  93.8 3.7 copy.74
  97.5 1.3 convolution_multiply_fusion
  98.8 75.3 %all-reduce.6 = bf16[1024,256]{1,0:T(8,128)(2,1)S(1)} all-reduce(f32[1024,256]{1,0:T(8,128)S(1)} %convolution_multiply_fusion), channel_id=1, replica_groups=mesh['src'=32,'tgt'=8] {'tgt'}, use_global_device_ids=true, to_apply=%region_3.4 | all-reduce | flops 262144 | bytes 1572864 | tf_op jit(solution)/shard_map/psum | solution.py:132
  174.4 1.3 collective-permute-start
  175.7 1.3 collective-permute-start.1
  177.0 1.0 convolution_bitcast_fusion
  178.0 28.5 %all_gather.3 = bf16[8,128,128]{2,1,0:T(8,128)(2,1)S(1)} all-gather(bf16[1,128,128]{2,1,0:T(8,128)(2,1)S(1)} %copy-done.7), channel_id=1, replica_groups=mesh['src'=32,'tgt'=8] {'tgt'}, dimensions={0}, use_global_device_ids=true | all-gather | bytes 294912 | tf_op jit(solution)/shard_map/all_gather | solution.py:136
  209.2 1.1 copy.58
  210.3 5.6 multiply_bitcast_fusion
  215.9 3.1 copy.47
  221.7 280.7 %all-reduce.5.cloned.1.call-done = (f32[128,256]{0,1:T(8,128)}, f32[3,3,128,128]{3,2,1,0:T(8,128)}) async-done(((f32[128,256]{0,1:T(8,128)}, f32[3,3,128,128]{3,2,1,0:T(8,128)}), (f32[128,256]{0,1:T(8,128)}, f32[3,3,128,128]{3,2,1,0:T(8,128)})) %all-reduce.5.cloned.1.call-update) | async-done | bytes 720912 | tf_op jit(solution)/shard_map/psum | solution.py:138
  504.1 1.9 broadcast_multiply_fusion
  506.0 91.0 %reduce-scatter.2.cloned.1.call-done = f32[8,8,256]{2,1,0:T(8,128)} async-done(((f32[256,8,256]{2,1,0:T(8,128)}), f32[8,8,256]{2,1,0:T(8,128)}) %reduce-scatter.2.cloned.1.call-update) | async-done | bytes 65552 | tf_op jit(solution)/shard_map/reduce_scatter | solution.py:122
  (211 shorter events, 42.4 us)
Async XLA Ops:
  7.2 90.3 %copy-start = (bf16[8,256,256]{2,1,0:T(8,128)(2,1)S(1)}, bf16[8,256,256]{2,1,0:T(8,128)(2,1)}, u32[]{:S(2)}) copy-start(bf16[8,256,256]{2,1,0:T(8,128)(2,1)} %param.13) | copy-start | bytes 3145732
  7.2 495.2 %all-reduce.5.cloned.1.call-start = ((), (), s32[]{:S(2)}) async-start(), calls=%async_computation.2 | async-start | bytes 1441792 | tf_op jit(solution)/shard_map/psum | solution.py:138
  9.3 2.5 copy-start.1
  22.5 1.6 copy-start.8
  22.5 2.2 copy-start.9
  24.7 5.7 copy-start.2
  30.4 2.5 copy-start.1
  43.6 1.6 copy-start.8
  43.6 2.2 copy-start.9
  45.9 5.7 copy-start.2
  51.6 2.5 copy-start.1
  64.8 1.6 copy-start.8
  64.8 2.2 copy-start.9
  67.0 5.7 copy-start.2
  72.7 2.5 copy-start.1
  85.9 1.6 copy-start.8
  85.9 2.2 copy-start.9
  88.1 5.7 copy-start.2
  97.5 76.6 %copy-start.3 = (bf16[8,128,128]{2,1,0:T(8,128)(2,1)S(1)}, bf16[8,128,128]{2,1,0:T(8,128)(2,1)}, u32[]{:S(2)}) copy-start(bf16[8,128,128]{2,1,0:T(8,128)(2,1)} %param.11) | copy-start | bytes 786436
  97.5 76.6 %copy-start.5 = (bf16[128,256]{1,0:T(8,128)(2,1)S(1)}, bf16[128,256]{1,0:T(8,128)(2,1)}, u32[]{:S(2)}) copy-start(bf16[128,256]{1,0:T(8,128)(2,1)} %param.14) | copy-start | bytes 196612
  97.5 80.6 %copy-start.7 = (bf16[1,128,128]{2,1,0:T(8,128)(2,1)S(1)}, bf16[1,128,128]{2,1,0:T(8,128)(2,1)}, u32[]{:S(2)}) copy-start(bf16[1,128,128]{2,1,0:T(8,128)(2,1)} %param.12) | copy-start | bytes 98308
  174.4 32.1 %collective-permute-start = (bf16[1,128,128]{2,1,0:T(8,128)(2,1)S(1)}, bf16[1,128,128]{2,1,0:T(8,128)(2,1)S(1)}, u32[]{:S(2)}, u32[]{:S(2)}) collective-permute-start(bf16[1,128,128]{2,1,0:T(8,128)(2,1)S(1)} %get-tuple-element.192), channel_id=1, source_target_pairs={{0,8},{8,16},{16,24},{24,32},{32,40},{40,48},{48,56},{56,64},{64,7... | collective-permute-start | bytes 98312 | tf_op jit(solution)/shard_map/ppermute | solution.py:16
  175.7 30.8 %collective-permute-start.1 = (bf16[1,128,128]{2,1,0:T(8,128)(2,1)S(1)}, bf16[1,128,128]{2,1,0:T(8,128)(2,1)S(1)}, u32[]{:S(2)}, u32[]{:S(2)}) collective-permute-start(bf16[1,128,128]{2,1,0:T(8,128)(2,1)S(1)} %get-tuple-element.193), channel_id=1, source_target_pairs={{8,0},{16,8},{24,16},{32,24},{40,32},{48,40},{56,48},{64,56},{72,6... | collective-permute-start | bytes 98312 | tf_op jit(solution)/shard_map/ppermute | solution.py:17
  206.7 3.6 copy-start.6
  210.2 386.7 %reduce-scatter.2.cloned.1.call-start = ((), (), s32[]{:S(2)}) async-start(), calls=%async_computation.1 | async-start | bytes 2162688 | tf_op jit(solution)/shard_map/reduce_scatter | solution.py:122
  215.9 3.1 copy-start.4
Sparse Core Ops, SparseCore 0:
  210.4 292.0 all-reduce.4
  506.3 90.6 reduce-scatter.1
where the time goes:
time: 606 us; the launch traced here: 605 us
  waiting for transfers between devices  372 us (61%)
  blocking collectives  104 us (17%)
  matrix products  62.9 us (10%)
  local copies, waits for them, and re-layouts  38.5 us (6%)
  between operations  14.3 us (2%)
  other arithmetic  8.06 us (1%)
    psum x1, waiting for transfers between devices, body(): out_total, conv_total = lax.psum((out_term, conv_term), 'src')  281 us
    reduce_scatter x1, waiting for transfers between devices, body(): lax.psum_scatter(jnp.einsum('syc,sd->cyd', corr_piece, src_feats, preferr...  91 us
    psum x1, blocking collectives, body(): src_total = lax.psum(src_partial, 'tgt')  75.3 us
    all_gather x1, blocking collectives, body(): whole_input = lax.all_gather(conv_input, 'tgt', axis=0, tiled=True)  28.5 us
    dot_general x16, matrix products, corr_block(): col_parts.append(jnp.einsum('sab,sbx->sax', level_grads, col_hot))  27.5 us
    dot_general x4, matrix products, corr_block(): return jnp.einsum('say,sax->syx', row_table, col_table).astype(jnp.bfloat16)  22.8 us
    reshape x32, local copies, waits for them, and re-layouts, corr_block(): level_grads = grad_rows[:, 81 * level_no:81 * (level_no + 1)].astype(jnp....  16.4 us
  transfers between devices with their start and end apart: 4, of which 2 were waited for; matrix products, arithmetic and copies ran while one was open for 3% of the time, Pallas kernels for 0%

commit v1 on v0

v1 whole, which is shorter than its diff:
```python
import math

import jax
import jax.numpy as jnp
from jax import lax
from jax.experimental import pallas as pl
from jax.experimental.pallas import tpu as pltpu
from jax.sharding import Mesh, PartitionSpec as P

SRC = ("zh", "x", "c")
TGT = ("y", "zl")
ALL = SRC + TGT
NEAR = ("c", "y", "zl")
FAR = ("zh", "x")


def corr_kernel(first_ref, grads_ref, cents_ref, corr_ref, wide, level_sums):
    row_no = pl.program_id(0)
    tgt_rows = 8
    lanes = corr_ref.shape[1]
    tgt_width = corr_ref.shape[0] // tgt_rows

    @pl.when(row_no == 0)
    def _():
        wide[...] = grads_ref[...].astype(jnp.float32)

    tile = (tgt_rows, lanes)
    center_y = jnp.broadcast_to(cents_ref[0, pl.ds(row_no, 1), :], tile)
    center_x = jnp.broadcast_to(cents_ref[1, pl.ds(row_no, 1), :], tile)
    ys = first_ref[0] + lax.broadcasted_iota(jnp.int32, tile, 0)
    zero = jnp.zeros(tile, jnp.float32)

    def spread(level):
        row_off = lax.shift_right_arithmetic(ys, level) - (
            lax.shift_right_arithmetic(center_y, level) - 4
        )
        hits = [row_off == a for a in range(9)]
        picked = []
        for b in range(9):
            acc = zero
            for a in range(9):
                entry = wide[81 * level + 9 * a + b, pl.ds(row_no, 1), :]
                acc = jnp.where(hits[a], jnp.broadcast_to(entry, tile), acc)
            picked.append(acc * (0.25**level) if level else acc)
        start = lax.shift_right_arithmetic(center_x, level) - 4
        turn = start & 15
        block = lax.shift_right_arithmetic(start, 4)
        slots = picked + [zero] * 7
        for bit in (8, 4, 2, 1):
            on = (turn & bit) != 0
            slots = [jnp.where(on, slots[(i - bit) % 16], slots[i]) for i in range(16)]
        homes = [jnp.where(turn > j, block + 1, block) for j in range(16)]
        return slots, homes

    offset = 0
    coarse = None
    for level in (3, 2, 1):
        slots, homes = spread(level)
        cells = tgt_width >> level
        for j in range(16):
            for q in range(cells // 16):
                x = 16 * q + j
                value = jnp.where(homes[j] == q, slots[j], 0.0)
                if coarse is not None:
                    value = value + level_sums[coarse + (x >> 1)]
                level_sums[offset + x] = value
        coarse = offset
        offset += cells
    slots, homes = spread(0)
    for j in range(0, 16, 2):
        for q in range(tgt_width // 16):
            x = 16 * q + j
            under = level_sums[coarse + (x >> 1)]
            left = jnp.where(homes[j] == q, slots[j], 0.0) + under
            right = jnp.where(homes[j + 1] == q, slots[j + 1], 0.0) + under
            pair = jnp.concatenate([left, right], axis=0).astype(jnp.bfloat16)
            corr_ref[x * tgt_rows : (x + 2) * tgt_rows, :] = pair


def corr_transposed(upstream, centers, row_first, tgt_rows, tgt_width):
    src_rows, src_width, lookups = upstream.shape
    grads = jnp.transpose(upstream, (2, 0, 1))
    return pl.pallas_call(
        corr_kernel,
        out_shape=jax.ShapeDtypeStruct((tgt_width * tgt_rows, src_rows * src_width), jnp.bfloat16),
        grid_spec=pltpu.PrefetchScalarGridSpec(
            num_scalar_prefetch=1,
            grid=(src_rows,),
            in_specs=[
                pl.BlockSpec((lookups, src_rows, src_width), lambda r, f: (0, 0, 0)),
                pl.BlockSpec((2, src_rows, src_width), lambda r, f: (0, 0, 0)),
            ],
            out_specs=pl.BlockSpec((tgt_width * tgt_rows, src_width), lambda r, f: (0, r)),
            scratch_shapes=[
                pltpu.VMEM((lookups, src_rows, src_width), jnp.float32),
                pltpu.VMEM((tgt_width, tgt_rows, src_width), jnp.float32),
            ],
        ),
        compiler_params=pltpu.CompilerParams(dimension_semantics=("arbitrary",)),
        cost_estimate=pl.CostEstimate(flops=20_000_000, bytes_accessed=6_000_000, transcendentals=0),
        name="corr_build",
    )(row_first.reshape(1), grads, centers)


def shares(value, axes):
    count = lax.axis_size(axes)
    return lax.all_to_all(jnp.broadcast_to(value[None], (count,) + value.shape), axes, 0, 0)


def summed(parts):
    return jnp.sum(parts.astype(jnp.float32), axis=0)


def moved(array, step):
    zero = jnp.zeros((1,) + array.shape[1:], array.dtype)
    if step > 0:
        return jnp.concatenate([zero, array[:-1]], axis=0)
    return jnp.concatenate([array[1:], zero], axis=0)


def body(upstream, centers, post_relu, conv_input, target_feats, out_weight, conv_weight):
    src_rows, src_width, lookups = upstream.shape
    tgt_rows, tgt_width, width = target_feats.shape
    chans = post_relu.shape[2]
    source_total = src_rows * src_width
    src_devices = lax.axis_size(SRC)
    row_total = src_devices * src_rows
    inv_root = 1.0 / math.sqrt(width)
    tgt_at = lax.axis_index(TGT)
    core_at = lax.axis_index("c")
    f32, bf16 = jnp.float32, jnp.bfloat16

    up = [(i, i + 1) for i in range(row_total - 1)]
    down = [(j, i) for i, j in up]
    own_input = conv_input[0]
    input_before = lax.ppermute(own_input, ALL, up)
    input_after = lax.ppermute(own_input, ALL, down)

    corr = corr_transposed(upstream, centers, tgt_at * tgt_rows, tgt_rows, tgt_width)
    targets = jnp.transpose(target_feats, (1, 0, 2)).reshape(tgt_width * tgt_rows, width)
    relu_flat = post_relu.reshape(source_total, chans)
    src_part = (
        lax.dot_general(corr, targets, (((0,), (0,)), ((), ())), preferred_element_type=f32)
        * inv_root
    ).astype(bf16)
    hidden = lax.dot_general(
        src_part, out_weight, (((1,), (1,)), ((), ())), preferred_element_type=f32
    ).astype(bf16)
    hidden = lax.all_to_all(hidden.reshape(src_rows, src_width, chans), TGT, 0, 0)
    out_term = lax.dot_general(
        relu_flat, src_part, (((0,), (0,)), ((), ())), preferred_element_type=f32
    )

    feats = jnp.dot(relu_flat, out_weight, preferred_element_type=f32).astype(bf16)
    tgt_part = (
        jnp.dot(corr, feats, preferred_element_type=f32) * inv_root
    ).astype(bf16)
    far = lax.axis_size(FAR)
    block = tgt_width // src_devices * tgt_rows
    tgt_part = tgt_part.reshape(far, 2, block, width)
    given = lax.dynamic_index_in_dim(tgt_part, 1 - core_at, 1, keepdims=False)
    kept = lax.dynamic_index_in_dim(tgt_part, core_at, 1, keepdims=False)
    swap = [
        (s * 8 + t, (s ^ 1) * 8 + t) for s in range(src_devices) for t in range(lax.axis_size(TGT))
    ]
    taken = lax.ppermute(given, ALL, swap)
    both = (kept.astype(f32) + taken.astype(f32)).astype(bf16)
    tgt_grad = summed(lax.all_to_all(both, FAR, 0, 0))
    tgt_grad = jnp.transpose(
        tgt_grad.reshape(tgt_width // src_devices, tgt_rows, width), (1, 0, 2)
    ).astype(bf16)

    own_relu = lax.dynamic_index_in_dim(post_relu, tgt_at, 0, keepdims=False)
    block_grad = jnp.where(own_relu > 0, summed(hidden), 0.0).astype(bf16)

    near_input = jnp.concatenate([input_before, own_input, input_after], axis=1)
    near_grad = jnp.concatenate([moved(block_grad, -1), block_grad, moved(block_grad, 1)], axis=1)
    conv_term = lax.dot_general(
        near_input, near_grad, (((0,), (0,)), ((), ())), preferred_element_type=f32
    )
    near = lax.axis_size(NEAR)
    terms = jnp.concatenate(
        [
            conv_term.astype(bf16).reshape(near, 3 * chans // near, 3 * chans),
            jnp.pad(
                out_term.astype(bf16).reshape(near, chans // near, width),
                ((0, 0), (0, 0), (0, 3 * chans - width)),
            ),
        ],
        axis=1,
    )
    piece = summed(lax.all_to_all(terms, NEAR, 0, 0)).astype(bf16)
    piece = (summed(shares(piece, FAR)) / row_total).astype(bf16)
    totals = shares(piece, NEAR).astype(f32)
    conv_total = totals[:, : 3 * chans // near].reshape(3, chans, 3, chans)
    conv_total = jnp.transpose(conv_total, (0, 2, 1, 3))
    out_total = totals[:, 3 * chans // near :, :width].reshape(chans, width)

    grad_before = lax.ppermute(block_grad, ALL, up)
    grad_after = lax.ppermute(block_grad, ALL, down)
    taps = []
    for row in (grad_after, block_grad, grad_before):
        taps += [moved(row, -1), row, moved(row, 1)]
    act_grad = lax.dot_general(
        jnp.concatenate(taps, axis=1),
        jnp.transpose(conv_weight, (0, 1, 3, 2)).reshape(9 * chans, chans),
        (((1,), (0,)), ((), ())),
        preferred_element_type=f32,
    ).astype(bf16)[None]
    return (tgt_grad, act_grad, out_total, conv_total)


def solution(mesh):
    grid = Mesh(mesh.devices.reshape(4, 4, 2, 4, 2), ALL)
    placed = (
        P(SRC, None, None),
        P(None, SRC, None),
        P(SRC, None, None),
        P(ALL, None, None),
        P(TGT, None, None),
        P(),
        P(),
    )
    return jax.shard_map(
        body,
        mesh=grid,
        in_specs=placed,
        out_specs=(P(TGT, SRC, None), P(ALL, None, None), P(), P()),
        check_vma=False,
    )
```

time: 606 us -> 115 us (0.19)
  waiting for transfers between devices: 372 us -> 36.3 us
  blocking collectives: 104 us -> 0 us
  matrix products: 62.9 us -> 10 us
  starting transfers between devices: 2.66 us -> 53.1 us
  local copies, waits for them, and re-layouts: 38.5 us -> 4.49 us
  between operations: 14.3 us -> 0.91 us
  Pallas kernels: 0 us -> 6.54 us
    psum x1 -> x0, waiting for transfers between devices: 281 us -> none  [body(): out_total, conv_total = lax.psum((out_term, conv_term), 'src')]
    reduce_scatter x1 -> x0, waiting for transfers between devices: 91 us -> none  [body(): lax.psum_scatter(jnp.einsum('syc,sd->cyd', corr_piece, src_feats, preferr...]
    psum x1 -> x0, blocking collectives: 75.3 us -> none  [body(): src_total = lax.psum(src_partial, 'tgt')]
    dot_general x42 -> x6, matrix products: 62.9 us -> 10 us  [the longest x1 3.85 us: body(): lax.dot_general(corr, targets, (((0,), (0,)), ((), ())), preferred_elemen...]
    all_to_all x0 -> x5, starting transfers between devices: none -> 39.4 us  [the longest x2 19.3 us: shares(): lax.all_to_all(jnp.broadcast_to(value[None], (count,) + value.shape), axe...]
    all_to_all x0 -> x5, waiting for transfers between devices: none -> 34.4 us  [the longest x2 18.3 us: shares(): lax.all_to_all(jnp.broadcast_to(value[None], (count,) + value.shape), axe...]
    all_gather x1 -> x0, blocking collectives: 28.5 us -> none  [body(): whole_input = lax.all_gather(conv_input, 'tgt', axis=0, tiled=True)]
    reshape x33 -> x2, local copies, waits for them, and re-layouts: 17.4 us -> 0.9 us  [the longest x1 0.67 us: body(): out_total = totals[:, 3 * chans // near:, :width].reshape(chans, width)]
  transfers between devices with their start and end apart: 4 -> 10, of which waited for: 2 -> 5; matrix products, arithmetic and copies ran while one was open for 3% -> 8% of each run, Pallas kernels for 0% -> 0%
where the time goes in v1:
time: 115 us; the launch traced here: 113 us
  starting transfers between devices  53.1 us (46%)
  waiting for transfers between devices  36.3 us (32%)
  matrix products  10 us (9%)
  Pallas kernels  6.54 us (6%)
  local copies, waits for them, and re-layouts  4.49 us (4%)
  other arithmetic  2.07 us (2%)
    all_to_all x2, starting transfers between devices, shares(): lax.all_to_all(jnp.broadcast_to(value[None], (count,) + value.shape), axe...  19.3 us
    all_to_all x2, waiting for transfers between devices, shares(): lax.all_to_all(jnp.broadcast_to(value[None], (count,) + value.shape), axe...  18.3 us
    all_to_all x1, waiting for transfers between devices, body(): tgt_grad = summed(lax.all_to_all(both, FAR, 0, 0))  12.3 us
    all_to_all x1, starting transfers between devices, body(): piece = summed(lax.all_to_all(terms, NEAR, 0, 0)).astype(bf16)  9.14 us
    pallas_call x1, Pallas kernels, corr_transposed(): pl.pallas_call(corr_kernel, out_shape=jax.ShapeDtypeStruct((tgt_width * t...  6.54 us
    all_to_all x1, starting transfers between devices, body(): lax.all_to_all(hidden.reshape(src_rows, src_width, chans), TGT, 0, 0)  6.27 us
    all_to_all x1, starting transfers between devices, body(): tgt_grad = summed(lax.all_to_all(both, FAR, 0, 0))  4.69 us
    ppermute x1, starting transfers between devices, body(): grad_after = lax.ppermute(block_grad, ALL, down)  4.27 us
  transfers between devices with their start and end apart: 10, of which 5 were waited for; matrix products, arithmetic and copies ran while one was open for 8% of the time, Pallas kernels for 0%

profile of v1, /device:TPU:8, one launch (start us, length us, event | category | flops | bytes accessed | tf_op | source)
XLA Modules:
  0.0 113.5 jit_solution(7182402092765715130)
XLA Ops:
  0.7 6.5 %corr_build.1 = bf16[2048,1024]{1,0:T(8,128)(2,1)} custom-call(s32[1]{0:T(128)} %bitcast.first_ref, bf16[324,8,128]{2,1,0:T(8,128)(2,1)} %bitcast.48, s32[2,8,128]{2,1,0:T(8,128)} %cents_ref.1), custom_call_target="tpu_custom_call" | custom-call | flops 20000000 | bytes 6000000 | tf_op jit(solution)/shard_map/corr_build/pallas_call | solution.py:83
  7.2 3.8 %fusion.1 = bf16[1024,256]{1,0:T(8,128)(2,1)S(1)} fusion(bf16[2048,1024]{1,0:T(8,128)(2,1)} %corr_build.1, bf16[8,256,256]{2,1,0:T(8,128)(2,1)S(1)} %copy-done.3), kind=kOutput, calls=%fused_computation.3 | convolution fusion | flops 1074266112 | bytes 5767168 | tf_op jit(solution)/shard_map/dot_general | solution.py:143
  11.1 1.0 convolution_convert_fusion.2
  12.1 6.3 %all-to-all-start.1 = ((bf16[8,128,128]{2,1,0:T(8,128)(2,1)}), bf16[8,128,128]{2,1,0:T(8,128)(2,1)S(1)}, u32[]{:S(2)}, u32[]{:S(2)}) async-start(bf16[8,128,128]{2,1,0:T(8,128)(2,1)} %bitcast.11), calls=%async_computation.1 | async-start | bytes 524288 | tf_op jit(solution)/shard_map/all_to_all | solution.py:149
  18.4 3.4 %collective-permute-start.4 = (bf16[128,128]{1,0:T(8,128)(2,1)S(1)}, bf16[128,128]{1,0:T(8,128)(2,1)S(1)}, u32[]{:S(2)}, u32[]{:S(2)}) collective-permute-start(bf16[128,128]{1,0:T(8,128)(2,1)S(1)} %bitcast.53), channel_id=1, source_target_pairs={{1,0},{2,1},{3,2},{4,3},{5,4},{6,5},{7,6},{8,7},{9,8},{10,9},{11,1... | collective-permute-start | bytes 98312 | tf_op jit(solution)/shard_map/ppermute | solution.py:137
  21.7 2.5 %collective-permute-start.3 = (bf16[128,128]{1,0:T(8,128)(2,1)S(1)}, bf16[128,128]{1,0:T(8,128)(2,1)S(1)}, u32[]{:S(2)}, u32[]{:S(2)}) collective-permute-start(bf16[128,128]{1,0:T(8,128)(2,1)S(1)} %bitcast.54), channel_id=1, source_target_pairs={{0,1},{1,2},{2,3},{3,4},{4,5},{5,6},{6,7},{7,8},{8,9},{9,10},{10,1... | collective-permute-start | bytes 98312 | tf_op jit(solution)/shard_map/ppermute | solution.py:136
  24.2 0.3 fusion.2
  24.6 4.3 %collective-permute-start.1 = (bf16[128,128]{1,0:T(8,128)(2,1)S(1)}, bf16[128,128]{1,0:T(8,128)(2,1)S(1)}, u32[]{:S(2)}, u32[]{:S(2)}) collective-permute-start(bf16[128,128]{1,0:T(8,128)(2,1)S(1)} %select_convert_fusion), channel_id=1, source_target_pairs={{1,0},{2,1},{3,2},{4,3},{5,4},{6,5},{7,6},{8,7},{9,8},{10,9},{11,1... | collective-permute-start | bytes 98312 | tf_op jit(solution)/shard_map/ppermute | solution.py:200
  28.9 1.9 %collective-permute-done.1 = bf16[128,128]{1,0:T(8,128)(2,1)S(1)} collective-permute-done((bf16[128,128]{1,0:T(8,128)(2,1)S(1)}, bf16[128,128]{1,0:T(8,128)(2,1)S(1)}, u32[]{:S(2)}, u32[]{:S(2)}) %collective-permute-start.1) | collective-permute-done | bytes 32800 | tf_op jit(solution)/shard_map/ppermute | solution.py:200
  30.9 0.3 convolution_convert_fusion.1
  31.2 0.8 fusion.8
  32.0 9.1 %all-to-all-start.2 = ((bf16[16,32,384]{2,1,0:T(8,128)(2,1)}), bf16[16,32,384]{2,1,0:T(8,128)(2,1)S(1)}, u32[]{:S(2)}, u32[]{:S(2)}) async-start(bf16[16,32,384]{2,1,0:T(8,128)(2,1)} %fusion.8), calls=%async_computation.2 | async-start | bytes 786432 | tf_op jit(solution)/shard_map/all_to_all | solution.py:192
  41.1 3.8 %fusion = bf16[2048,256]{1,0:T(8,128)(2,1)S(1)} fusion(bf16[2048,1024]{1,0:T(8,128)(2,1)} %corr_build.1, bf16[1024,128]{1,0:T(8,128)(2,1)S(1)} %bitcast.50, bf16[128,256]{1,0:T(8,128)(2,1)S(1)} %copy-done), kind=kOutput, calls=%fused_computation.1 | convolution fusion | flops 1142161408 | bytes 5570560 | tf_op jit(solution)/shard_map/dot_general | solution.py:156
  45.0 0.2 collective-permute-start
  45.2 3.8 %all-to-all-done.2 = bf16[16,32,384]{2,1,0:T(8,128)(2,1)S(1)} async-done(((bf16[16,32,384]{2,1,0:T(8,128)(2,1)}), bf16[16,32,384]{2,1,0:T(8,128)(2,1)S(1)}, u32[]{:S(2)}, u32[]{:S(2)}) %all-to-all-start.2) | async-done | bytes 393248 | tf_op jit(solution)/shard_map/all_to_all | solution.py:192
  49.0 0.8 broadcast_in_dim.21
  49.8 12.3 %all-to-all-start.3 = ((bf16[16,32,384]{2,1,0:T(8,128)(2,1)}), bf16[16,32,384]{2,1,0:T(8,128)(2,1)S(1)}, u32[]{:S(2)}, u32[]{:S(2)}) async-start(bf16[16,32,384]{2,1,0:T(8,128)(2,1)} %broadcast_in_dim.21), calls=%async_computation.3 | async-start | bytes 786432 | tf_op jit(solution)/shard_map/all_to_all | solution.py:107
  62.1 1.0 fusion.5
  63.0 12.4 %all-to-all-done.3 = bf16[16,32,384]{2,1,0:T(8,128)(2,1)S(1)} async-done(((bf16[16,32,384]{2,1,0:T(8,128)(2,1)}), bf16[16,32,384]{2,1,0:T(8,128)(2,1)S(1)}, u32[]{:S(2)}, u32[]{:S(2)}) %all-to-all-start.3) | async-done | bytes 393248 | tf_op jit(solution)/shard_map/all_to_all | solution.py:107
  75.4 4.7 %all-to-all-start = ((bf16[16,64,256]{2,1,0:T(8,128)(2,1)}), bf16[16,64,256]{2,1,0:T(8,128)(2,1)S(1)}, u32[]{:S(2)}, u32[]{:S(2)}) async-start(bf16[16,64,256]{2,1,0:T(8,128)(2,1)} %fusion.5), calls=%async_computation | async-start | bytes 1048576 | tf_op jit(solution)/shard_map/all_to_all | solution.py:168
  80.1 3.5 %collective-permute-start.2 = (bf16[128,128]{1,0:T(8,128)(2,1)S(1)}, bf16[128,128]{1,0:T(8,128)(2,1)S(1)}, u32[]{:S(2)}, u32[]{:S(2)}) collective-permute-start(bf16[128,128]{1,0:T(8,128)(2,1)S(1)} %select_convert_fusion), channel_id=1, source_target_pairs={{0,1},{1,2},{2,3},{3,4},{4,5},{5,6},{6,7},{7,8},{8,9},{9,10},{10,1... | collective-permute-start | bytes 98312 | tf_op jit(solution)/shard_map/ppermute | solution.py:199
  83.6 12.3 %all-to-all-done = bf16[16,64,256]{2,1,0:T(8,128)(2,1)S(1)} async-done(((bf16[16,64,256]{2,1,0:T(8,128)(2,1)}), bf16[16,64,256]{2,1,0:T(8,128)(2,1)S(1)}, u32[]{:S(2)}, u32[]{:S(2)}) %all-to-all-start) | async-done | bytes 524320 | tf_op jit(solution)/shard_map/all_to_all | solution.py:168
  95.9 0.8 broadcast_in_dim.22
  96.7 7.0 %all-to-all-start.4 = ((bf16[16,32,384]{2,1,0:T(8,128)(2,1)}), bf16[16,32,384]{2,1,0:T(8,128)(2,1)S(1)}, u32[]{:S(2)}, u32[]{:S(2)}) async-start(bf16[16,32,384]{2,1,0:T(8,128)(2,1)} %broadcast_in_dim.22), calls=%async_computation.4 | async-start | bytes 786432 | tf_op jit(solution)/shard_map/all_to_all | solution.py:107
  103.7 0.2 copy.16
  104.0 0.8 fusion.3
  104.9 0.1 reduce_sum.42
  105.0 0.6 copy.17
  105.6 6.0 %all-to-all-done.4 = bf16[16,32,384]{2,1,0:T(8,128)(2,1)S(1)} async-done(((bf16[16,32,384]{2,1,0:T(8,128)(2,1)}), bf16[16,32,384]{2,1,0:T(8,128)(2,1)S(1)}, u32[]{:S(2)}, u32[]{:S(2)}) %all-to-all-start.4) | async-done | bytes 393248 | tf_op jit(solution)/shard_map/all_to_all | solution.py:107
  111.6 0.2 reshape.58
  111.9 0.9 copy.18
  112.8 0.7 slice_bitcast_fusion
  (35 shorter events, 0.6 us)
Async XLA Ops:
  0.6 10.4 %copy-start = (bf16[128,256]{1,0:T(8,128)(2,1)S(1)}, bf16[128,256]{1,0:T(8,128)(2,1)}, u32[]{:S(2)}) copy-start(bf16[128,256]{1,0:T(8,128)(2,1)} %param.12) | copy-start | bytes 196612
  0.6 6.6 %copy-start.3 = (bf16[8,256,256]{2,1,0:T(8,128)(2,1)S(1)}, bf16[8,256,256]{2,1,0:T(8,128)(2,1)}, u32[]{:S(2)}) copy-start(bf16[8,256,256]{2,1,0:T(8,128)(2,1)} %param.11) | copy-start | bytes 3145732
  7.2 11.2 %copy-start.4 = (bf16[1,128,128]{2,1,0:T(8,128)(2,1)S(1)}, bf16[1,128,128]{2,1,0:T(8,128)(2,1)}, u32[]{:S(2)}) copy-start(bf16[1,128,128]{2,1,0:T(8,128)(2,1)} %param.10) | copy-start | bytes 98308
  7.2 17.0 %copy-start.1 = (bf16[8,128,128]{2,1,0:T(8,128)(2,1)S(1)}, bf16[8,128,128]{2,1,0:T(8,128)(2,1)}, u32[]{:S(2)}) copy-start(bf16[8,128,128]{2,1,0:T(8,128)(2,1)} %param.9) | copy-start | bytes 786436
  12.1 12.4 %all-to-all-start.1 = ((bf16[8,128,128]{2,1,0:T(8,128)(2,1)}), bf16[8,128,128]{2,1,0:T(8,128)(2,1)S(1)}, u32[]{:S(2)}, u32[]{:S(2)}) async-start(bf16[8,128,128]{2,1,0:T(8,128)(2,1)} %bitcast.11), calls=%async_computation.1 | async-start | bytes 524288 | tf_op jit(solution)/shard_map/all_to_all | solution.py:149
  18.4 12.5 %collective-permute-start.4 = (bf16[128,128]{1,0:T(8,128)(2,1)S(1)}, bf16[128,128]{1,0:T(8,128)(2,1)S(1)}, u32[]{:S(2)}, u32[]{:S(2)}) collective-permute-start(bf16[128,128]{1,0:T(8,128)(2,1)S(1)} %bitcast.53), channel_id=1, source_target_pairs={{1,0},{2,1},{3,2},{4,3},{5,4},{6,5},{7,6},{8,7},{9,8},{10,9},{11,1... | collective-permute-start | bytes 98312 | tf_op jit(solution)/shard_map/ppermute | solution.py:137
  21.7 9.2 %collective-permute-start.3 = (bf16[128,128]{1,0:T(8,128)(2,1)S(1)}, bf16[128,128]{1,0:T(8,128)(2,1)S(1)}, u32[]{:S(2)}, u32[]{:S(2)}) collective-permute-start(bf16[128,128]{1,0:T(8,128)(2,1)S(1)} %bitcast.54), channel_id=1, source_target_pairs={{0,1},{1,2},{2,3},{3,4},{4,5},{5,6},{6,7},{7,8},{8,9},{9,10},{10,1... | collective-permute-start | bytes 98312 | tf_op jit(solution)/shard_map/ppermute | solution.py:136
  24.6 6.2 %collective-permute-start.1 = (bf16[128,128]{1,0:T(8,128)(2,1)S(1)}, bf16[128,128]{1,0:T(8,128)(2,1)S(1)}, u32[]{:S(2)}, u32[]{:S(2)}) collective-permute-start(bf16[128,128]{1,0:T(8,128)(2,1)S(1)} %select_convert_fusion), channel_id=1, source_target_pairs={{1,0},{2,1},{3,2},{4,3},{5,4},{6,5},{7,6},{8,7},{9,8},{10,9},{11,1... | collective-permute-start | bytes 98312 | tf_op jit(solution)/shard_map/ppermute | solution.py:200
  32.0 17.0 %all-to-all-start.2 = ((bf16[16,32,384]{2,1,0:T(8,128)(2,1)}), bf16[16,32,384]{2,1,0:T(8,128)(2,1)S(1)}, u32[]{:S(2)}, u32[]{:S(2)}) async-start(bf16[16,32,384]{2,1,0:T(8,128)(2,1)} %fusion.8), calls=%async_computation.2 | async-start | bytes 786432 | tf_op jit(solution)/shard_map/all_to_all | solution.py:192
  44.9 58.8 %copy-start.2 = (bf16[3,3,128,128]{3,2,1,0:T(8,128)(2,1)S(1)}, bf16[3,3,128,128]{3,2,1,0:T(8,128)(2,1)}, u32[]{:S(2)}) copy-start(bf16[3,3,128,128]{3,2,1,0:T(8,128)(2,1)} %param.13) | copy-start | bytes 884740
  45.0 17.1 %collective-permute-start = (bf16[16,64,256]{2,1,0:T(8,128)(2,1)S(1)}, bf16[16,64,256]{2,1,0:T(8,128)(2,1)S(1)}, u32[]{:S(2)}, u32[]{:S(2)}) collective-permute-start(bf16[16,64,256]{2,1,0:T(8,128)(2,1)S(1)} %dynamic-slice_bitcast_fusion), channel_id=1, source_target_pairs={{0,8},{1,9},{2,10},{3,11},{4,12},{5,13},{6,14},{7,15},{8,0},{9,1},... | collective-permute-start | bytes 1572872 | tf_op jit(solution)/shard_map/ppermute | solution.py:166
  49.8 25.6 %all-to-all-start.3 = ((bf16[16,32,384]{2,1,0:T(8,128)(2,1)}), bf16[16,32,384]{2,1,0:T(8,128)(2,1)S(1)}, u32[]{:S(2)}, u32[]{:S(2)}) async-start(bf16[16,32,384]{2,1,0:T(8,128)(2,1)} %broadcast_in_dim.21), calls=%async_computation.3 | async-start | bytes 786432 | tf_op jit(solution)/shard_map/all_to_all | solution.py:107
  75.4 20.6 %all-to-all-start = ((bf16[16,64,256]{2,1,0:T(8,128)(2,1)}), bf16[16,64,256]{2,1,0:T(8,128)(2,1)S(1)}, u32[]{:S(2)}, u32[]{:S(2)}) async-start(bf16[16,64,256]{2,1,0:T(8,128)(2,1)} %fusion.5), calls=%async_computation | async-start | bytes 1048576 | tf_op jit(solution)/shard_map/all_to_all | solution.py:168
  80.1 23.9 %collective-permute-start.2 = (bf16[128,128]{1,0:T(8,128)(2,1)S(1)}, bf16[128,128]{1,0:T(8,128)(2,1)S(1)}, u32[]{:S(2)}, u32[]{:S(2)}) collective-permute-start(bf16[128,128]{1,0:T(8,128)(2,1)S(1)} %select_convert_fusion), channel_id=1, source_target_pairs={{0,1},{1,2},{2,3},{3,4},{4,5},{5,6},{6,7},{7,8},{8,9},{9,10},{10,1... | collective-permute-start | bytes 98312 | tf_op jit(solution)/shard_map/ppermute | solution.py:199
  96.7 14.8 %all-to-all-start.4 = ((bf16[16,32,384]{2,1,0:T(8,128)(2,1)}), bf16[16,32,384]{2,1,0:T(8,128)(2,1)S(1)}, u32[]{:S(2)}, u32[]{:S(2)}) async-start(bf16[16,32,384]{2,1,0:T(8,128)(2,1)} %broadcast_in_dim.22), calls=%async_computation.4 | async-start | bytes 786432 | tf_op jit(solution)/shard_map/all_to_all | solution.py:107

commit v2 on v1

v2 whole, which is shorter than its diff:
```python
import functools
import math

import jax
import jax.numpy as jnp
from jax import lax
from jax.experimental import pallas as pl
from jax.experimental.pallas import tpu as pltpu
from jax.sharding import Mesh, PartitionSpec as P


SRC = ("zh", "x", "c")
TGT = ("y", "zl")
ALL = SRC + TGT
NEAR = ("c", "y", "zl")
FAR = ("zh", "x")


def corr_kernel(
    first_ref,
    grads_ref,
    cents_ref,
    targets_ref,
    relu_ref,
    weight_ref,
    corr_ref,
    hidden_ref,
    out_ref,
    wide,
    level_sums,
    tall,
    targets,
):
    step_no = pl.program_id(0)
    tgt_rows, tgt_width, width = targets_ref.shape
    lanes = grads_ref.shape[2]
    pair_rows = corr_ref.shape[1] // lanes
    tile = (tgt_rows, lanes)

    @pl.when(step_no == 0)
    def _():
        wide[...] = grads_ref[...].astype(jnp.float32)
        for h in range(width // lanes):
            part = slice(h * lanes, (h + 1) * lanes)
            for y in range(tgt_rows):
                rows = targets_ref[y, :, part].astype(jnp.float32)
                tall[pl.ds(y, tgt_width, stride=tgt_rows), :] = rows
            targets[:, part] = tall[...].astype(jnp.bfloat16)
        out_ref[...] = jnp.zeros_like(out_ref)

    def build(half, carry):
        row_no = step_no * pair_rows + half
        at = pl.ds(pl.multiple_of(half * lanes, lanes), lanes)
        center_y = jnp.broadcast_to(cents_ref[0, pl.ds(row_no, 1), :], tile)
        center_x = jnp.broadcast_to(cents_ref[1, pl.ds(row_no, 1), :], tile)
        ys = first_ref[0] + lax.broadcasted_iota(jnp.int32, tile, 0)
        zero = jnp.zeros(tile, jnp.float32)

        def spread(level):
            row_off = lax.shift_right_arithmetic(ys, level) - (
                lax.shift_right_arithmetic(center_y, level) - 4
            )
            hits = [row_off == a for a in range(9)]
            picked = []
            for b in range(9):
                acc = zero
                for a in range(9):
                    entry = wide[81 * level + 9 * a + b, pl.ds(row_no, 1), :]
                    acc = jnp.where(hits[a], jnp.broadcast_to(entry, tile), acc)
                picked.append(acc * (0.25**level) if level else acc)
            start = lax.shift_right_arithmetic(center_x, level) - 4
            turn = start & 15
            block = lax.shift_right_arithmetic(start, 4)
            slots = picked + [zero] * 7
            for bit in (8, 4, 2, 1):
                on = (turn & bit) != 0
                slots = [jnp.where(on, slots[(i - bit) % 16], slots[i]) for i in range(16)]
            homes = [jnp.where(turn > j, block + 1, block) for j in range(16)]
            return slots, homes

        offset = 0
        coarse = None
        for level in (3, 2, 1):
            slots, homes = spread(level)
            cells = tgt_width >> level
            for j in range(16):
                for q in range(cells // 16):
                    x = 16 * q + j
                    value = jnp.where(homes[j] == q, slots[j], 0.0)
                    if coarse is not None:
                        value = value + level_sums[coarse + (x >> 1)]
                    level_sums[offset + x] = value
            coarse = offset
            offset += cells
        slots, homes = spread(0)
        for j in range(0, 16, 2):
            for q in range(tgt_width // 16):
                x = 16 * q + j
                under = level_sums[coarse + (x >> 1)]
                left = jnp.where(homes[j] == q, slots[j], 0.0) + under
                right = jnp.where(homes[j + 1] == q, slots[j + 1], 0.0) + under
                pair = jnp.concatenate([left, right], axis=0).astype(jnp.bfloat16)
                corr_ref[x * tgt_rows : (x + 2) * tgt_rows, at] = pair
        return carry

    lax.fori_loop(0, pair_rows, build, 0)
    src = lax.dot_general(
        corr_ref[...],
        targets[...],
        (((0,), (0,)), ((), ())),
        preferred_element_type=jnp.float32,
    )
    src = (src * (1.0 / math.sqrt(width))).astype(jnp.bfloat16)
    hidden = lax.dot_general(
        src, weight_ref[...], (((1,), (1,)), ((), ())), preferred_element_type=jnp.float32
    )
    hidden_ref[...] = hidden.astype(jnp.bfloat16)
    out_ref[...] += lax.dot_general(
        relu_ref[...], src, (((0,), (0,)), ((), ())), preferred_element_type=jnp.float32
    )


def source_pass(upstream, centers, relu_flat, target_feats, out_weight, row_first):
    src_rows, src_width, lookups = upstream.shape
    tgt_rows, tgt_width, width = target_feats.shape
    chans = relu_flat.shape[1]
    pair = 2 * src_width
    grads = jnp.transpose(upstream, (2, 0, 1))
    whole = lambda *shape: pl.BlockSpec(shape, lambda r, f: (0,) * len(shape))
    return pl.pallas_call(
        corr_kernel,
        out_shape=(
            jax.ShapeDtypeStruct((tgt_width * tgt_rows, src_rows * src_width), jnp.bfloat16),
            jax.ShapeDtypeStruct((src_rows * src_width, chans), jnp.bfloat16),
            jax.ShapeDtypeStruct((chans, width), jnp.float32),
        ),
        grid_spec=pltpu.PrefetchScalarGridSpec(
            num_scalar_prefetch=1,
            grid=(src_rows // 2,),
            in_specs=[
                whole(lookups, src_rows, src_width),
                whole(2, src_rows, src_width),
                whole(tgt_rows, tgt_width, width),
                pl.BlockSpec((pair, chans), lambda r, f: (r, 0)),
                whole(chans, width),
            ],
            out_specs=(
                pl.BlockSpec((tgt_width * tgt_rows, pair), lambda r, f: (0, r)),
                pl.BlockSpec((pair, chans), lambda r, f: (r, 0)),
                whole(chans, width),
            ),
            scratch_shapes=[
                pltpu.VMEM((lookups, src_rows, src_width), jnp.float32),
                pltpu.VMEM((tgt_width, tgt_rows, src_width), jnp.float32),
                pltpu.VMEM((tgt_width * tgt_rows, src_width), jnp.float32),
                pltpu.VMEM((tgt_width * tgt_rows, width), jnp.bfloat16),
            ],
        ),
        compiler_params=pltpu.CompilerParams(dimension_semantics=("arbitrary",)),
        cost_estimate=pl.CostEstimate(
            flops=4_000_000_000, bytes_accessed=7_000_000, transcendentals=0
        ),
        name="source_pass",
    )(row_first.reshape(1), grads, centers, target_feats, relu_flat, out_weight)


def target_kernel(core_ref, corr_ref, relu_ref, weight_ref, given_ref, kept_ref, feats):
    @pl.when(pl.program_id(0) == 0)
    def _():
        feats[...] = jnp.dot(
            relu_ref[...], weight_ref[...], preferred_element_type=jnp.float32
        ).astype(jnp.bfloat16)

    count, block, width = given_ref.shape
    part = jnp.dot(corr_ref[...], feats[...], preferred_element_type=jnp.float32)
    part = (part * (1.0 / math.sqrt(width))).astype(jnp.bfloat16).reshape(count, 2, block, width)
    first = core_ref[0] == 0

    @pl.when(first)
    def _():
        given_ref[...] = part[:, 1]
        kept_ref[...] = part[:, 0]

    @pl.when(jnp.logical_not(first))
    def _():
        given_ref[...] = part[:, 0]
        kept_ref[...] = part[:, 1]


def target_pass(corr, relu_flat, out_weight, core_at, far, block):
    cells, sources = corr.shape
    chans, width = out_weight.shape
    steps = 4
    whole = lambda *shape: pl.BlockSpec(shape, lambda r, f: (0,) * len(shape))
    part = pl.BlockSpec((far // steps, block, width), lambda r, f: (r, 0, 0))
    return pl.pallas_call(
        target_kernel,
        out_shape=(jax.ShapeDtypeStruct((far, block, width), jnp.bfloat16),) * 2,
        grid_spec=pltpu.PrefetchScalarGridSpec(
            num_scalar_prefetch=1,
            grid=(steps,),
            in_specs=[
                pl.BlockSpec((cells // steps, sources), lambda r, f: (r, 0)),
                whole(sources, chans),
                whole(chans, width),
            ],
            out_specs=(part, part),
            scratch_shapes=[pltpu.VMEM((sources, width), jnp.bfloat16)],
        ),
        compiler_params=pltpu.CompilerParams(dimension_semantics=("arbitrary",)),
        cost_estimate=pl.CostEstimate(
            flops=2 * cells * sources * width, bytes_accessed=6_500_000, transcendentals=0
        ),
        name="target_pass",
    )(core_at.reshape(1), corr, relu_flat, out_weight)


def terms_kernel(tgt_ref, parts_ref, relu_ref, before_ref, own_ref, after_ref, out_ref, grad_ref, terms_ref):
    total = parts_ref[0].astype(jnp.float32)
    for k in range(1, parts_ref.shape[0]):
        total += parts_ref[k].astype(jnp.float32)
    grad = jnp.where(relu_ref[0].astype(jnp.float32) > 0, total, 0.0).astype(jnp.bfloat16)
    grad_ref[...] = grad
    wide = grad.astype(jnp.float32)
    count = wide.shape[0]
    rows = lax.broadcasted_iota(jnp.int32, wide.shape, 0)
    left = jnp.where(rows == count - 1, 0.0, pltpu.roll(wide, count - 1, 0))
    right = jnp.where(rows == 0, 0.0, pltpu.roll(wide, 1, 0))
    near_grad = jnp.concatenate([left, wide, right], axis=1).astype(jnp.bfloat16)
    near_input = jnp.concatenate([before_ref[...], own_ref[...], after_ref[...]], axis=1)
    conv = lax.dot_general(
        near_input, near_grad, (((0,), (0,)), ((), ())), preferred_element_type=jnp.float32
    )
    near, _, across = terms_ref.shape
    chans, width = out_ref.shape
    out = jnp.concatenate(
        [out_ref[...], jnp.zeros((chans, across - width), jnp.float32)], axis=1
    )
    terms_ref[...] = jnp.concatenate(
        [
            conv.reshape(near, conv.shape[0] // near, across),
            out.reshape(near, chans // near, across),
        ],
        axis=1,
    ).astype(jnp.bfloat16)


def weight_terms(parts, post_relu, inputs, out_term, tgt_at, near):
    count, src_width, chans = parts.shape
    width = out_term.shape[1]
    whole = lambda *shape: pl.BlockSpec(shape, lambda r, f: (0,) * len(shape))
    across = 3 * chans
    down = (across + chans) // near
    return pl.pallas_call(
        terms_kernel,
        out_shape=(
            jax.ShapeDtypeStruct((src_width, chans), jnp.bfloat16),
            jax.ShapeDtypeStruct((near, down, across), jnp.bfloat16),
        ),
        grid_spec=pltpu.PrefetchScalarGridSpec(
            num_scalar_prefetch=1,
            grid=(1,),
            in_specs=[
                whole(count, src_width, chans),
                pl.BlockSpec((1, src_width, chans), lambda r, f: (f[0], 0, 0)),
                whole(src_width, chans),
                whole(src_width, chans),
                whole(src_width, chans),
                whole(chans, width),
            ],
            out_specs=(whole(src_width, chans), whole(near, down, across)),
        ),
        compiler_params=pltpu.CompilerParams(vmem_limit_bytes=8 * 2**20),
        name="weight_terms",
    )(tgt_at.reshape(1), parts, post_relu, *inputs, out_term)


def near_sum_kernel(parts_ref, kept_ref, taken_ref, joint_ref):
    total = parts_ref[0].astype(jnp.float32)
    for k in range(1, parts_ref.shape[0]):
        total += parts_ref[k].astype(jnp.float32)
    rows = total.shape[0]
    last = total[:, 256:]
    total = jnp.concatenate(
        [total[:, :256], jnp.concatenate([last[: rows // 2], last[rows // 2 :]], axis=1)], axis=0
    ).astype(jnp.bfloat16)
    block = kept_ref.shape[1]
    for k in range(joint_ref.shape[0]):
        both = kept_ref[k].astype(jnp.float32) + taken_ref[k].astype(jnp.float32)
        joint_ref[k, :block] = both.astype(jnp.bfloat16)
        joint_ref[k, block:] = total


def near_sum(parts, kept, taken):
    far, block, width = kept.shape
    return pl.pallas_call(
        near_sum_kernel,
        out_shape=jax.ShapeDtypeStruct(
            (far, block + parts.shape[1] * parts.shape[2] // width, width), jnp.bfloat16
        ),
        compiler_params=pltpu.CompilerParams(vmem_limit_bytes=8 * 2**20),
        name="near_sum",
    )(parts, kept, taken)


def far_sum_kernel(scale, parts_ref, tgt_ref, shared_ref, left, right):
    total = parts_ref[0].astype(jnp.float32)
    for k in range(1, parts_ref.shape[0]):
        total += parts_ref[k].astype(jnp.float32)
    tgt_rows, cols, width = tgt_ref.shape
    block = tgt_rows * cols
    near, rows, _ = shared_ref.shape
    left[...] = total[:block, : width // 2]
    right[...] = total[:block, width // 2 :]
    for y in range(tgt_rows):
        at = pl.ds(y, cols, stride=tgt_rows)
        row = jnp.concatenate([left[at, :], right[at, :]], axis=1)
        tgt_ref[y] = row.astype(jnp.bfloat16)
    first = total[block : block + rows]
    second = total[block + rows :]
    second = jnp.concatenate([second[:, : width // 2], second[:, width // 2 :]], axis=0)
    piece = (jnp.concatenate([first, second], axis=1) * scale).astype(jnp.bfloat16)
    for k in range(near):
        shared_ref[k] = piece


def far_sum(parts, tgt_rows, cols, near, rows, across, scale):
    width = parts.shape[2]
    return pl.pallas_call(
        functools.partial(far_sum_kernel, scale),
        out_shape=(
            jax.ShapeDtypeStruct((tgt_rows, cols, width), jnp.bfloat16),
            jax.ShapeDtypeStruct((near, rows, across), jnp.bfloat16),
        ),
        scratch_shapes=[pltpu.VMEM((tgt_rows * cols, width // 2), jnp.float32)] * 2,
        compiler_params=pltpu.CompilerParams(vmem_limit_bytes=8 * 2**20),
        name="far_sum",
    )(parts)


def unpack_kernel(totals_ref, conv_ref, out_ref):
    totals = totals_ref[...].astype(jnp.float32)
    near, _, across = totals.shape
    chans, width = out_ref.shape
    depth = across // near
    conv = totals[:, :depth, :].reshape(across, across)
    for p in range(3):
        for q in range(3):
            conv_ref[p, q] = conv[p * chans : (p + 1) * chans, q * chans : (q + 1) * chans]
    out_ref[...] = totals[:, depth:, :width].reshape(chans, width)


def unpack(totals, chans, width):
    return pl.pallas_call(
        unpack_kernel,
        out_shape=(
            jax.ShapeDtypeStruct((3, 3, chans, chans), jnp.float32),
            jax.ShapeDtypeStruct((chans, width), jnp.float32),
        ),
        compiler_params=pltpu.CompilerParams(vmem_limit_bytes=8 * 2**20),
        name="unpack",
    )(totals)


def moved(array, step):
    zero = jnp.zeros((1,) + array.shape[1:], array.dtype)
    if step > 0:
        return jnp.concatenate([zero, array[:-1]], axis=0)
    return jnp.concatenate([array[1:], zero], axis=0)


def body(upstream, centers, post_relu, conv_input, target_feats, out_weight, conv_weight):
    src_rows, src_width, _ = upstream.shape
    tgt_rows, tgt_width, width = target_feats.shape
    chans = post_relu.shape[2]
    source_total = src_rows * src_width
    src_devices = lax.axis_size(SRC)
    tgt_devices = lax.axis_size(TGT)
    row_total = src_devices * src_rows
    near, far = lax.axis_size(NEAR), lax.axis_size(FAR)
    tgt_at = lax.axis_index(TGT)
    core_at = lax.axis_index("c")
    f32, bf16 = jnp.float32, jnp.bfloat16

    up = [(i, i + 1) for i in range(row_total - 1)]
    down = [(j, i) for i, j in up]
    own_input = conv_input[0]
    input_before = lax.ppermute(own_input, ALL, up)
    input_after = lax.ppermute(own_input, ALL, down)

    relu_flat = post_relu.reshape(source_total, chans)
    corr, hidden, out_term = source_pass(
        upstream, centers, relu_flat, target_feats, out_weight, tgt_at * tgt_rows
    )
    hidden = lax.all_to_all(hidden.reshape(src_rows, src_width, chans), TGT, 0, 0)

    block = tgt_width // src_devices * tgt_rows
    given, kept = target_pass(corr, relu_flat, out_weight, core_at, far, block)
    swap = [(s * tgt_devices + t, (s ^ 1) * tgt_devices + t) for s in range(src_devices) for t in range(tgt_devices)]
    taken = lax.ppermute(given, ALL, swap)
    block_grad, terms = weight_terms(
        hidden, post_relu, (input_before, own_input, input_after), out_term, tgt_at, near
    )
    terms = lax.all_to_all(terms, NEAR, 0, 0)
    grad_before = lax.ppermute(block_grad, ALL, up)
    grad_after = lax.ppermute(block_grad, ALL, down)
    joint = near_sum(terms, kept, taken)
    joint = lax.all_to_all(joint, FAR, 0, 0)
    tgt_grad, pieces = far_sum(
        joint, tgt_rows, tgt_width // src_devices, near, terms.shape[1], terms.shape[2], 1.0 / row_total
    )
    pieces = lax.all_to_all(pieces, NEAR, 0, 0)
    conv_total, out_total = unpack(pieces, chans, width)

    taps = []
    for row in (grad_after, block_grad, grad_before):
        taps += [moved(row, -1), row, moved(row, 1)]
    act_grad = lax.dot_general(
        jnp.concatenate(taps, axis=1),
        jnp.transpose(conv_weight, (0, 1, 3, 2)).reshape(9 * chans, chans),
        (((1,), (0,)), ((), ())),
        preferred_element_type=f32,
    ).astype(bf16)[None]
    return (tgt_grad, act_grad, out_total, conv_total)


def solution(mesh):
    grid = Mesh(mesh.devices.reshape(4, 4, 2, 4, 2), ALL)
    placed = (
        P(SRC, None, None),
        P(None, SRC, None),
        P(SRC, None, None),
        P(ALL, None, None),
        P(TGT, None, None),
        P(),
        P(),
    )
    return jax.shard_map(
        body,
        mesh=grid,
        in_specs=placed,
        out_specs=(P(TGT, SRC, None), P(ALL, None, None), P(), P()),
        check_vma=False,
    )
```

time: 115 us -> 98.5 us (0.86)
  Pallas kernels: 6.54 us -> 18 us
  matrix products: 10 us -> 0.84 us
  starting transfers between devices: 53.1 us -> 45.4 us
  waiting for transfers between devices: 36.3 us -> 29.5 us
  local copies, waits for them, and re-layouts: 4.49 us -> 2.38 us
  other arithmetic: 2.07 us -> 0 us
    all_to_all x4 -> x3, waiting for transfers between devices: 34.4 us -> 8.66 us  [the longest x1 6.86 us: body(): pieces = lax.all_to_all(pieces, NEAR, 0, 0)]
    ppermute x1, waiting for transfers between devices: 1.86 us -> 16.5 us  [body(): grad_after = lax.ppermute(block_grad, ALL, down)]
    pallas_call x1 -> x6, Pallas kernels: 6.54 us -> 18 us  [the longest x1 8.83 us: source_pass(): pl.pallas_call(corr_kernel, out_shape=(jax.ShapeDtypeStruct((tgt_width *...]
    dot_general x5 -> x0, matrix products: 9.18 us -> none  [the longest x1 3.85 us: body(): lax.dot_general(corr, targets, (((0,), (0,)), ((), ())), preferred_elemen...]
    all_to_all x4 -> x3, starting transfers between devices: 33.1 us -> 26.5 us  [the longest x1 10.4 us: body(): joint = lax.all_to_all(joint, FAR, 0, 0)]
    ppermute x1, waiting for transfers between devices: 0.01 us -> 2.42 us  [body(): input_after = lax.ppermute(own_input, ALL, down)]
    ppermute x1, waiting for transfers between devices: 0.01 us -> 1.99 us  [body(): taken = lax.ppermute(given, ALL, swap)]
    broadcast_in_dim x2 -> x0, local copies, waits for them, and re-layouts: 1.56 us -> none  [shares(): jnp.broadcast_to(value[None], (count,) + value.shape)]
  transfers between devices with their start and end apart: 10 -> 9, of which waited for: 5 -> 6; matrix products, arithmetic and copies ran while one was open for 8% -> 1% of each run, Pallas kernels for 0% -> 6%
where the time goes in v2:
time: 98.5 us; the launch traced here: 97 us
  starting transfers between devices  45.4 us (46%)
  waiting for transfers between devices  29.5 us (30%)
  Pallas kernels  18 us (18%)
  local copies, waits for them, and re-layouts  2.38 us (2%)
    ppermute x1, waiting for transfers between devices, body(): grad_after = lax.ppermute(block_grad, ALL, down)  16.5 us
    all_to_all x1, starting transfers between devices, body(): joint = lax.all_to_all(joint, FAR, 0, 0)  10.4 us
    all_to_all x1, starting transfers between devices, body(): pieces = lax.all_to_all(pieces, NEAR, 0, 0)  9.04 us
    pallas_call x1, Pallas kernels, source_pass(): pl.pallas_call(corr_kernel, out_shape=(jax.ShapeDtypeStruct((tgt_width *...  8.83 us
    all_to_all x1, starting transfers between devices, body(): terms = lax.all_to_all(terms, NEAR, 0, 0)  7.06 us
    all_to_all x1, waiting for transfers between devices, body(): pieces = lax.all_to_all(pieces, NEAR, 0, 0)  6.86 us
    all_to_all x1, starting transfers between devices, body(): lax.all_to_all(hidden.reshape(src_rows, src_width, chans), TGT, 0, 0)  6.27 us
    pallas_call x1, Pallas kernels, target_pass(): pl.pallas_call(target_kernel, out_shape=(jax.ShapeDtypeStruct((far, block...  5.22 us
  transfers between devices with their start and end apart: 9, of which 6 were waited for; matrix products, arithmetic and copies ran while one was open for 1% of the time, Pallas kernels for 6%

profile of v2, /device:TPU:8, one launch (start us, length us, event | category | flops | bytes accessed | tf_op | source)
XLA Modules:
  0.0 97.0 jit_solution(4848338737397168308)
XLA Ops:
  0.6 0.0 copy-start.3
  0.6 0.0 copy-start
  0.7 8.8 %source_pass.1 = (bf16[2048,1024]{1,0:T(8,128)(2,1)}, bf16[1024,128]{1,0:T(8,128)(2,1)}, f32[128,256]{1,0:T(8,128)}) custom-call(s32[1]{0:T(128)} %bitcast.1.first_ref, bf16[324,8,128]{2,1,0:T(8,128)(2,1)} %bitcast.21, s32[2,8,128]{2,1,0:T(8,128)} %cents_ref.1, bf16[8,256,256]{2,1,0:T(8,128)(2,1)} %targets_ref.1, bf16[1024,128]{1,0:T(8,128)(2,1)} %bitcast.14, ...), custom_call_target="tpu_custom_call" | custom-call | flops 4000000000 | bytes 7000000 | tf_op jit(solution)/shard_map/source_pass/pallas_call | solution.py:130
  9.5 6.3 %all-to-all-start = ((bf16[8,128,128]{2,1,0:T(8,128)(2,1)}), bf16[8,128,128]{2,1,0:T(8,128)(2,1)S(1)}, u32[]{:S(2)}, u32[]{:S(2)}) async-start(bf16[8,128,128]{2,1,0:T(8,128)(2,1)} %bitcast.20), calls=%async_computation | async-start | bytes 524288 | tf_op jit(solution)/shard_map/all_to_all | solution.py:395
  15.8 0.0 copy-done.3
  15.8 3.4 %collective-permute-start = (bf16[128,128]{1,0:T(8,128)(2,1)S(1)}, bf16[128,128]{1,0:T(8,128)(2,1)S(1)}, u32[]{:S(2)}, u32[]{:S(2)}) collective-permute-start(bf16[128,128]{1,0:T(8,128)(2,1)S(1)} %bitcast.16), channel_id=1, source_target_pairs={{0,1},{1,2},{2,3},{3,4},{4,5},{5,6},{6,7},{7,8},{8,9},{9,10},{10,1... | collective-permute-start | bytes 98312 | tf_op jit(solution)/shard_map/ppermute | solution.py:388
  19.1 3.4 %collective-permute-start.1 = (bf16[128,128]{1,0:T(8,128)(2,1)S(1)}, bf16[128,128]{1,0:T(8,128)(2,1)S(1)}, u32[]{:S(2)}, u32[]{:S(2)}) collective-permute-start(bf16[128,128]{1,0:T(8,128)(2,1)S(1)} %bitcast.17), channel_id=1, source_target_pairs={{1,0},{2,1},{3,2},{4,3},{5,4},{6,5},{7,6},{8,7},{9,8},{10,9},{11,1... | collective-permute-start | bytes 98312 | tf_op jit(solution)/shard_map/ppermute | solution.py:389
  22.5 0.0 collective-permute-done.before_ref
  22.5 2.4 %collective-permute-done.1.after_ref = bf16[128,128]{1,0:T(8,128)(2,1)S(1)} collective-permute-done((bf16[128,128]{1,0:T(8,128)(2,1)S(1)}, bf16[128,128]{1,0:T(8,128)(2,1)S(1)}, u32[]{:S(2)}, u32[]{:S(2)}) %collective-permute-start.1) | collective-permute-done | bytes 32800 | tf_op jit(solution)/shard_map/ppermute | solution.py:389
  24.9 0.0 all-to-all-done.parts_ref
  24.9 0.0 copy-done
  25.0 0.9 copy-done.2
  25.9 1.0 %weight_terms.1 = (bf16[128,128]{1,0:T(8,128)(2,1)S(1)}, bf16[16,32,384]{2,1,0:T(8,128)(2,1)}) custom-call(s32[1]{0:T(128)} %bitcast.tgt_ref, bf16[8,128,128]{2,1,0:T(8,128)(2,1)S(1)} %all-to-all-done.parts_ref, bf16[8,128,128]{2,1,0:T(8,128)(2,1)S(1)} %copy-done, bf16[128,128]{1,0:T(8,128)(2,1)S(1)} %collective-permute-done.before_ref, ...), custom_call_target="tpu_custom_call" | custom-call | tf_op jit(solution)/shard_map/weight_terms/pallas_call | solution.py:254
  26.9 7.1 %all-to-all-start.1 = ((bf16[16,32,384]{2,1,0:T(8,128)(2,1)}), bf16[16,32,384]{2,1,0:T(8,128)(2,1)S(1)}, u32[]{:S(2)}, u32[]{:S(2)}) async-start(bf16[16,32,384]{2,1,0:T(8,128)(2,1)} %get-tuple-element.17), calls=%async_computation.1 | async-start | bytes 786432 | tf_op jit(solution)/shard_map/all_to_all | solution.py:404
  34.0 5.2 %target_pass.1 = (bf16[16,64,256]{2,1,0:T(8,128)(2,1)}, bf16[16,64,256]{2,1,0:T(8,128)(2,1)}) custom-call(s32[1]{0:T(128)} %bitcast.6.core_ref, bf16[2048,1024]{1,0:T(8,128)(2,1)} %get-tuple-element.18.corr_ref, bf16[1024,128]{1,0:T(8,128)(2,1)} %bitcast.15, bf16[128,256]{1,0:T(8,128)(2,1)} %weight_ref.3), custom_call_target="tpu_custom_call" | custom-call | flops 1073741824 | bytes 6500000 | tf_op jit(solution)/shard_map/target_pass/pallas_call | solution.py:196
  39.2 0.1 collective-permute-start.2
  39.3 2.0 %collective-permute-done.2.taken_ref = bf16[16,64,256]{2,1,0:T(8,128)(2,1)S(1)} collective-permute-done((bf16[16,64,256]{2,1,0:T(8,128)(2,1)}, bf16[16,64,256]{2,1,0:T(8,128)(2,1)S(1)}, u32[]{:S(2)}, u32[]{:S(2)}) %collective-permute-start.2) | collective-permute-done | bytes 524320 | tf_op jit(solution)/shard_map/ppermute | solution.py:400
  41.3 0.5 all-to-all-done.1.parts_ref
  41.8 1.0 %copy-done.1 = bf16[16,64,256]{2,1,0:T(8,128)(2,1)S(1)} copy-done((bf16[16,64,256]{2,1,0:T(8,128)(2,1)S(1)}, bf16[16,64,256]{2,1,0:T(8,128)(2,1)}, u32[]{:S(2)}) %copy-start.1) | copy-done | bytes 524312
  42.8 1.1 %near_sum.1 = bf16[16,112,256]{2,1,0:T(8,128)(2,1)} custom-call(bf16[16,32,384]{2,1,0:T(8,128)(2,1)S(1)} %all-to-all-done.1.parts_ref, bf16[16,64,256]{2,1,0:T(8,128)(2,1)S(1)} %copy-done.1, bf16[16,64,256]{2,1,0:T(8,128)(2,1)S(1)} %collective-permute-done.2.taken_ref), custom_call_target="tpu_custom_call" | custom-call | tf_op jit(solution)/shard_map/near_sum/pallas_call | solution.py:296
  43.9 10.4 %all-to-all-start.2 = ((bf16[16,112,256]{2,1,0:T(8,128)(2,1)}), bf16[16,112,256]{2,1,0:T(8,128)(2,1)S(1)}, u32[]{:S(2)}, u32[]{:S(2)}) async-start(bf16[16,112,256]{2,1,0:T(8,128)(2,1)} %near_sum.1), calls=%async_computation.2 | async-start | bytes 1835008 | tf_op jit(solution)/shard_map/all_to_all | solution.py:408
  54.3 0.2 copy.11
  54.5 3.6 %collective-permute-start.3 = (bf16[128,128]{1,0:T(8,128)(2,1)S(1)}, bf16[128,128]{1,0:T(8,128)(2,1)S(1)}, u32[]{:S(2)}, u32[]{:S(2)}) collective-permute-start(bf16[128,128]{1,0:T(8,128)(2,1)S(1)} %get-tuple-element.22), channel_id=1, source_target_pairs={{1,0},{2,1},{3,2},{4,3},{5,4},{6,5},{7,6},{8,7},{9,8},{10,9},{11,1... | collective-permute-start | bytes 98312 | tf_op jit(solution)/shard_map/ppermute | solution.py:406
  58.2 2.2 %collective-permute-start.4 = (bf16[128,128]{1,0:T(8,128)(2,1)S(1)}, bf16[128,128]{1,0:T(8,128)(2,1)S(1)}, u32[]{:S(2)}, u32[]{:S(2)}) collective-permute-start(bf16[128,128]{1,0:T(8,128)(2,1)S(1)} %get-tuple-element.22), channel_id=1, source_target_pairs={{0,1},{1,2},{2,3},{3,4},{4,5},{5,6},{6,7},{7,8},{8,9},{9,10},{10,1... | collective-permute-start | bytes 98312 | tf_op jit(solution)/shard_map/ppermute | solution.py:405
  60.4 16.5 %collective-permute-done.3 = bf16[128,128]{1,0:T(8,128)(2,1)S(1)} collective-permute-done((bf16[128,128]{1,0:T(8,128)(2,1)S(1)}, bf16[128,128]{1,0:T(8,128)(2,1)S(1)}, u32[]{:S(2)}, u32[]{:S(2)}) %collective-permute-start.3) | collective-permute-done | bytes 32800 | tf_op jit(solution)/shard_map/ppermute | solution.py:406
  77.0 1.3 %all-to-all-done.2.parts_ref = bf16[16,112,256]{2,1,0:T(8,128)(2,1)S(1)} async-done(((bf16[16,112,256]{2,1,0:T(8,128)(2,1)}), bf16[16,112,256]{2,1,0:T(8,128)(2,1)S(1)}, u32[]{:S(2)}, u32[]{:S(2)}) %all-to-all-start.2) | async-done | bytes 917536 | tf_op jit(solution)/shard_map/all_to_all | solution.py:408
  78.3 0.9 far_sum.1
  79.3 9.0 %all-to-all-start.3 = ((bf16[16,32,384]{2,1,0:T(8,128)(2,1)}), bf16[16,32,384]{2,1,0:T(8,128)(2,1)S(1)}, u32[]{:S(2)}, u32[]{:S(2)}) async-start(bf16[16,32,384]{2,1,0:T(8,128)(2,1)} %get-tuple-element.23), calls=%async_computation.3 | async-start | bytes 786432 | tf_op jit(solution)/shard_map/all_to_all | solution.py:412
  88.3 0.0 collective-permute-done.4
  88.4 0.8 fusion
  89.3 6.9 %all-to-all-done.3.totals_ref = bf16[16,32,384]{2,1,0:T(8,128)(2,1)S(1)} async-done(((bf16[16,32,384]{2,1,0:T(8,128)(2,1)}), bf16[16,32,384]{2,1,0:T(8,128)(2,1)S(1)}, u32[]{:S(2)}, u32[]{:S(2)}) %all-to-all-start.3) | async-done | bytes 393248 | tf_op jit(solution)/shard_map/all_to_all | solution.py:412
  96.1 0.9 unpack.1
  (16 shorter events, 0.2 us)
Async XLA Ops:
  0.6 15.1 %copy-start.3 = (bf16[1,128,128]{2,1,0:T(8,128)(2,1)S(1)}, bf16[1,128,128]{2,1,0:T(8,128)(2,1)}, u32[]{:S(2)}) copy-start(bf16[1,128,128]{2,1,0:T(8,128)(2,1)} %param.10) | copy-start | bytes 98308
  0.6 24.3 %copy-start = (bf16[8,128,128]{2,1,0:T(8,128)(2,1)S(1)}, bf16[8,128,128]{2,1,0:T(8,128)(2,1)}, u32[]{:S(2)}) copy-start(bf16[8,128,128]{2,1,0:T(8,128)(2,1)} %relu_ref.1) | copy-start | bytes 786436
  9.5 15.5 %all-to-all-start = ((bf16[8,128,128]{2,1,0:T(8,128)(2,1)}), bf16[8,128,128]{2,1,0:T(8,128)(2,1)S(1)}, u32[]{:S(2)}, u32[]{:S(2)}) async-start(bf16[8,128,128]{2,1,0:T(8,128)(2,1)} %bitcast.20), calls=%async_computation | async-start | bytes 524288 | tf_op jit(solution)/shard_map/all_to_all | solution.py:395
  15.8 6.7 %collective-permute-start = (bf16[128,128]{1,0:T(8,128)(2,1)S(1)}, bf16[128,128]{1,0:T(8,128)(2,1)S(1)}, u32[]{:S(2)}, u32[]{:S(2)}) collective-permute-start(bf16[128,128]{1,0:T(8,128)(2,1)S(1)} %bitcast.16), channel_id=1, source_target_pairs={{0,1},{1,2},{2,3},{3,4},{4,5},{5,6},{6,7},{7,8},{8,9},{9,10},{10,1... | collective-permute-start | bytes 98312 | tf_op jit(solution)/shard_map/ppermute | solution.py:388
  19.1 5.8 %collective-permute-start.1 = (bf16[128,128]{1,0:T(8,128)(2,1)S(1)}, bf16[128,128]{1,0:T(8,128)(2,1)S(1)}, u32[]{:S(2)}, u32[]{:S(2)}) collective-permute-start(bf16[128,128]{1,0:T(8,128)(2,1)S(1)} %bitcast.17), channel_id=1, source_target_pairs={{1,0},{2,1},{3,2},{4,3},{5,4},{6,5},{7,6},{8,7},{9,8},{10,9},{11,1... | collective-permute-start | bytes 98312 | tf_op jit(solution)/shard_map/ppermute | solution.py:389
  24.9 0.9 copy-start.2
  26.9 14.9 %all-to-all-start.1 = ((bf16[16,32,384]{2,1,0:T(8,128)(2,1)}), bf16[16,32,384]{2,1,0:T(8,128)(2,1)S(1)}, u32[]{:S(2)}, u32[]{:S(2)}) async-start(bf16[16,32,384]{2,1,0:T(8,128)(2,1)} %get-tuple-element.17), calls=%async_computation.1 | async-start | bytes 786432 | tf_op jit(solution)/shard_map/all_to_all | solution.py:404
  33.9 20.4 %copy-start.4 = (bf16[3,3,128,128]{3,2,1,0:T(8,128)(2,1)S(1)}, bf16[3,3,128,128]{3,2,1,0:T(8,128)(2,1)}, u32[]{:S(2)}) copy-start(bf16[3,3,128,128]{3,2,1,0:T(8,128)(2,1)} %param.13) | copy-start | bytes 884740
  39.2 2.1 %collective-permute-start.2 = (bf16[16,64,256]{2,1,0:T(8,128)(2,1)}, bf16[16,64,256]{2,1,0:T(8,128)(2,1)S(1)}, u32[]{:S(2)}, u32[]{:S(2)}) collective-permute-start(bf16[16,64,256]{2,1,0:T(8,128)(2,1)} %get-tuple-element.20), channel_id=1, source_target_pairs={{0,8},{1,9},{2,10},{3,11},{4,12},{5,13},{6,14},{7,15},{8,0},{9,1},... | collective-permute-start | bytes 1572872 | tf_op jit(solution)/shard_map/ppermute | solution.py:400
  41.8 1.0 %copy-start.1 = (bf16[16,64,256]{2,1,0:T(8,128)(2,1)S(1)}, bf16[16,64,256]{2,1,0:T(8,128)(2,1)}, u32[]{:S(2)}) copy-start(bf16[16,64,256]{2,1,0:T(8,128)(2,1)} %get-tuple-element.19.kept_ref) | copy-start | bytes 1572868
  43.9 34.4 %all-to-all-start.2 = ((bf16[16,112,256]{2,1,0:T(8,128)(2,1)}), bf16[16,112,256]{2,1,0:T(8,128)(2,1)S(1)}, u32[]{:S(2)}, u32[]{:S(2)}) async-start(bf16[16,112,256]{2,1,0:T(8,128)(2,1)} %near_sum.1), calls=%async_computation.2 | async-start | bytes 1835008 | tf_op jit(solution)/shard_map/all_to_all | solution.py:408
  54.5 22.3 %collective-permute-start.3 = (bf16[128,128]{1,0:T(8,128)(2,1)S(1)}, bf16[128,128]{1,0:T(8,128)(2,1)S(1)}, u32[]{:S(2)}, u32[]{:S(2)}) collective-permute-start(bf16[128,128]{1,0:T(8,128)(2,1)S(1)} %get-tuple-element.22), channel_id=1, source_target_pairs={{1,0},{2,1},{3,2},{4,3},{5,4},{6,5},{7,6},{8,7},{9,8},{10,9},{11,1... | collective-permute-start | bytes 98312 | tf_op jit(solution)/shard_map/ppermute | solution.py:406
  58.2 30.1 %collective-permute-start.4 = (bf16[128,128]{1,0:T(8,128)(2,1)S(1)}, bf16[128,128]{1,0:T(8,128)(2,1)S(1)}, u32[]{:S(2)}, u32[]{:S(2)}) collective-permute-start(bf16[128,128]{1,0:T(8,128)(2,1)S(1)} %get-tuple-element.22), channel_id=1, source_target_pairs={{0,1},{1,2},{2,3},{3,4},{4,5},{5,6},{6,7},{7,8},{8,9},{9,10},{10,1... | collective-permute-start | bytes 98312 | tf_op jit(solution)/shard_map/ppermute | solution.py:405
  79.3 16.9 %all-to-all-start.3 = ((bf16[16,32,384]{2,1,0:T(8,128)(2,1)}), bf16[16,32,384]{2,1,0:T(8,128)(2,1)S(1)}, u32[]{:S(2)}, u32[]{:S(2)}) async-start(bf16[16,32,384]{2,1,0:T(8,128)(2,1)} %get-tuple-element.23), calls=%async_computation.3 | async-start | bytes 786432 | tf_op jit(solution)/shard_map/all_to_all | solution.py:412

commit v3 on v2

--- a/solution.py
+++ b/solution.py
@@ -13,7 +13,6 @@
 TGT = ("y", "zl")
 ALL = SRC + TGT
 NEAR = ("c", "y", "zl")
-FAR = ("zh", "x")
 
 
 def corr_kernel(
@@ -110,10 +109,13 @@
         (((0,), (0,)), ((), ())),
         preferred_element_type=jnp.float32,
     )
-    src = (src * (1.0 / math.sqrt(width))).astype(jnp.bfloat16)
+    exact = src * (1.0 / math.sqrt(width))
+    src = exact.astype(jnp.bfloat16)
+    rest = (exact - src.astype(jnp.float32)).astype(jnp.bfloat16)
+    across = (((1,), (1,)), ((), ()))
     hidden = lax.dot_general(
-        src, weight_ref[...], (((1,), (1,)), ((), ())), preferred_element_type=jnp.float32
-    )
+        src, weight_ref[...], across, preferred_element_type=jnp.float32
+    ) + lax.dot_general(rest, weight_ref[...], across, preferred_element_type=jnp.float32)
     hidden_ref[...] = hidden.astype(jnp.bfloat16)
     out_ref[...] += lax.dot_general(
         relu_ref[...], src, (((0,), (0,)), ((), ())), preferred_element_type=jnp.float32
@@ -171,36 +173,44 @@
             relu_ref[...], weight_ref[...], preferred_element_type=jnp.float32
         ).astype(jnp.bfloat16)
 
-    count, block, width = given_ref.shape
-    part = jnp.dot(corr_ref[...], feats[...], preferred_element_type=jnp.float32)
-    part = (part * (1.0 / math.sqrt(width))).astype(jnp.bfloat16).reshape(count, 2, block, width)
+    highs, _, both, sources = corr_ref.shape
+    width = given_ref.shape[2]
+    block = both // 2
+    part = jnp.dot(
+        corr_ref[...].reshape(highs * both, sources),
+        feats[...],
+        preferred_element_type=jnp.float32,
+    )
+    part = (part * (1.0 / math.sqrt(width))).astype(jnp.bfloat16).reshape(highs, 2, block, width)
+    rows = highs * block
     first = core_ref[0] == 0
 
     @pl.when(first)
     def _():
-        given_ref[...] = part[:, 1]
-        kept_ref[...] = part[:, 0]
+        given_ref[0] = part[:, 1].reshape(rows, width)
+        kept_ref[0] = part[:, 0].reshape(rows, width)
 
     @pl.when(jnp.logical_not(first))
     def _():
-        given_ref[...] = part[:, 0]
-        kept_ref[...] = part[:, 1]
-
-
-def target_pass(corr, relu_flat, out_weight, core_at, far, block):
+        given_ref[0] = part[:, 0].reshape(rows, width)
+        kept_ref[0] = part[:, 1].reshape(rows, width)
+
+
+def target_pass(corr, relu_flat, out_weight, core_at, highs, steps):
     cells, sources = corr.shape
     chans, width = out_weight.shape
-    steps = 4
+    rows = cells // steps // 2
     whole = lambda *shape: pl.BlockSpec(shape, lambda r, f: (0,) * len(shape))
-    part = pl.BlockSpec((far // steps, block, width), lambda r, f: (r, 0, 0))
+    part = pl.BlockSpec((1, rows, width), lambda r, f: (r, 0, 0))
+    both = cells // steps // highs
     return pl.pallas_call(
         target_kernel,
-        out_shape=(jax.ShapeDtypeStruct((far, block, width), jnp.bfloat16),) * 2,
+        out_shape=(jax.ShapeDtypeStruct((steps, rows, width), jnp.bfloat16),) * 2,
         grid_spec=pltpu.PrefetchScalarGridSpec(
             num_scalar_prefetch=1,
             grid=(steps,),
             in_specs=[
-                pl.BlockSpec((cells // steps, sources), lambda r, f: (r, 0)),
+                pl.BlockSpec((highs, 1, both, sources), lambda r, f: (0, r, 0, 0)),
                 whole(sources, chans),
                 whole(chans, width),
             ],
@@ -212,22 +222,28 @@
             flops=2 * cells * sources * width, bytes_accessed=6_500_000, transcendentals=0
         ),
         name="target_pass",
-    )(core_at.reshape(1), corr, relu_flat, out_weight)
-
-
-def terms_kernel(tgt_ref, parts_ref, relu_ref, before_ref, own_ref, after_ref, out_ref, grad_ref, terms_ref):
+    )(core_at.reshape(1), corr.reshape(highs, steps, both, sources), relu_flat, out_weight)
+
+
+def shifted(wide):
+    count = wide.shape[0]
+    rows = lax.broadcasted_iota(jnp.int32, wide.shape, 0)
+    left = jnp.where(rows == count - 1, 0.0, pltpu.roll(wide, count - 1, 0))
+    right = jnp.where(rows == 0, 0.0, pltpu.roll(wide, 1, 0))
+    return left, wide, right
+
+
+def terms_kernel(at_ref, parts_ref, relu_ref, paired_ref, own_ref, linked_ref, out_ref, grad_ref, terms_ref):
     total = parts_ref[0].astype(jnp.float32)
     for k in range(1, parts_ref.shape[0]):
         total += parts_ref[k].astype(jnp.float32)
     grad = jnp.where(relu_ref[0].astype(jnp.float32) > 0, total, 0.0).astype(jnp.bfloat16)
     grad_ref[...] = grad
-    wide = grad.astype(jnp.float32)
-    count = wide.shape[0]
-    rows = lax.broadcasted_iota(jnp.int32, wide.shape, 0)
-    left = jnp.where(rows == count - 1, 0.0, pltpu.roll(wide, count - 1, 0))
-    right = jnp.where(rows == 0, 0.0, pltpu.roll(wide, 1, 0))
-    near_grad = jnp.concatenate([left, wide, right], axis=1).astype(jnp.bfloat16)
-    near_input = jnp.concatenate([before_ref[...], own_ref[...], after_ref[...]], axis=1)
+    near_grad = jnp.concatenate(shifted(grad.astype(jnp.float32)), axis=1).astype(jnp.bfloat16)
+    even = at_ref[1] == 0
+    before = jnp.where(even, linked_ref[...], paired_ref[...])
+    after = jnp.where(even, paired_ref[...], linked_ref[...])
+    near_input = jnp.concatenate([before, own_ref[...], after], axis=1)
     conv = lax.dot_general(
         near_input, near_grad, (((0,), (0,)), ((), ())), preferred_element_type=jnp.float32
     )
@@ -245,7 +261,7 @@
     ).astype(jnp.bfloat16)
 
 
-def weight_terms(parts, post_relu, inputs, out_term, tgt_at, near):
+def weight_terms(parts, post_relu, inputs, out_term, tgt_at, odd, near):
     count, src_width, chans = parts.shape
     width = out_term.shape[1]
     whole = lambda *shape: pl.BlockSpec(shape, lambda r, f: (0,) * len(shape))
@@ -272,7 +288,7 @@
         ),
         compiler_params=pltpu.CompilerParams(vmem_limit_bytes=8 * 2**20),
         name="weight_terms",
-    )(tgt_at.reshape(1), parts, post_relu, *inputs, out_term)
+    )(jnp.stack([tgt_at, odd]), parts, post_relu, *inputs, out_term)
 
 
 def near_sum_kernel(parts_ref, kept_ref, taken_ref, joint_ref):
@@ -280,9 +296,10 @@
     for k in range(1, parts_ref.shape[0]):
         total += parts_ref[k].astype(jnp.float32)
     rows = total.shape[0]
-    last = total[:, 256:]
+    width = joint_ref.shape[2]
+    last = total[:, width:]
     total = jnp.concatenate(
-        [total[:, :256], jnp.concatenate([last[: rows // 2], last[rows // 2 :]], axis=1)], axis=0
+        [total[:, :width], jnp.concatenate([last[: rows // 2], last[rows // 2 :]], axis=1)], axis=0
     ).astype(jnp.bfloat16)
     block = kept_ref.shape[1]
     for k in range(joint_ref.shape[0]):
@@ -292,15 +309,74 @@
 
 
 def near_sum(parts, kept, taken):
-    far, block, width = kept.shape
+    count, block, width = kept.shape
     return pl.pallas_call(
         near_sum_kernel,
         out_shape=jax.ShapeDtypeStruct(
-            (far, block + parts.shape[1] * parts.shape[2] // width, width), jnp.bfloat16
+            (count, block + parts.shape[1] * parts.shape[2] // width, width), jnp.bfloat16
         ),
         compiler_params=pltpu.CompilerParams(vmem_limit_bytes=8 * 2**20),
         name="near_sum",
     )(parts, kept, taken)
+
+
+def x_sum_kernel(parts_ref, joint_ref):
+    total = parts_ref[0].astype(jnp.float32)
+    for k in range(1, parts_ref.shape[0]):
+        total += parts_ref[k].astype(jnp.float32)
+    total = total.astype(jnp.bfloat16)
+    count, rows, _ = joint_ref.shape
+    piece = (count * rows - total.shape[0]) // (count - 1)
+    block = rows - piece
+    for k in range(count):
+        joint_ref[k, :block] = total[k * block : (k + 1) * block]
+        joint_ref[k, block:] = total[count * block :]
+
+
+def x_sum(parts, count, block):
+    _, rows, width = parts.shape
+    return pl.pallas_call(
+        x_sum_kernel,
+        out_shape=jax.ShapeDtypeStruct(
+            (count, block + rows - count * block, width), jnp.bfloat16
+        ),
+        compiler_params=pltpu.CompilerParams(vmem_limit_bytes=8 * 2**20),
+        name="x_sum",
+    )(parts)
+
+
+def act_kernel(at_ref, grad_ref, paired_ref, linked_ref, weight_ref, act_ref):
+    even = at_ref[0] == 0
+    before = jnp.where(even, linked_ref[...], paired_ref[...])
+    after = jnp.where(even, paired_ref[...], linked_ref[...])
+    total = jnp.zeros(grad_ref.shape, jnp.float32)
+    for p, row in enumerate((after, grad_ref[...], before)):
+        for q, tap in enumerate(shifted(row.astype(jnp.float32))):
+            total += lax.dot_general(
+                tap.astype(jnp.bfloat16),
+                weight_ref[p, q],
+                (((1,), (1,)), ((), ())),
+                preferred_element_type=jnp.float32,
+            )
+    act_ref[0] = total.astype(jnp.bfloat16)
+
+
+def act_rows(block_grad, paired, linked, conv_weight, odd):
+    whole = lambda *shape: pl.BlockSpec(shape, lambda r, f: (0,) * len(shape))
+    cols, chans = block_grad.shape
+    row = whole(cols, chans)
+    return pl.pallas_call(
+        act_kernel,
+        out_shape=jax.ShapeDtypeStruct((1, cols, chans), jnp.bfloat16),
+        grid_spec=pltpu.PrefetchScalarGridSpec(
+            num_scalar_prefetch=1,
+            grid=(1,),
+            in_specs=[row, row, row, whole(3, 3, chans, chans)],
+            out_specs=whole(1, cols, chans),
+        ),
+        compiler_params=pltpu.CompilerParams(vmem_limit_bytes=8 * 2**20),
+        name="act_rows",
+    )(odd.reshape(1), block_grad, paired, linked, conv_weight)
 
 
 def far_sum_kernel(scale, parts_ref, tgt_ref, shared_ref, left, right):
@@ -362,65 +438,50 @@
     )(totals)
 
 
-def moved(array, step):
-    zero = jnp.zeros((1,) + array.shape[1:], array.dtype)
-    if step > 0:
-        return jnp.concatenate([zero, array[:-1]], axis=0)
-    return jnp.concatenate([array[1:], zero], axis=0)
-
-
 def body(upstream, centers, post_relu, conv_input, target_feats, out_weight, conv_weight):
     src_rows, src_width, _ = upstream.shape
     tgt_rows, tgt_width, width = target_feats.shape
     chans = post_relu.shape[2]
-    source_total = src_rows * src_width
     src_devices = lax.axis_size(SRC)
-    tgt_devices = lax.axis_size(TGT)
     row_total = src_devices * src_rows
-    near, far = lax.axis_size(NEAR), lax.axis_size(FAR)
+    near, highs, lows = lax.axis_size(NEAR), lax.axis_size("zh"), lax.axis_size("x")
     tgt_at = lax.axis_index(TGT)
     core_at = lax.axis_index("c")
-    f32, bf16 = jnp.float32, jnp.bfloat16
-
-    up = [(i, i + 1) for i in range(row_total - 1)]
-    down = [(j, i) for i, j in up]
+    odd = lax.axis_index("zl")
+
+    pairs = [(i, i ^ 1) for i in range(row_total)]
+    links = [(i, i + 1) for i in range(1, row_total - 1, 2)]
+    links += [(j, i) for i, j in links]
     own_input = conv_input[0]
-    input_before = lax.ppermute(own_input, ALL, up)
-    input_after = lax.ppermute(own_input, ALL, down)
-
-    relu_flat = post_relu.reshape(source_total, chans)
+    input_paired = lax.ppermute(own_input, ALL, pairs)
+    input_linked = lax.ppermute(own_input, ALL, links)
+
+    relu_flat = post_relu.reshape(src_rows * src_width, chans)
     corr, hidden, out_term = source_pass(
         upstream, centers, relu_flat, target_feats, out_weight, tgt_at * tgt_rows
     )
     hidden = lax.all_to_all(hidden.reshape(src_rows, src_width, chans), TGT, 0, 0)
 
-    block = tgt_width // src_devices * tgt_rows
-    given, kept = target_pass(corr, relu_flat, out_weight, core_at, far, block)
-    swap = [(s * tgt_devices + t, (s ^ 1) * tgt_devices + t) for s in range(src_devices) for t in range(tgt_devices)]
-    taken = lax.ppermute(given, ALL, swap)
+    given, kept = target_pass(corr, relu_flat, out_weight, core_at, highs, lows)
+    taken = lax.ppermute(given, "c", [(0, 1), (1, 0)])
+
     block_grad, terms = weight_terms(
-        hidden, post_relu, (input_before, own_input, input_after), out_term, tgt_at, near
+        hidden, post_relu, (input_paired, own_input, input_linked), out_term, tgt_at, odd, near
     )
     terms = lax.all_to_all(terms, NEAR, 0, 0)
-    grad_before = lax.ppermute(block_grad, ALL, up)
-    grad_after = lax.ppermute(block_grad, ALL, down)
+    grad_paired = lax.ppermute(block_grad, ALL, pairs)
+    grad_linked = lax.ppermute(block_grad, ALL, links)
     joint = near_sum(terms, kept, taken)
-    joint = lax.all_to_all(joint, FAR, 0, 0)
+    joint = lax.all_to_all(joint, "x", 0, 0)
+    cols = tgt_width // src_devices
+    joint = x_sum(joint, highs, cols * tgt_rows)
+    joint = lax.all_to_all(joint, "zh", 0, 0)
     tgt_grad, pieces = far_sum(
-        joint, tgt_rows, tgt_width // src_devices, near, terms.shape[1], terms.shape[2], 1.0 / row_total
+        joint, tgt_rows, cols, near, terms.shape[1], terms.shape[2], 1.0 / row_total
     )
     pieces = lax.all_to_all(pieces, NEAR, 0, 0)
+    act_grad = act_rows(block_grad, grad_paired, grad_linked, conv_weight, odd)
     conv_total, out_total = unpack(pieces, chans, width)
-
-    taps = []
-    for row in (grad_after, block_grad, grad_before):
-        taps += [moved(row, -1), row, moved(row, 1)]
-    act_grad = lax.dot_general(
-        jnp.concatenate(taps, axis=1),
-        jnp.transpose(conv_weight, (0, 1, 3, 2)).reshape(9 * chans, chans),
-        (((1,), (0,)), ((), ())),
-        preferred_element_type=f32,
-    ).astype(bf16)[None]
     return (tgt_grad, act_grad, out_total, conv_total)
 
 

time: 98.5 us -> 92.9 us (0.943)
  the two profiles are of different devices: /device:TPU:8 before, /device:TPU:1 now
where the time goes in v3:
time: 92.9 us; the launch traced here: 92.2 us
  starting transfers between devices  33.7 us (36%)
  blocking collectives  27.6 us (30%)
  Pallas kernels  19.1 us (21%)
  waiting for transfers between devices  9 us (10%)
  local copies, waits for them, and re-layouts  1.96 us (2%)
    all_to_all x1, blocking collectives, body(): joint = lax.all_to_all(joint, 'zh', 0, 0)  15.2 us
    all_to_all x1, blocking collectives, body(): joint = lax.all_to_all(joint, 'x', 0, 0)  12.4 us
    all_to_all x1, starting transfers between devices, body(): pieces = lax.all_to_all(pieces, NEAR, 0, 0)  10.1 us
    pallas_call x1, Pallas kernels, source_pass(): pl.pallas_call(corr_kernel, out_shape=(jax.ShapeDtypeStruct((tgt_width *...  9.43 us
    ppermute x1, starting transfers between devices, body(): input_linked = lax.ppermute(own_input, ALL, links)  6.59 us
    all_to_all x1, starting transfers between devices, body(): lax.all_to_all(hidden.reshape(src_rows, src_width, chans), TGT, 0, 0)  6.36 us
    ppermute x1, starting transfers between devices, body(): grad_linked = lax.ppermute(block_grad, ALL, links)  5.64 us
    pallas_call x1, Pallas kernels, target_pass(): pl.pallas_call(target_kernel, out_shape=(jax.ShapeDtypeStruct((steps, row...  5.26 us
  transfers between devices with their start and end apart: 8, of which 5 were waited for; matrix products, arithmetic and copies ran while one was open for 0% of the time, Pallas kernels for 7%

profile of v3, /device:TPU:1, one launch (start us, length us, event | category | flops | bytes accessed | tf_op | source)
XLA Modules:
  0.0 92.2 jit_solution(8414244758601982869)
XLA Ops:
  0.6 0.0 copy-start.4
  0.7 0.0 copy-start
  0.7 9.4 %source_pass.1 = (bf16[2048,1024]{1,0:T(8,128)(2,1)}, bf16[1024,128]{1,0:T(8,128)(2,1)}, f32[128,256]{1,0:T(8,128)}) custom-call(s32[1]{0:T(128)} %bitcast.2.first_ref, bf16[324,8,128]{2,1,0:T(8,128)(2,1)} %bitcast.16, s32[2,8,128]{2,1,0:T(8,128)} %cents_ref.1, bf16[8,256,256]{2,1,0:T(8,128)(2,1)} %targets_ref.1, bf16[1024,128]{1,0:T(8,128)(2,1)} %bitcast.9, ...), custom_call_target="tpu_custom_call" | custom-call | flops 4000000000 | bytes 7000000 | tf_op jit(solution)/shard_map/source_pass/pallas_call | solution.py:132
  10.1 6.4 %all-to-all-start = ((bf16[8,128,128]{2,1,0:T(8,128)(2,1)}), bf16[8,128,128]{2,1,0:T(8,128)(2,1)S(1)}, u32[]{:S(2)}, u32[]{:S(2)}) async-start(bf16[8,128,128]{2,1,0:T(8,128)(2,1)} %bitcast.15), calls=%async_computation | async-start | bytes 524288 | tf_op jit(solution)/shard_map/all_to_all | solution.py:463
  16.5 0.0 copy-done.4
  16.5 6.6 %collective-permute-start.1 = (bf16[128,128]{1,0:T(8,128)(2,1)S(1)}, bf16[128,128]{1,0:T(8,128)(2,1)S(1)}, u32[]{:S(2)}, u32[]{:S(2)}) collective-permute-start(bf16[128,128]{1,0:T(8,128)(2,1)S(1)} %bitcast.11), channel_id=1, source_target_pairs={{1,2},{3,4},{5,6},{7,8},{9,10},{11,12},{13,14},{15,16},{17,18},{19... | collective-permute-start | bytes 98312 | tf_op jit(solution)/shard_map/ppermute | solution.py:457
  23.1 0.1 collective-permute-start
  23.2 0.1 pad_add_fusion.at_ref
  23.2 1.4 %collective-permute-done.1.linked_ref = bf16[128,128]{1,0:T(8,128)(2,1)S(1)} collective-permute-done((bf16[128,128]{1,0:T(8,128)(2,1)S(1)}, bf16[128,128]{1,0:T(8,128)(2,1)S(1)}, u32[]{:S(2)}, u32[]{:S(2)}) %collective-permute-start.1) | collective-permute-done | bytes 32800 | tf_op jit(solution)/shard_map/ppermute | solution.py:457
  24.6 1.3 %collective-permute-done.paired_ref = bf16[128,128]{1,0:T(8,128)(2,1)S(1)} collective-permute-done((bf16[128,128]{1,0:T(8,128)(2,1)S(1)}, bf16[128,128]{1,0:T(8,128)(2,1)S(1)}, u32[]{:S(2)}, u32[]{:S(2)}) %collective-permute-start) | collective-permute-done | bytes 32800 | tf_op jit(solution)/shard_map/ppermute | solution.py:456
  25.9 0.0 all-to-all-done.parts_ref
  25.9 0.9 copy-done.3
  26.8 1.6 %weight_terms.1 = (bf16[128,128]{1,0:T(8,128)(2,1)S(1)}, bf16[16,32,384]{2,1,0:T(8,128)(2,1)}) custom-call(s32[2]{0:T(128)S(1)} %pad_add_fusion.at_ref, bf16[8,128,128]{2,1,0:T(8,128)(2,1)S(1)} %all-to-all-done.parts_ref, bf16[8,128,128]{2,1,0:T(8,128)(2,1)S(1)} %copy-done, bf16[128,128]{1,0:T(8,128)(2,1)S(1)} %collective-permute-done.paired_ref, ...), custom_call_target="tpu_custom_call" | custom-call | tf_op jit(solution)/shard_map/weight_terms/pallas_call | solution.py:270
  28.4 4.7 %all-to-all-start.1 = ((bf16[16,32,384]{2,1,0:T(8,128)(2,1)}), bf16[16,32,384]{2,1,0:T(8,128)(2,1)S(1)}, u32[]{:S(2)}, u32[]{:S(2)}) async-start(bf16[16,32,384]{2,1,0:T(8,128)(2,1)} %get-tuple-element.17), calls=%async_computation.1 | async-start | bytes 786432 | tf_op jit(solution)/shard_map/all_to_all | solution.py:471
  33.1 5.3 %target_pass.1 = (bf16[4,256,256]{2,1,0:T(8,128)(2,1)}, bf16[4,256,256]{2,1,0:T(8,128)(2,1)}) custom-call(s32[1]{0:T(128)} %bitcast.7.core_ref, bf16[4,4,128,1024]{3,2,1,0:T(8,128)(2,1)} %bitcast.14, bf16[1024,128]{1,0:T(8,128)(2,1)} %bitcast.10, bf16[128,256]{1,0:T(8,128)(2,1)} %weight_ref.4), custom_call_target="tpu_custom_call" | custom-call | flops 1073741824 | bytes 6500000 | tf_op jit(solution)/shard_map/target_pass/pallas_call | solution.py:206
  38.4 0.1 collective-permute-start.2
  38.5 2.0 %collective-permute-done.2.taken_ref = bf16[4,256,256]{2,1,0:T(8,128)(2,1)S(1)} collective-permute-done((bf16[4,256,256]{2,1,0:T(8,128)(2,1)}, bf16[4,256,256]{2,1,0:T(8,128)(2,1)S(1)}, u32[]{:S(2)}, u32[]{:S(2)}) %collective-permute-start.2) | collective-permute-done | bytes 524320 | tf_op jit(solution)/shard_map/ppermute | solution.py:466
  40.5 0.1 all-to-all-done.1.parts_ref
  40.6 1.0 %copy-done.1 = bf16[4,256,256]{2,1,0:T(8,128)(2,1)S(1)} copy-done((bf16[4,256,256]{2,1,0:T(8,128)(2,1)S(1)}, bf16[4,256,256]{2,1,0:T(8,128)(2,1)}, u32[]{:S(2)}) %copy-start.1) | copy-done | bytes 524312
  41.7 0.2 near_sum.1
  41.9 12.4 %all_to_all.25.parts_ref = bf16[4,304,256]{2,1,0:T(8,128)(2,1)S(1)} all-to-all(bf16[4,304,256]{2,1,0:T(8,128)(2,1)S(1)} %near_sum.1), channel_id=1, replica_groups=mesh['zh'=4,'x'=4,'c'=2,'y'=4,'zl'=2] {'x'}, dimensions={0} | all-to-all | bytes 1245184 | tf_op jit(solution)/shard_map/all_to_all | solution.py:475
  54.3 0.1 x_sum.1
  54.3 15.2 %all_to_all.26.parts_ref = bf16[4,112,256]{2,1,0:T(8,128)(2,1)S(1)} all-to-all(bf16[4,112,256]{2,1,0:T(8,128)(2,1)S(1)} %x_sum.1), channel_id=1, replica_groups=mesh['zh'=4,'x'=4,'c'=2,'y'=4,'zl'=2] {'zh'}, dimensions={0} | all-to-all | bytes 458752 | tf_op jit(solution)/shard_map/all_to_all | solution.py:478
  69.5 0.8 far_sum.1
  70.3 10.1 %all-to-all-start.4 = ((bf16[16,32,384]{2,1,0:T(8,128)(2,1)}), bf16[16,32,384]{2,1,0:T(8,128)(2,1)S(1)}, u32[]{:S(2)}, u32[]{:S(2)}) async-start(bf16[16,32,384]{2,1,0:T(8,128)(2,1)} %get-tuple-element.23), calls=%async_computation.4 | async-start | bytes 786432 | tf_op jit(solution)/shard_map/all_to_all | solution.py:482
  80.5 5.6 %collective-permute-start.4 = (bf16[128,128]{1,0:T(8,128)(2,1)S(1)}, bf16[128,128]{1,0:T(8,128)(2,1)S(1)}, u32[]{:S(2)}, u32[]{:S(2)}) collective-permute-start(bf16[128,128]{1,0:T(8,128)(2,1)S(1)} %get-tuple-element.22.grad_ref), channel_id=1, source_target_pairs={{1,2},{3,4},{5,6},{7,8},{9,10},{11,12},{13,14},{15,16},{17,18},{19... | collective-permute-start | bytes 98312 | tf_op jit(solution)/shard_map/ppermute | solution.py:473
  86.1 0.1 collective-permute-start.3
  86.2 4.1 %collective-permute-done.4.linked_ref = bf16[128,128]{1,0:T(8,128)(2,1)S(1)} collective-permute-done((bf16[128,128]{1,0:T(8,128)(2,1)S(1)}, bf16[128,128]{1,0:T(8,128)(2,1)S(1)}, u32[]{:S(2)}, u32[]{:S(2)}) %collective-permute-start.4) | collective-permute-done | bytes 32800 | tf_op jit(solution)/shard_map/ppermute | solution.py:473
  90.4 0.0 collective-permute-done.3.paired_ref
  90.4 0.9 %act_rows.1 = bf16[1,128,128]{2,1,0:T(8,128)(2,1)} custom-call(s32[1]{0:T(128)} %bitcast.1.at_ref, bf16[128,128]{1,0:T(8,128)(2,1)S(1)} %get-tuple-element.22.grad_ref, bf16[128,128]{1,0:T(8,128)(2,1)S(1)} %collective-permute-done.3.paired_ref, bf16[128,128]{1,0:T(8,128)(2,1)S(1)} %collective-permute-done.4.linked_ref, bf16[3,3,128,128]{3,2,1,0:T(8,128)(2,1)S(1)} %copy-done.2), custom_call_target="tpu_custom_call" | custom-call | tf_op jit(solution)/shard_map/act_rows/pallas_call | solution.py:368
  91.3 0.0 all-to-all-done.4.totals_ref
  91.3 0.9 unpack.1
  (5 shorter events, 0.0 us)
Async XLA Ops:
  0.6 15.8 %copy-start.4 = (bf16[1,128,128]{2,1,0:T(8,128)(2,1)S(1)}, bf16[1,128,128]{2,1,0:T(8,128)(2,1)}, u32[]{:S(2)}) copy-start(bf16[1,128,128]{2,1,0:T(8,128)(2,1)} %param.10) | copy-start | bytes 98308
  0.7 25.3 %copy-start = (bf16[8,128,128]{2,1,0:T(8,128)(2,1)S(1)}, bf16[8,128,128]{2,1,0:T(8,128)(2,1)}, u32[]{:S(2)}) copy-start(bf16[8,128,128]{2,1,0:T(8,128)(2,1)} %relu_ref.1) | copy-start | bytes 786436
  10.1 15.8 %all-to-all-start = ((bf16[8,128,128]{2,1,0:T(8,128)(2,1)}), bf16[8,128,128]{2,1,0:T(8,128)(2,1)S(1)}, u32[]{:S(2)}, u32[]{:S(2)}) async-start(bf16[8,128,128]{2,1,0:T(8,128)(2,1)} %bitcast.15), calls=%async_computation | async-start | bytes 524288 | tf_op jit(solution)/shard_map/all_to_all | solution.py:463
  16.5 8.2 %collective-permute-start.1 = (bf16[128,128]{1,0:T(8,128)(2,1)S(1)}, bf16[128,128]{1,0:T(8,128)(2,1)S(1)}, u32[]{:S(2)}, u32[]{:S(2)}) collective-permute-start(bf16[128,128]{1,0:T(8,128)(2,1)S(1)} %bitcast.11), channel_id=1, source_target_pairs={{1,2},{3,4},{5,6},{7,8},{9,10},{11,12},{13,14},{15,16},{17,18},{19... | collective-permute-start | bytes 98312 | tf_op jit(solution)/shard_map/ppermute | solution.py:457
  23.1 2.9 %collective-permute-start = (bf16[128,128]{1,0:T(8,128)(2,1)S(1)}, bf16[128,128]{1,0:T(8,128)(2,1)S(1)}, u32[]{:S(2)}, u32[]{:S(2)}) collective-permute-start(bf16[128,128]{1,0:T(8,128)(2,1)S(1)} %bitcast.12), channel_id=1, source_target_pairs={{0,1},{1,0},{2,3},{3,2},{4,5},{5,4},{6,7},{7,6},{8,9},{9,8},{10,11... | collective-permute-start | bytes 98312 | tf_op jit(solution)/shard_map/ppermute | solution.py:456
  25.9 0.9 copy-start.3
  28.4 12.3 %all-to-all-start.1 = ((bf16[16,32,384]{2,1,0:T(8,128)(2,1)}), bf16[16,32,384]{2,1,0:T(8,128)(2,1)S(1)}, u32[]{:S(2)}, u32[]{:S(2)}) async-start(bf16[16,32,384]{2,1,0:T(8,128)(2,1)} %get-tuple-element.17), calls=%async_computation.1 | async-start | bytes 786432 | tf_op jit(solution)/shard_map/all_to_all | solution.py:471
  33.1 57.3 %copy-start.2 = (bf16[3,3,128,128]{3,2,1,0:T(8,128)(2,1)S(1)}, bf16[3,3,128,128]{3,2,1,0:T(8,128)(2,1)}, u32[]{:S(2)}) copy-start(bf16[3,3,128,128]{3,2,1,0:T(8,128)(2,1)} %weight_ref.5) | copy-start | bytes 884740
  38.4 2.1 %collective-permute-start.2 = (bf16[4,256,256]{2,1,0:T(8,128)(2,1)}, bf16[4,256,256]{2,1,0:T(8,128)(2,1)S(1)}, u32[]{:S(2)}, u32[]{:S(2)}) collective-permute-start(bf16[4,256,256]{2,1,0:T(8,128)(2,1)} %get-tuple-element.20), channel_id=1, source_target_pairs={{0,8},{8,0},{1,9},{9,1},{2,10},{10,2},{3,11},{11,3},{4,12},{12,4},... | collective-permute-start | bytes 1572872 | tf_op jit(solution)/shard_map/ppermute | solution.py:466
  40.6 1.0 %copy-start.1 = (bf16[4,256,256]{2,1,0:T(8,128)(2,1)S(1)}, bf16[4,256,256]{2,1,0:T(8,128)(2,1)}, u32[]{:S(2)}) copy-start(bf16[4,256,256]{2,1,0:T(8,128)(2,1)} %get-tuple-element.19.kept_ref) | copy-start | bytes 1572868
  70.3 21.0 %all-to-all-start.4 = ((bf16[16,32,384]{2,1,0:T(8,128)(2,1)}), bf16[16,32,384]{2,1,0:T(8,128)(2,1)S(1)}, u32[]{:S(2)}, u32[]{:S(2)}) async-start(bf16[16,32,384]{2,1,0:T(8,128)(2,1)} %get-tuple-element.23), calls=%async_computation.4 | async-start | bytes 786432 | tf_op jit(solution)/shard_map/all_to_all | solution.py:482
  80.5 9.9 %collective-permute-start.4 = (bf16[128,128]{1,0:T(8,128)(2,1)S(1)}, bf16[128,128]{1,0:T(8,128)(2,1)S(1)}, u32[]{:S(2)}, u32[]{:S(2)}) collective-permute-start(bf16[128,128]{1,0:T(8,128)(2,1)S(1)} %get-tuple-element.22.grad_ref), channel_id=1, source_target_pairs={{1,2},{3,4},{5,6},{7,8},{9,10},{11,12},{13,14},{15,16},{17,18},{19... | collective-permute-start | bytes 98312 | tf_op jit(solution)/shard_map/ppermute | solution.py:473
  86.1 4.2 %collective-permute-start.3 = (bf16[128,128]{1,0:T(8,128)(2,1)S(1)}, bf16[128,128]{1,0:T(8,128)(2,1)S(1)}, u32[]{:S(2)}, u32[]{:S(2)}) collective-permute-start(bf16[128,128]{1,0:T(8,128)(2,1)S(1)} %get-tuple-element.22.grad_ref), channel_id=1, source_target_pairs={{0,1},{1,0},{2,3},{3,2},{4,5},{5,4},{6,7},{7,6},{8,9},{9,8},{10,11... | collective-permute-start | bytes 98312 | tf_op jit(solution)/shard_map/ppermute | solution.py:472

commit v4 on v3

--- a/solution.py
+++ b/solution.py
@@ -248,22 +248,12 @@
         near_input, near_grad, (((0,), (0,)), ((), ())), preferred_element_type=jnp.float32
     )
     near, _, across = terms_ref.shape
-    chans, width = out_ref.shape
-    out = jnp.concatenate(
-        [out_ref[...], jnp.zeros((chans, across - width), jnp.float32)], axis=1
-    )
-    terms_ref[...] = jnp.concatenate(
-        [
-            conv.reshape(near, conv.shape[0] // near, across),
-            out.reshape(near, chans // near, across),
-        ],
-        axis=1,
-    ).astype(jnp.bfloat16)
+    conv = conv.reshape(near, conv.shape[0] // near, across)
+    terms_ref[...] = jnp.concatenate([conv, out_ref[...]], axis=1).astype(jnp.bfloat16)
 
 
 def weight_terms(parts, post_relu, inputs, out_term, tgt_at, odd, near):
     count, src_width, chans = parts.shape
-    width = out_term.shape[1]
     whole = lambda *shape: pl.BlockSpec(shape, lambda r, f: (0,) * len(shape))
     across = 3 * chans
     down = (across + chans) // near
@@ -282,7 +272,7 @@
                 whole(src_width, chans),
                 whole(src_width, chans),
                 whole(src_width, chans),
-                whole(chans, width),
+                whole(*out_term.shape),
             ],
             out_specs=(whole(src_width, chans), whole(near, down, across)),
         ),
@@ -291,7 +281,7 @@
     )(jnp.stack([tgt_at, odd]), parts, post_relu, *inputs, out_term)
 
 
-def near_sum_kernel(parts_ref, kept_ref, taken_ref, joint_ref):
+def near_sum_kernel(parts_ref, both_ref, joint_ref):
     total = parts_ref[0].astype(jnp.float32)
     for k in range(1, parts_ref.shape[0]):
         total += parts_ref[k].astype(jnp.float32)
@@ -301,15 +291,14 @@
     total = jnp.concatenate(
         [total[:, :width], jnp.concatenate([last[: rows // 2], last[rows // 2 :]], axis=1)], axis=0
     ).astype(jnp.bfloat16)
-    block = kept_ref.shape[1]
+    block = both_ref.shape[1]
     for k in range(joint_ref.shape[0]):
-        both = kept_ref[k].astype(jnp.float32) + taken_ref[k].astype(jnp.float32)
-        joint_ref[k, :block] = both.astype(jnp.bfloat16)
+        joint_ref[k, :block] = both_ref[k]
         joint_ref[k, block:] = total
 
 
-def near_sum(parts, kept, taken):
-    count, block, width = kept.shape
+def near_sum(parts, both):
+    count, block, width = both.shape
     return pl.pallas_call(
         near_sum_kernel,
         out_shape=jax.ShapeDtypeStruct(
@@ -317,7 +306,7 @@
         ),
         compiler_params=pltpu.CompilerParams(vmem_limit_bytes=8 * 2**20),
         name="near_sum",
-    )(parts, kept, taken)
+    )(parts, both)
 
 
 def x_sum_kernel(parts_ref, joint_ref):
@@ -462,8 +451,12 @@
     )
     hidden = lax.all_to_all(hidden.reshape(src_rows, src_width, chans), TGT, 0, 0)
 
+    out_term = jnp.pad(
+        out_term.reshape(near, chans // near, width), ((0, 0), (0, 0), (0, 3 * chans - width))
+    )
     given, kept = target_pass(corr, relu_flat, out_weight, core_at, highs, lows)
     taken = lax.ppermute(given, "c", [(0, 1), (1, 0)])
+    both = (kept.astype(jnp.float32) + taken.astype(jnp.float32)).astype(jnp.bfloat16)
 
     block_grad, terms = weight_terms(
         hidden, post_relu, (input_paired, own_input, input_linked), out_term, tgt_at, odd, near
@@ -471,7 +464,7 @@
     terms = lax.all_to_all(terms, NEAR, 0, 0)
     grad_paired = lax.ppermute(block_grad, ALL, pairs)
     grad_linked = lax.ppermute(block_grad, ALL, links)
-    joint = near_sum(terms, kept, taken)
+    joint = near_sum(terms, both)
     joint = lax.all_to_all(joint, "x", 0, 0)
     cols = tgt_width // src_devices
     joint = x_sum(joint, highs, cols * tgt_rows)

time: 92.9 us -> 91.7 us (0.987)
  local copies, waits for them, and re-layouts: 1.96 us -> 0.03 us
  starting transfers between devices: 33.7 us -> 32.2 us
  waiting for transfers between devices: 9 us -> 10.5 us
  other arithmetic: 0.08 us -> 1.24 us
    all_to_all x1, waiting for transfers between devices: 0.15 us -> 6.36 us  [body(): terms = lax.all_to_all(terms, NEAR, 0, 0)]
    ppermute x1, waiting for transfers between devices: 2.03 us -> 0.01 us  [body(): taken = lax.ppermute(given, 'c', [(0, 1), (1, 0)])]
    unnamed x10 -> x8, local copies, waits for them, and re-layouts: 1.96 us -> 0.02 us
    ppermute x1, waiting for transfers between devices: 1.4 us -> 0.01 us  [body(): input_linked = lax.ppermute(own_input, ALL, links)]
    ppermute x1, waiting for transfers between devices: 1.27 us -> 0.01 us  [body(): input_paired = lax.ppermute(own_input, ALL, pairs)]
    convert_element_type x0 -> x1, other arithmetic: none -> 1.16 us  [body(): (kept.astype(jnp.float32) + taken.astype(jnp.float32)).astype(jnp.bfloat16)]
  transfers between devices with their start and end apart: 8 -> 8, of which waited for: 5 -> 2; matrix products, arithmetic and copies ran while one was open for 0% -> 1% of each run, Pallas kernels for 7% -> 8%
where the time goes in v4:
time: 91.7 us; the launch traced here: 91.1 us
  starting transfers between devices  32.2 us (35%)
  blocking collectives  27.3 us (30%)
  Pallas kernels  19 us (21%)
  waiting for transfers between devices  10.5 us (11%)
  other arithmetic  1.24 us (1%)
    all_to_all x1, blocking collectives, body(): joint = lax.all_to_all(joint, 'zh', 0, 0)  15.2 us
    all_to_all x1, blocking collectives, body(): joint = lax.all_to_all(joint, 'x', 0, 0)  12.1 us
    pallas_call x1, Pallas kernels, source_pass(): pl.pallas_call(corr_kernel, out_shape=(jax.ShapeDtypeStruct((tgt_width *...  9.43 us
    all_to_all x1, starting transfers between devices, body(): pieces = lax.all_to_all(pieces, NEAR, 0, 0)  9.23 us
    ppermute x1, starting transfers between devices, body(): input_linked = lax.ppermute(own_input, ALL, links)  6.59 us
    all_to_all x1, starting transfers between devices, body(): lax.all_to_all(hidden.reshape(src_rows, src_width, chans), TGT, 0, 0)  6.51 us
    all_to_all x1, waiting for transfers between devices, body(): terms = lax.all_to_all(terms, NEAR, 0, 0)  6.36 us
    ppermute x1, starting transfers between devices, body(): grad_linked = lax.ppermute(block_grad, ALL, links)  5.64 us
  transfers between devices with their start and end apart: 8, of which 2 were waited for; matrix products, arithmetic and copies ran while one was open for 1% of the time, Pallas kernels for 8%

profile of v4, /device:TPU:1, one launch (start us, length us, event | category | flops | bytes accessed | tf_op | source)
XLA Modules:
  0.0 91.1 jit_solution(5604217326366868277)
XLA Ops:
  0.6 0.0 copy-start.2
  0.7 9.4 %source_pass.1 = (bf16[2048,1024]{1,0:T(8,128)(2,1)}, bf16[1024,128]{1,0:T(8,128)(2,1)}, f32[128,256]{1,0:T(8,128)}) custom-call(s32[1]{0:T(128)} %bitcast.2.first_ref, bf16[324,8,128]{2,1,0:T(8,128)(2,1)} %bitcast.18, s32[2,8,128]{2,1,0:T(8,128)} %cents_ref.1, bf16[8,256,256]{2,1,0:T(8,128)(2,1)} %targets_ref.1, bf16[1024,128]{1,0:T(8,128)(2,1)} %bitcast.10, ...), custom_call_target="tpu_custom_call" | custom-call | flops 4000000000 | bytes 7000000 | tf_op jit(solution)/shard_map/source_pass/pallas_call | solution.py:132
  10.1 6.5 %all-to-all-start = ((bf16[8,128,128]{2,1,0:T(8,128)(2,1)}), bf16[8,128,128]{2,1,0:T(8,128)(2,1)S(1)}, u32[]{:S(2)}, u32[]{:S(2)}) async-start(bf16[8,128,128]{2,1,0:T(8,128)(2,1)} %bitcast.16), calls=%async_computation | async-start | bytes 524288 | tf_op jit(solution)/shard_map/all_to_all | solution.py:452
  16.6 0.0 copy-done.2
  16.6 6.6 %collective-permute-start.1 = (bf16[128,128]{1,0:T(8,128)(2,1)S(1)}, bf16[128,128]{1,0:T(8,128)(2,1)S(1)}, u32[]{:S(2)}, u32[]{:S(2)}) collective-permute-start(bf16[128,128]{1,0:T(8,128)(2,1)S(1)} %bitcast.12), channel_id=1, source_target_pairs={{1,2},{3,4},{5,6},{7,8},{9,10},{11,12},{13,14},{15,16},{17,18},{19... | collective-permute-start | bytes 98312 | tf_op jit(solution)/shard_map/ppermute | solution.py:446
  23.2 0.1 collective-permute-start
  23.3 5.2 %target_pass.1 = (bf16[4,256,256]{2,1,0:T(8,128)(2,1)}, bf16[4,256,256]{2,1,0:T(8,128)(2,1)}) custom-call(s32[1]{0:T(128)} %bitcast.8.core_ref, bf16[4,4,128,1024]{3,2,1,0:T(8,128)(2,1)} %bitcast.15, bf16[1024,128]{1,0:T(8,128)(2,1)} %bitcast.11, bf16[128,256]{1,0:T(8,128)(2,1)} %weight_ref.4), custom_call_target="tpu_custom_call" | custom-call | flops 1073741824 | bytes 6500000 | tf_op jit(solution)/shard_map/target_pass/pallas_call | solution.py:206
  28.5 0.0 collective-permute-start.2
  28.5 0.1 pad_add_fusion.at_ref
  28.6 0.0 copy-done.3
  28.6 0.0 copy-start.1
  28.6 0.0 collective-permute-done.1.linked_ref
  28.6 0.0 collective-permute-done.paired_ref
  28.6 0.0 all-to-all-done.parts_ref
  28.6 1.6 %weight_terms.1 = (bf16[128,128]{1,0:T(8,128)(2,1)S(1)}, bf16[16,32,384]{2,1,0:T(8,128)(2,1)}) custom-call(s32[2]{0:T(128)S(1)} %pad_add_fusion.at_ref, bf16[8,128,128]{2,1,0:T(8,128)(2,1)S(1)} %all-to-all-done.parts_ref, bf16[8,128,128]{2,1,0:T(8,128)(2,1)S(1)} %copy-done, bf16[128,128]{1,0:T(8,128)(2,1)S(1)} %collective-permute-done.paired_ref, ...), custom_call_target="tpu_custom_call" | custom-call | tf_op jit(solution)/shard_map/weight_terms/pallas_call | solution.py:260
  30.2 4.1 %all-to-all-start.1 = ((bf16[16,32,384]{2,1,0:T(8,128)(2,1)}), bf16[16,32,384]{2,1,0:T(8,128)(2,1)S(1)}, u32[]{:S(2)}, u32[]{:S(2)}) async-start(bf16[16,32,384]{2,1,0:T(8,128)(2,1)} %get-tuple-element.17), calls=%async_computation.1 | async-start | bytes 786432 | tf_op jit(solution)/shard_map/all_to_all | solution.py:464
  34.3 0.0 collective-permute-done.2
  34.3 1.2 %add_convert_fusion.both_ref = bf16[4,256,256]{2,1,0:T(8,128)(2,1)S(1)} fusion(bf16[4,256,256]{2,1,0:T(8,128)(2,1)S(1)} %collective-permute-done.2, bf16[4,256,256]{2,1,0:T(8,128)(2,1)} %get-tuple-element.19), kind=kLoop, calls=%fused_computation | loop fusion | flops 1048576 | bytes 1572864 | tf_op jit(solution)/shard_map/convert_element_type | solution.py:459
  35.5 6.4 %all-to-all-done.1.parts_ref = bf16[16,32,384]{2,1,0:T(8,128)(2,1)S(1)} async-done(((bf16[16,32,384]{2,1,0:T(8,128)(2,1)}), bf16[16,32,384]{2,1,0:T(8,128)(2,1)S(1)}, u32[]{:S(2)}, u32[]{:S(2)}) %all-to-all-start.1) | async-done | bytes 393248 | tf_op jit(solution)/shard_map/all_to_all | solution.py:464
  41.8 0.1 near_sum.1
  41.9 12.1 %all_to_all.25.parts_ref = bf16[4,304,256]{2,1,0:T(8,128)(2,1)S(1)} all-to-all(bf16[4,304,256]{2,1,0:T(8,128)(2,1)S(1)} %near_sum.1), channel_id=1, replica_groups=mesh['zh'=4,'x'=4,'c'=2,'y'=4,'zl'=2] {'x'}, dimensions={0} | all-to-all | bytes 1245184 | tf_op jit(solution)/shard_map/all_to_all | solution.py:468
  54.0 0.1 x_sum.1
  54.1 15.2 %all_to_all.26.parts_ref = bf16[4,112,256]{2,1,0:T(8,128)(2,1)S(1)} all-to-all(bf16[4,112,256]{2,1,0:T(8,128)(2,1)S(1)} %x_sum.1), channel_id=1, replica_groups=mesh['zh'=4,'x'=4,'c'=2,'y'=4,'zl'=2] {'zh'}, dimensions={0} | all-to-all | bytes 458752 | tf_op jit(solution)/shard_map/all_to_all | solution.py:471
  69.3 0.8 far_sum.1
  70.1 9.2 %all-to-all-start.4 = ((bf16[16,32,384]{2,1,0:T(8,128)(2,1)}), bf16[16,32,384]{2,1,0:T(8,128)(2,1)S(1)}, u32[]{:S(2)}, u32[]{:S(2)}) async-start(bf16[16,32,384]{2,1,0:T(8,128)(2,1)} %get-tuple-element.23), calls=%async_computation.4 | async-start | bytes 786432 | tf_op jit(solution)/shard_map/all_to_all | solution.py:475
  79.3 5.6 %collective-permute-start.4 = (bf16[128,128]{1,0:T(8,128)(2,1)S(1)}, bf16[128,128]{1,0:T(8,128)(2,1)S(1)}, u32[]{:S(2)}, u32[]{:S(2)}) collective-permute-start(bf16[128,128]{1,0:T(8,128)(2,1)S(1)} %get-tuple-element.22.grad_ref), channel_id=1, source_target_pairs={{1,2},{3,4},{5,6},{7,8},{9,10},{11,12},{13,14},{15,16},{17,18},{19... | collective-permute-start | bytes 98312 | tf_op jit(solution)/shard_map/ppermute | solution.py:466
  85.0 0.1 collective-permute-start.3
  85.1 4.1 %collective-permute-done.4.linked_ref = bf16[128,128]{1,0:T(8,128)(2,1)S(1)} collective-permute-done((bf16[128,128]{1,0:T(8,128)(2,1)S(1)}, bf16[128,128]{1,0:T(8,128)(2,1)S(1)}, u32[]{:S(2)}, u32[]{:S(2)}) %collective-permute-start.4) | collective-permute-done | bytes 32800 | tf_op jit(solution)/shard_map/ppermute | solution.py:466
  89.2 0.0 collective-permute-done.3.paired_ref
  89.2 0.9 %act_rows.1 = bf16[1,128,128]{2,1,0:T(8,128)(2,1)} custom-call(s32[1]{0:T(128)} %bitcast.1.at_ref, bf16[128,128]{1,0:T(8,128)(2,1)S(1)} %get-tuple-element.22.grad_ref, bf16[128,128]{1,0:T(8,128)(2,1)S(1)} %collective-permute-done.3.paired_ref, bf16[128,128]{1,0:T(8,128)(2,1)S(1)} %collective-permute-done.4.linked_ref, bf16[3,3,128,128]{3,2,1,0:T(8,128)(2,1)S(1)} %copy-done.1), custom_call_target="tpu_custom_call" | custom-call | tf_op jit(solution)/shard_map/act_rows/pallas_call | solution.py:357
  90.2 0.0 all-to-all-done.4.totals_ref
  90.2 0.9 unpack.1
  (5 shorter events, 0.0 us)
Async XLA Ops:
  0.6 16.0 %copy-start.2 = (bf16[1,128,128]{2,1,0:T(8,128)(2,1)S(1)}, bf16[1,128,128]{2,1,0:T(8,128)(2,1)}, u32[]{:S(2)}) copy-start(bf16[1,128,128]{2,1,0:T(8,128)(2,1)} %param.10) | copy-start | bytes 98308
  10.1 18.5 %copy-start.3 = (f32[128,256]{1,0:T(8,128)S(1)}, f32[128,256]{1,0:T(8,128)}, u32[]{:S(2)}) copy-start(f32[128,256]{1,0:T(8,128)} %get-tuple-element.16) | copy-start | bytes 393220
  10.1 18.6 %copy-start = (bf16[8,128,128]{2,1,0:T(8,128)(2,1)S(1)}, bf16[8,128,128]{2,1,0:T(8,128)(2,1)}, u32[]{:S(2)}) copy-start(bf16[8,128,128]{2,1,0:T(8,128)(2,1)} %relu_ref.1) | copy-start | bytes 786436
  10.1 18.5 %all-to-all-start = ((bf16[8,128,128]{2,1,0:T(8,128)(2,1)}), bf16[8,128,128]{2,1,0:T(8,128)(2,1)S(1)}, u32[]{:S(2)}, u32[]{:S(2)}) async-start(bf16[8,128,128]{2,1,0:T(8,128)(2,1)} %bitcast.16), calls=%async_computation | async-start | bytes 524288 | tf_op jit(solution)/shard_map/all_to_all | solution.py:452
  16.6 12.0 %collective-permute-start.1 = (bf16[128,128]{1,0:T(8,128)(2,1)S(1)}, bf16[128,128]{1,0:T(8,128)(2,1)S(1)}, u32[]{:S(2)}, u32[]{:S(2)}) collective-permute-start(bf16[128,128]{1,0:T(8,128)(2,1)S(1)} %bitcast.12), channel_id=1, source_target_pairs={{1,2},{3,4},{5,6},{7,8},{9,10},{11,12},{13,14},{15,16},{17,18},{19... | collective-permute-start | bytes 98312 | tf_op jit(solution)/shard_map/ppermute | solution.py:446
  23.2 5.4 %collective-permute-start = (bf16[128,128]{1,0:T(8,128)(2,1)S(1)}, bf16[128,128]{1,0:T(8,128)(2,1)S(1)}, u32[]{:S(2)}, u32[]{:S(2)}) collective-permute-start(bf16[128,128]{1,0:T(8,128)(2,1)S(1)} %bitcast.13), channel_id=1, source_target_pairs={{0,1},{1,0},{2,3},{3,2},{4,5},{5,4},{6,7},{7,6},{8,9},{9,8},{10,11... | collective-permute-start | bytes 98312 | tf_op jit(solution)/shard_map/ppermute | solution.py:445
  28.5 5.8 %collective-permute-start.2 = (bf16[4,256,256]{2,1,0:T(8,128)(2,1)}, bf16[4,256,256]{2,1,0:T(8,128)(2,1)S(1)}, u32[]{:S(2)}, u32[]{:S(2)}) collective-permute-start(bf16[4,256,256]{2,1,0:T(8,128)(2,1)} %get-tuple-element.20), channel_id=1, source_target_pairs={{0,8},{8,0},{1,9},{9,1},{2,10},{10,2},{3,11},{11,3},{4,12},{12,4},... | collective-permute-start | bytes 1572872 | tf_op jit(solution)/shard_map/ppermute | solution.py:458
  28.6 60.6 %copy-start.1 = (bf16[3,3,128,128]{3,2,1,0:T(8,128)(2,1)S(1)}, bf16[3,3,128,128]{3,2,1,0:T(8,128)(2,1)}, u32[]{:S(2)}) copy-start(bf16[3,3,128,128]{3,2,1,0:T(8,128)(2,1)} %weight_ref.5) | copy-start | bytes 884740
  30.2 11.6 %all-to-all-start.1 = ((bf16[16,32,384]{2,1,0:T(8,128)(2,1)}), bf16[16,32,384]{2,1,0:T(8,128)(2,1)S(1)}, u32[]{:S(2)}, u32[]{:S(2)}) async-start(bf16[16,32,384]{2,1,0:T(8,128)(2,1)} %get-tuple-element.17), calls=%async_computation.1 | async-start | bytes 786432 | tf_op jit(solution)/shard_map/all_to_all | solution.py:464
  70.1 20.1 %all-to-all-start.4 = ((bf16[16,32,384]{2,1,0:T(8,128)(2,1)}), bf16[16,32,384]{2,1,0:T(8,128)(2,1)S(1)}, u32[]{:S(2)}, u32[]{:S(2)}) async-start(bf16[16,32,384]{2,1,0:T(8,128)(2,1)} %get-tuple-element.23), calls=%async_computation.4 | async-start | bytes 786432 | tf_op jit(solution)/shard_map/all_to_all | solution.py:475
  79.3 9.9 %collective-permute-start.4 = (bf16[128,128]{1,0:T(8,128)(2,1)S(1)}, bf16[128,128]{1,0:T(8,128)(2,1)S(1)}, u32[]{:S(2)}, u32[]{:S(2)}) collective-permute-start(bf16[128,128]{1,0:T(8,128)(2,1)S(1)} %get-tuple-element.22.grad_ref), channel_id=1, source_target_pairs={{1,2},{3,4},{5,6},{7,8},{9,10},{11,12},{13,14},{15,16},{17,18},{19... | collective-permute-start | bytes 98312 | tf_op jit(solution)/shard_map/ppermute | solution.py:466
  85.0 4.2 %collective-permute-start.3 = (bf16[128,128]{1,0:T(8,128)(2,1)S(1)}, bf16[128,128]{1,0:T(8,128)(2,1)S(1)}, u32[]{:S(2)}, u32[]{:S(2)}) collective-permute-start(bf16[128,128]{1,0:T(8,128)(2,1)S(1)} %get-tuple-element.22.grad_ref), channel_id=1, source_target_pairs={{0,1},{1,0},{2,3},{3,2},{4,5},{5,4},{6,7},{7,6},{8,9},{9,8},{10,11... | collective-permute-start | bytes 98312 | tf_op jit(solution)/shard_map/ppermute | solution.py:465

commit v5 on v4

--- a/solution.py
+++ b/solution.py
@@ -15,45 +15,49 @@
 NEAR = ("c", "y", "zl")
 
 
-def corr_kernel(
-    first_ref,
+def source_kernel(
+    highs,
+    at_ref,
     grads_ref,
     cents_ref,
     targets_ref,
     relu_ref,
     weight_ref,
-    corr_ref,
     hidden_ref,
     out_ref,
+    given_ref,
+    kept_ref,
     wide,
     level_sums,
     tall,
     targets,
+    feats,
+    sums,
+    corr_a,
+    corr_b,
 ):
-    step_no = pl.program_id(0)
     tgt_rows, tgt_width, width = targets_ref.shape
-    lanes = grads_ref.shape[2]
-    pair_rows = corr_ref.shape[1] // lanes
+    src_rows, lanes = grads_ref.shape[1:]
+    pair = 2 * lanes
     tile = (tgt_rows, lanes)
-
-    @pl.when(step_no == 0)
-    def _():
-        wide[...] = grads_ref[...].astype(jnp.float32)
-        for h in range(width // lanes):
-            part = slice(h * lanes, (h + 1) * lanes)
-            for y in range(tgt_rows):
-                rows = targets_ref[y, :, part].astype(jnp.float32)
-                tall[pl.ds(y, tgt_width, stride=tgt_rows), :] = rows
-            targets[:, part] = tall[...].astype(jnp.bfloat16)
-        out_ref[...] = jnp.zeros_like(out_ref)
-
-    def build(half, carry):
-        row_no = step_no * pair_rows + half
-        at = pl.ds(pl.multiple_of(half * lanes, lanes), lanes)
-        center_y = jnp.broadcast_to(cents_ref[0, pl.ds(row_no, 1), :], tile)
-        center_x = jnp.broadcast_to(cents_ref[1, pl.ds(row_no, 1), :], tile)
-        ys = first_ref[0] + lax.broadcasted_iota(jnp.int32, tile, 0)
-        zero = jnp.zeros(tile, jnp.float32)
+    f32, bf16 = jnp.float32, jnp.bfloat16
+    scale = 1.0 / math.sqrt(width)
+    across = (((1,), (1,)), ((), ()))
+    down = (((0,), (0,)), ((), ()))
+
+    wide[...] = grads_ref[...].astype(f32)
+    for h in range(width // lanes):
+        part = slice(h * lanes, (h + 1) * lanes)
+        for y in range(tgt_rows):
+            tall[pl.ds(y, tgt_width, stride=tgt_rows), :] = targets_ref[y, :, part].astype(f32)
+        targets[:, part] = tall[...].astype(bf16)
+    feats[...] = jnp.dot(relu_ref[...], weight_ref[...], preferred_element_type=f32).astype(bf16)
+
+    def build(row_no, corr, at):
+        center_y = jnp.broadcast_to(cents_ref[0, row_no : row_no + 1, :], tile)
+        center_x = jnp.broadcast_to(cents_ref[1, row_no : row_no + 1, :], tile)
+        ys = at_ref[0] + lax.broadcasted_iota(jnp.int32, tile, 0)
+        zero = jnp.zeros(tile, f32)
 
         def spread(level):
             row_off = lax.shift_right_arithmetic(ys, level) - (
@@ -64,7 +68,7 @@
             for b in range(9):
                 acc = zero
                 for a in range(9):
-                    entry = wide[81 * level + 9 * a + b, pl.ds(row_no, 1), :]
+                    entry = wide[81 * level + 9 * a + b, row_no : row_no + 1, :]
                     acc = jnp.where(hits[a], jnp.broadcast_to(entry, tile), acc)
                 picked.append(acc * (0.25**level) if level else acc)
             start = lax.shift_right_arithmetic(center_x, level) - 4
@@ -98,131 +102,87 @@
                 under = level_sums[coarse + (x >> 1)]
                 left = jnp.where(homes[j] == q, slots[j], 0.0) + under
                 right = jnp.where(homes[j + 1] == q, slots[j + 1], 0.0) + under
-                pair = jnp.concatenate([left, right], axis=0).astype(jnp.bfloat16)
-                corr_ref[x * tgt_rows : (x + 2) * tgt_rows, at] = pair
-        return carry
-
-    lax.fori_loop(0, pair_rows, build, 0)
-    src = lax.dot_general(
-        corr_ref[...],
-        targets[...],
-        (((0,), (0,)), ((), ())),
-        preferred_element_type=jnp.float32,
-    )
-    exact = src * (1.0 / math.sqrt(width))
-    src = exact.astype(jnp.bfloat16)
-    rest = (exact - src.astype(jnp.float32)).astype(jnp.bfloat16)
-    across = (((1,), (1,)), ((), ()))
-    hidden = lax.dot_general(
-        src, weight_ref[...], across, preferred_element_type=jnp.float32
-    ) + lax.dot_general(rest, weight_ref[...], across, preferred_element_type=jnp.float32)
-    hidden_ref[...] = hidden.astype(jnp.bfloat16)
-    out_ref[...] += lax.dot_general(
-        relu_ref[...], src, (((0,), (0,)), ((), ())), preferred_element_type=jnp.float32
-    )
-
-
-def source_pass(upstream, centers, relu_flat, target_feats, out_weight, row_first):
+                both = jnp.concatenate([left, right], axis=0).astype(bf16)
+                corr[x * tgt_rows : (x + 2) * tgt_rows, at : at + lanes] = both
+
+    def products(step, corr):
+        at = pl.ds(pl.multiple_of(step * pair, pair), pair)
+        exact = lax.dot_general(corr[...], targets[...], down, preferred_element_type=f32) * scale
+        src = exact.astype(bf16)
+        rest = (exact - src.astype(f32)).astype(bf16)
+        hidden = lax.dot_general(src, weight_ref[...], across, preferred_element_type=f32)
+        hidden += lax.dot_general(rest, weight_ref[...], across, preferred_element_type=f32)
+        hidden_ref[at, :] = hidden.astype(bf16)
+        out = lax.dot_general(relu_ref[at, :], src, down, preferred_element_type=f32)
+        part = jnp.dot(corr[...], feats[at, :], preferred_element_type=f32)
+        return out, part
+
+    steps = src_rows // 2
+    ring = (corr_a, corr_b)
+    for half in range(2):
+        build(half, ring[0], half * lanes)
+    for step in range(steps):
+        out, part = products(step, ring[step % 2])
+        if step == 0:
+            out_ref[...] = out
+            sums[...] = part
+        else:
+            out_ref[...] += out
+            if step < steps - 1:
+                sums[...] += part
+        if step < steps - 1:
+            for half in range(2):
+                build(2 * step + 2 + half, ring[(step + 1) % 2], half * lanes)
+    count, block, _ = given_ref.shape
+    single = block // highs
+    total = ((sums[...] + part) * scale).astype(bf16).reshape(highs, count, 2, single, width)
+    first = at_ref[1] == 0
+
+    @pl.when(first)
+    def _():
+        for k in range(count):
+            given_ref[k] = total[:, k, 1].reshape(block, width)
+            kept_ref[k] = total[:, k, 0].reshape(block, width)
+
+    @pl.when(jnp.logical_not(first))
+    def _():
+        for k in range(count):
+            given_ref[k] = total[:, k, 0].reshape(block, width)
+            kept_ref[k] = total[:, k, 1].reshape(block, width)
+
+
+def source_pass(upstream, centers, target_feats, relu_flat, out_weight, at, highs, lows):
     src_rows, src_width, lookups = upstream.shape
     tgt_rows, tgt_width, width = target_feats.shape
     chans = relu_flat.shape[1]
-    pair = 2 * src_width
-    grads = jnp.transpose(upstream, (2, 0, 1))
-    whole = lambda *shape: pl.BlockSpec(shape, lambda r, f: (0,) * len(shape))
-    return pl.pallas_call(
-        corr_kernel,
+    sources, cells = src_rows * src_width, tgt_rows * tgt_width
+    f32, bf16 = jnp.float32, jnp.bfloat16
+    part = jax.ShapeDtypeStruct((lows, cells // lows // 2, width), bf16)
+    return pl.pallas_call(
+        functools.partial(source_kernel, highs),
         out_shape=(
-            jax.ShapeDtypeStruct((tgt_width * tgt_rows, src_rows * src_width), jnp.bfloat16),
-            jax.ShapeDtypeStruct((src_rows * src_width, chans), jnp.bfloat16),
-            jax.ShapeDtypeStruct((chans, width), jnp.float32),
-        ),
-        grid_spec=pltpu.PrefetchScalarGridSpec(
-            num_scalar_prefetch=1,
-            grid=(src_rows // 2,),
-            in_specs=[
-                whole(lookups, src_rows, src_width),
-                whole(2, src_rows, src_width),
-                whole(tgt_rows, tgt_width, width),
-                pl.BlockSpec((pair, chans), lambda r, f: (r, 0)),
-                whole(chans, width),
-            ],
-            out_specs=(
-                pl.BlockSpec((tgt_width * tgt_rows, pair), lambda r, f: (0, r)),
-                pl.BlockSpec((pair, chans), lambda r, f: (r, 0)),
-                whole(chans, width),
-            ),
-            scratch_shapes=[
-                pltpu.VMEM((lookups, src_rows, src_width), jnp.float32),
-                pltpu.VMEM((tgt_width, tgt_rows, src_width), jnp.float32),
-                pltpu.VMEM((tgt_width * tgt_rows, src_width), jnp.float32),
-                pltpu.VMEM((tgt_width * tgt_rows, width), jnp.bfloat16),
-            ],
-        ),
-        compiler_params=pltpu.CompilerParams(dimension_semantics=("arbitrary",)),
+            jax.ShapeDtypeStruct((sources, chans), bf16),
+            jax.ShapeDtypeStruct((chans, width), f32),
+            part,
+            part,
+        ),
+        in_specs=[pl.BlockSpec(memory_space=pltpu.SMEM)] + [pl.BlockSpec(memory_space=pltpu.VMEM)] * 5,
+        out_specs=[pl.BlockSpec(memory_space=pltpu.VMEM)] * 4,
+        scratch_shapes=[
+            pltpu.VMEM((lookups, src_rows, src_width), f32),
+            pltpu.VMEM((tgt_width, tgt_rows, src_width), f32),
+            pltpu.VMEM((cells, src_width), f32),
+            pltpu.VMEM((cells, width), bf16),
+            pltpu.VMEM((sources, width), bf16),
+            pltpu.VMEM((cells, width), f32),
+            pltpu.VMEM((cells, 2 * src_width), bf16),
+            pltpu.VMEM((cells, 2 * src_width), bf16),
+        ],
         cost_estimate=pl.CostEstimate(
-            flops=4_000_000_000, bytes_accessed=7_000_000, transcendentals=0
+            flops=4_000_000_000, bytes_accessed=4_000_000, transcendentals=0
         ),
         name="source_pass",
-    )(row_first.reshape(1), grads, centers, target_feats, relu_flat, out_weight)
-
-
-def target_kernel(core_ref, corr_ref, relu_ref, weight_ref, given_ref, kept_ref, feats):
-    @pl.when(pl.program_id(0) == 0)
-    def _():
-        feats[...] = jnp.dot(
-            relu_ref[...], weight_ref[...], preferred_element_type=jnp.float32
-        ).astype(jnp.bfloat16)
-
-    highs, _, both, sources = corr_ref.shape
-    width = given_ref.shape[2]
-    block = both // 2
-    part = jnp.dot(
-        corr_ref[...].reshape(highs * both, sources),
-        feats[...],
-        preferred_element_type=jnp.float32,
-    )
-    part = (part * (1.0 / math.sqrt(width))).astype(jnp.bfloat16).reshape(highs, 2, block, width)
-    rows = highs * block
-    first = core_ref[0] == 0
-
-    @pl.when(first)
-    def _():
-        given_ref[0] = part[:, 1].reshape(rows, width)
-        kept_ref[0] = part[:, 0].reshape(rows, width)
-
-    @pl.when(jnp.logical_not(first))
-    def _():
-        given_ref[0] = part[:, 0].reshape(rows, width)
-        kept_ref[0] = part[:, 1].reshape(rows, width)
-
-
-def target_pass(corr, relu_flat, out_weight, core_at, highs, steps):
-    cells, sources = corr.shape
-    chans, width = out_weight.shape
-    rows = cells // steps // 2
-    whole = lambda *shape: pl.BlockSpec(shape, lambda r, f: (0,) * len(shape))
-    part = pl.BlockSpec((1, rows, width), lambda r, f: (r, 0, 0))
-    both = cells // steps // highs
-    return pl.pallas_call(
-        target_kernel,
-        out_shape=(jax.ShapeDtypeStruct((steps, rows, width), jnp.bfloat16),) * 2,
-        grid_spec=pltpu.PrefetchScalarGridSpec(
-            num_scalar_prefetch=1,
-            grid=(steps,),
-            in_specs=[
-                pl.BlockSpec((highs, 1, both, sources), lambda r, f: (0, r, 0, 0)),
-                whole(sources, chans),
-                whole(chans, width),
-            ],
-            out_specs=(part, part),
-            scratch_shapes=[pltpu.VMEM((sources, width), jnp.bfloat16)],
-        ),
-        compiler_params=pltpu.CompilerParams(dimension_semantics=("arbitrary",)),
-        cost_estimate=pl.CostEstimate(
-            flops=2 * cells * sources * width, bytes_accessed=6_500_000, transcendentals=0
-        ),
-        name="target_pass",
-    )(core_at.reshape(1), corr.reshape(highs, steps, both, sources), relu_flat, out_weight)
+    )(at, jnp.transpose(upstream, (2, 0, 1)), centers, target_feats, relu_flat, out_weight)
 
 
 def shifted(wide):
@@ -446,15 +406,21 @@
     input_linked = lax.ppermute(own_input, ALL, links)
 
     relu_flat = post_relu.reshape(src_rows * src_width, chans)
-    corr, hidden, out_term = source_pass(
-        upstream, centers, relu_flat, target_feats, out_weight, tgt_at * tgt_rows
+    hidden, out_term, given, kept = source_pass(
+        upstream,
+        centers,
+        target_feats,
+        relu_flat,
+        out_weight,
+        jnp.stack([tgt_at * tgt_rows, core_at]),
+        highs,
+        lows,
     )
     hidden = lax.all_to_all(hidden.reshape(src_rows, src_width, chans), TGT, 0, 0)
 
     out_term = jnp.pad(
         out_term.reshape(near, chans // near, width), ((0, 0), (0, 0), (0, 3 * chans - width))
     )
-    given, kept = target_pass(corr, relu_flat, out_weight, core_at, highs, lows)
     taken = lax.ppermute(given, "c", [(0, 1), (1, 0)])
     both = (kept.astype(jnp.float32) + taken.astype(jnp.float32)).astype(jnp.bfloat16)
 

time: 91.7 us -> 90.3 us (0.985)
  Pallas kernels: 19 us -> 13.2 us
  waiting for transfers between devices: 10.5 us -> 14.1 us
  starting transfers between devices: 32.2 us -> 33.4 us
    pallas_call x2 -> x1, Pallas kernels: 14.6 us -> 8.86 us  [source_pass(): pl.pallas_call(functools.partial(source_kernel, highs), out_shape=(jax.Sh...]
    ppermute x1, waiting for transfers between devices: 0.01 us -> 1.28 us  [body(): input_linked = lax.ppermute(own_input, ALL, links)]
    ppermute x1, waiting for transfers between devices: 0.01 us -> 1.27 us  [body(): input_paired = lax.ppermute(own_input, ALL, pairs)]
    convert_element_type x1, other arithmetic: 1.16 us -> 0.13 us  [body(): (kept.astype(jnp.float32) + taken.astype(jnp.float32)).astype(jnp.bfloat16)]
    all_to_all x1, waiting for transfers between devices: 6.36 us -> 7.39 us  [body(): terms = lax.all_to_all(terms, NEAR, 0, 0)]
  transfers between devices with their start and end apart: 8 -> 8, of which waited for: 2 -> 4; matrix products, arithmetic and copies ran while one was open for 1% -> 0% of each run, Pallas kernels for 8% -> 3%
where the time goes in v5:
time: 90.3 us; the launch traced here: 89.8 us
  starting transfers between devices  33.4 us (37%)
  blocking collectives  27.6 us (31%)
  waiting for transfers between devices  14.1 us (16%)
  Pallas kernels  13.2 us (15%)
    all_to_all x1, blocking collectives, body(): joint = lax.all_to_all(joint, 'zh', 0, 0)  15.2 us
    all_to_all x1, blocking collectives, body(): joint = lax.all_to_all(joint, 'x', 0, 0)  12.4 us
    all_to_all x1, starting transfers between devices, body(): pieces = lax.all_to_all(pieces, NEAR, 0, 0)  9.36 us
    pallas_call x1, Pallas kernels, source_pass(): pl.pallas_call(functools.partial(source_kernel, highs), out_shape=(jax.Sh...  8.86 us
    all_to_all x1, waiting for transfers between devices, body(): terms = lax.all_to_all(terms, NEAR, 0, 0)  7.39 us
    ppermute x1, starting transfers between devices, body(): input_linked = lax.ppermute(own_input, ALL, links)  6.72 us
    all_to_all x1, starting transfers between devices, body(): lax.all_to_all(hidden.reshape(src_rows, src_width, chans), TGT, 0, 0)  6.5 us
    ppermute x1, starting transfers between devices, body(): grad_linked = lax.ppermute(block_grad, ALL, links)  5.64 us
  transfers between devices with their start and end apart: 8, of which 4 were waited for; matrix products, arithmetic and copies ran while one was open for 0% of the time, Pallas kernels for 3%

profile of v5, /device:TPU:1, one launch (start us, length us, event | category | flops | bytes accessed | tf_op | source)
XLA Modules:
  0.0 89.8 jit_solution(15204043593272380348)
XLA Ops:
  0.6 0.6 pad_add_fusion.1.at_ref
  1.2 8.9 %source_pass.1 = (bf16[1024,128]{1,0:T(8,128)(2,1)}, f32[128,256]{1,0:T(8,128)}, bf16[4,256,256]{2,1,0:T(8,128)(2,1)}, bf16[4,256,256]{2,1,0:T(8,128)(2,1)}) custom-call(s32[2]{0:T(128)} %pad_add_fusion.1.at_ref, bf16[324,8,128]{2,1,0:T(8,128)(2,1)} %bitcast.15, s32[2,8,128]{2,1,0:T(8,128)} %cents_ref.1, bf16[8,256,256]{2,1,0:T(8,128)(2,1)} %targets_ref.1, ...), custom_call_target="tpu_custom_call" | custom-call | flops 4000000000 | bytes 4000000 | tf_op jit(solution)/shard_map/source_pass/pallas_call | solution.py:161
  10.1 6.5 %all-to-all-start = ((bf16[8,128,128]{2,1,0:T(8,128)(2,1)}), bf16[8,128,128]{2,1,0:T(8,128)(2,1)S(1)}, u32[]{:S(2)}, u32[]{:S(2)}) async-start(bf16[8,128,128]{2,1,0:T(8,128)(2,1)} %bitcast.13), calls=%async_computation | async-start | bytes 524288 | tf_op jit(solution)/shard_map/all_to_all | solution.py:419
  16.6 0.0 copy-done.2
  16.6 6.7 %collective-permute-start.1 = (bf16[128,128]{1,0:T(8,128)(2,1)S(1)}, bf16[128,128]{1,0:T(8,128)(2,1)S(1)}, u32[]{:S(2)}, u32[]{:S(2)}) collective-permute-start(bf16[128,128]{1,0:T(8,128)(2,1)S(1)} %bitcast.10), channel_id=1, source_target_pairs={{1,2},{3,4},{5,6},{7,8},{9,10},{11,12},{13,14},{15,16},{17,18},{19... | collective-permute-start | bytes 98312 | tf_op jit(solution)/shard_map/ppermute | solution.py:406
  23.3 0.1 collective-permute-start
  23.4 0.1 collective-permute-start.2
  23.5 0.1 pad_add_fusion.at_ref
  23.6 0.0 copy-done.4
  23.6 1.3 %collective-permute-done.1.linked_ref = bf16[128,128]{1,0:T(8,128)(2,1)S(1)} collective-permute-done((bf16[128,128]{1,0:T(8,128)(2,1)S(1)}, bf16[128,128]{1,0:T(8,128)(2,1)S(1)}, u32[]{:S(2)}, u32[]{:S(2)}) %collective-permute-start.1) | collective-permute-done | bytes 32800 | tf_op jit(solution)/shard_map/ppermute | solution.py:406
  24.9 1.3 %collective-permute-done.paired_ref = bf16[128,128]{1,0:T(8,128)(2,1)S(1)} collective-permute-done((bf16[128,128]{1,0:T(8,128)(2,1)S(1)}, bf16[128,128]{1,0:T(8,128)(2,1)S(1)}, u32[]{:S(2)}, u32[]{:S(2)}) %collective-permute-start) | collective-permute-done | bytes 32800 | tf_op jit(solution)/shard_map/ppermute | solution.py:405
  26.2 0.0 all-to-all-done.parts_ref
  26.2 0.0 copy-done.1
  26.2 1.6 %weight_terms.1 = (bf16[128,128]{1,0:T(8,128)(2,1)S(1)}, bf16[16,32,384]{2,1,0:T(8,128)(2,1)}) custom-call(s32[2]{0:T(128)S(1)} %pad_add_fusion.at_ref, bf16[8,128,128]{2,1,0:T(8,128)(2,1)S(1)} %all-to-all-done.parts_ref, bf16[8,128,128]{2,1,0:T(8,128)(2,1)S(1)} %copy-done.1, bf16[128,128]{1,0:T(8,128)(2,1)S(1)} %collective-permute-done.paired_ref, ...), custom_call_target="tpu_custom_call" | custom-call | tf_op jit(solution)/shard_map/weight_terms/pallas_call | solution.py:220
  27.7 4.9 %all-to-all-start.1 = ((bf16[16,32,384]{2,1,0:T(8,128)(2,1)}), bf16[16,32,384]{2,1,0:T(8,128)(2,1)S(1)}, u32[]{:S(2)}, u32[]{:S(2)}) async-start(bf16[16,32,384]{2,1,0:T(8,128)(2,1)} %get-tuple-element.16), calls=%async_computation.1 | async-start | bytes 786432 | tf_op jit(solution)/shard_map/all_to_all | solution.py:430
  32.6 0.0 collective-permute-done.2
  32.6 0.0 copy-done.3
  32.6 0.1 add_convert_fusion.both_ref
  32.7 7.4 %all-to-all-done.1.parts_ref = bf16[16,32,384]{2,1,0:T(8,128)(2,1)S(1)} async-done(((bf16[16,32,384]{2,1,0:T(8,128)(2,1)}), bf16[16,32,384]{2,1,0:T(8,128)(2,1)S(1)}, u32[]{:S(2)}, u32[]{:S(2)}) %all-to-all-start.1) | async-done | bytes 393248 | tf_op jit(solution)/shard_map/all_to_all | solution.py:430
  40.1 0.1 near_sum.1
  40.2 12.4 %all_to_all.25.parts_ref = bf16[4,304,256]{2,1,0:T(8,128)(2,1)S(1)} all-to-all(bf16[4,304,256]{2,1,0:T(8,128)(2,1)S(1)} %near_sum.1), channel_id=1, replica_groups=mesh['zh'=4,'x'=4,'c'=2,'y'=4,'zl'=2] {'x'}, dimensions={0} | all-to-all | bytes 1245184 | tf_op jit(solution)/shard_map/all_to_all | solution.py:434
  52.6 0.1 x_sum.1
  52.7 15.2 %all_to_all.26.parts_ref = bf16[4,112,256]{2,1,0:T(8,128)(2,1)S(1)} all-to-all(bf16[4,112,256]{2,1,0:T(8,128)(2,1)S(1)} %x_sum.1), channel_id=1, replica_groups=mesh['zh'=4,'x'=4,'c'=2,'y'=4,'zl'=2] {'zh'}, dimensions={0} | all-to-all | bytes 458752 | tf_op jit(solution)/shard_map/all_to_all | solution.py:437
  67.9 0.8 far_sum.1
  68.7 9.4 %all-to-all-start.4 = ((bf16[16,32,384]{2,1,0:T(8,128)(2,1)}), bf16[16,32,384]{2,1,0:T(8,128)(2,1)S(1)}, u32[]{:S(2)}, u32[]{:S(2)}) async-start(bf16[16,32,384]{2,1,0:T(8,128)(2,1)} %get-tuple-element.21), calls=%async_computation.4 | async-start | bytes 786432 | tf_op jit(solution)/shard_map/all_to_all | solution.py:441
  78.0 5.6 %collective-permute-start.4 = (bf16[128,128]{1,0:T(8,128)(2,1)S(1)}, bf16[128,128]{1,0:T(8,128)(2,1)S(1)}, u32[]{:S(2)}, u32[]{:S(2)}) collective-permute-start(bf16[128,128]{1,0:T(8,128)(2,1)S(1)} %get-tuple-element.20.grad_ref), channel_id=1, source_target_pairs={{1,2},{3,4},{5,6},{7,8},{9,10},{11,12},{13,14},{15,16},{17,18},{19... | collective-permute-start | bytes 98312 | tf_op jit(solution)/shard_map/ppermute | solution.py:432
  83.7 0.1 collective-permute-start.3
  83.8 4.1 %collective-permute-done.4.linked_ref = bf16[128,128]{1,0:T(8,128)(2,1)S(1)} collective-permute-done((bf16[128,128]{1,0:T(8,128)(2,1)S(1)}, bf16[128,128]{1,0:T(8,128)(2,1)S(1)}, u32[]{:S(2)}, u32[]{:S(2)}) %collective-permute-start.4) | collective-permute-done | bytes 32800 | tf_op jit(solution)/shard_map/ppermute | solution.py:432
  87.9 0.0 collective-permute-done.3.paired_ref
  87.9 0.9 %act_rows.1 = bf16[1,128,128]{2,1,0:T(8,128)(2,1)} custom-call(s32[1]{0:T(128)} %bitcast.1.at_ref, bf16[128,128]{1,0:T(8,128)(2,1)S(1)} %get-tuple-element.20.grad_ref, bf16[128,128]{1,0:T(8,128)(2,1)S(1)} %collective-permute-done.3.paired_ref, bf16[128,128]{1,0:T(8,128)(2,1)S(1)} %collective-permute-done.4.linked_ref, bf16[3,3,128,128]{3,2,1,0:T(8,128)(2,1)S(1)} %copy-done), custom_call_target="tpu_custom_call" | custom-call | tf_op jit(solution)/shard_map/act_rows/pallas_call | solution.py:317
  88.9 0.0 all-to-all-done.4.totals_ref
  88.9 0.9 unpack.1
  (7 shorter events, 0.0 us)
Async XLA Ops:
  10.1 6.5 %copy-start.2 = (bf16[1,128,128]{2,1,0:T(8,128)(2,1)S(1)}, bf16[1,128,128]{2,1,0:T(8,128)(2,1)}, u32[]{:S(2)}) copy-start(bf16[1,128,128]{2,1,0:T(8,128)(2,1)} %param.10) | copy-start | bytes 98308
  10.1 13.5 %copy-start.4 = (f32[128,256]{1,0:T(8,128)S(1)}, f32[128,256]{1,0:T(8,128)}, u32[]{:S(2)}) copy-start(f32[128,256]{1,0:T(8,128)} %get-tuple-element.15) | copy-start | bytes 393220
  10.1 16.1 %all-to-all-start = ((bf16[8,128,128]{2,1,0:T(8,128)(2,1)}), bf16[8,128,128]{2,1,0:T(8,128)(2,1)S(1)}, u32[]{:S(2)}, u32[]{:S(2)}) async-start(bf16[8,128,128]{2,1,0:T(8,128)(2,1)} %bitcast.13), calls=%async_computation | async-start | bytes 524288 | tf_op jit(solution)/shard_map/all_to_all | solution.py:419
  16.6 9.6 %copy-start.1 = (bf16[8,128,128]{2,1,0:T(8,128)(2,1)S(1)}, bf16[8,128,128]{2,1,0:T(8,128)(2,1)}, u32[]{:S(2)}) copy-start(bf16[8,128,128]{2,1,0:T(8,128)(2,1)} %relu_ref.1) | copy-start | bytes 786436
  16.6 8.3 %collective-permute-start.1 = (bf16[128,128]{1,0:T(8,128)(2,1)S(1)}, bf16[128,128]{1,0:T(8,128)(2,1)S(1)}, u32[]{:S(2)}, u32[]{:S(2)}) collective-permute-start(bf16[128,128]{1,0:T(8,128)(2,1)S(1)} %bitcast.10), channel_id=1, source_target_pairs={{1,2},{3,4},{5,6},{7,8},{9,10},{11,12},{13,14},{15,16},{17,18},{19... | collective-permute-start | bytes 98312 | tf_op jit(solution)/shard_map/ppermute | solution.py:406
  23.3 2.9 %collective-permute-start = (bf16[128,128]{1,0:T(8,128)(2,1)S(1)}, bf16[128,128]{1,0:T(8,128)(2,1)S(1)}, u32[]{:S(2)}, u32[]{:S(2)}) collective-permute-start(bf16[128,128]{1,0:T(8,128)(2,1)S(1)} %bitcast.11), channel_id=1, source_target_pairs={{0,1},{1,0},{2,3},{3,2},{4,5},{5,4},{6,7},{7,6},{8,9},{9,8},{10,11... | collective-permute-start | bytes 98312 | tf_op jit(solution)/shard_map/ppermute | solution.py:405
  23.4 9.2 %collective-permute-start.2 = (bf16[4,256,256]{2,1,0:T(8,128)(2,1)}, bf16[4,256,256]{2,1,0:T(8,128)(2,1)S(1)}, u32[]{:S(2)}, u32[]{:S(2)}) collective-permute-start(bf16[4,256,256]{2,1,0:T(8,128)(2,1)} %get-tuple-element.18), channel_id=1, source_target_pairs={{0,8},{8,0},{1,9},{9,1},{2,10},{10,2},{3,11},{11,3},{4,12},{12,4},... | collective-permute-start | bytes 1572872 | tf_op jit(solution)/shard_map/ppermute | solution.py:424
  27.7 4.9 %copy-start.3 = (bf16[4,256,256]{2,1,0:T(8,128)(2,1)S(1)}, bf16[4,256,256]{2,1,0:T(8,128)(2,1)}, u32[]{:S(2)}) copy-start(bf16[4,256,256]{2,1,0:T(8,128)(2,1)} %get-tuple-element.17) | copy-start | bytes 1572868
  27.7 12.4 %all-to-all-start.1 = ((bf16[16,32,384]{2,1,0:T(8,128)(2,1)}), bf16[16,32,384]{2,1,0:T(8,128)(2,1)S(1)}, u32[]{:S(2)}, u32[]{:S(2)}) async-start(bf16[16,32,384]{2,1,0:T(8,128)(2,1)} %get-tuple-element.16), calls=%async_computation.1 | async-start | bytes 786432 | tf_op jit(solution)/shard_map/all_to_all | solution.py:430
  68.7 19.3 %copy-start = (bf16[3,3,128,128]{3,2,1,0:T(8,128)(2,1)S(1)}, bf16[3,3,128,128]{3,2,1,0:T(8,128)(2,1)}, u32[]{:S(2)}) copy-start(bf16[3,3,128,128]{3,2,1,0:T(8,128)(2,1)} %weight_ref.3) | copy-start | bytes 884740
  68.7 20.2 %all-to-all-start.4 = ((bf16[16,32,384]{2,1,0:T(8,128)(2,1)}), bf16[16,32,384]{2,1,0:T(8,128)(2,1)S(1)}, u32[]{:S(2)}, u32[]{:S(2)}) async-start(bf16[16,32,384]{2,1,0:T(8,128)(2,1)} %get-tuple-element.21), calls=%async_computation.4 | async-start | bytes 786432 | tf_op jit(solution)/shard_map/all_to_all | solution.py:441
  78.0 9.9 %collective-permute-start.4 = (bf16[128,128]{1,0:T(8,128)(2,1)S(1)}, bf16[128,128]{1,0:T(8,128)(2,1)S(1)}, u32[]{:S(2)}, u32[]{:S(2)}) collective-permute-start(bf16[128,128]{1,0:T(8,128)(2,1)S(1)} %get-tuple-element.20.grad_ref), channel_id=1, source_target_pairs={{1,2},{3,4},{5,6},{7,8},{9,10},{11,12},{13,14},{15,16},{17,18},{19... | collective-permute-start | bytes 98312 | tf_op jit(solution)/shard_map/ppermute | solution.py:432
  83.7 4.2 %collective-permute-start.3 = (bf16[128,128]{1,0:T(8,128)(2,1)S(1)}, bf16[128,128]{1,0:T(8,128)(2,1)S(1)}, u32[]{:S(2)}, u32[]{:S(2)}) collective-permute-start(bf16[128,128]{1,0:T(8,128)(2,1)S(1)} %get-tuple-element.20.grad_ref), channel_id=1, source_target_pairs={{0,1},{1,0},{2,3},{3,2},{4,5},{5,4},{6,7},{7,6},{8,9},{9,8},{10,11... | collective-permute-start | bytes 98312 | tf_op jit(solution)/shard_map/ppermute | solution.py:431

commit v6 on v5

--- a/solution.py
+++ b/solution.py
@@ -17,6 +17,7 @@
 
 def source_kernel(
     highs,
+    tgt_devices,
     at_ref,
     grads_ref,
     cents_ref,
@@ -44,6 +45,7 @@
     scale = 1.0 / math.sqrt(width)
     across = (((1,), (1,)), ((), ()))
     down = (((0,), (0,)), ((), ()))
+    row_first = lax.rem(at_ref[0], tgt_devices) * tgt_rows
 
     wide[...] = grads_ref[...].astype(f32)
     for h in range(width // lanes):
@@ -56,7 +58,7 @@
     def build(row_no, corr, at):
         center_y = jnp.broadcast_to(cents_ref[0, row_no : row_no + 1, :], tile)
         center_x = jnp.broadcast_to(cents_ref[1, row_no : row_no + 1, :], tile)
-        ys = at_ref[0] + lax.broadcasted_iota(jnp.int32, tile, 0)
+        ys = row_first + lax.broadcasted_iota(jnp.int32, tile, 0)
         zero = jnp.zeros(tile, f32)
 
         def spread(level):
@@ -136,7 +138,7 @@
     count, block, _ = given_ref.shape
     single = block // highs
     total = ((sums[...] + part) * scale).astype(bf16).reshape(highs, count, 2, single, width)
-    first = at_ref[1] == 0
+    first = lax.rem(lax.div(at_ref[0], tgt_devices), 2) == 0
 
     @pl.when(first)
     def _():
@@ -151,7 +153,9 @@
             kept_ref[k] = total[:, k, 1].reshape(block, width)
 
 
-def source_pass(upstream, centers, target_feats, relu_flat, out_weight, at, highs, lows):
+def source_pass(
+    upstream, centers, target_feats, relu_flat, out_weight, at, highs, lows, tgt_devices
+):
     src_rows, src_width, lookups = upstream.shape
     tgt_rows, tgt_width, width = target_feats.shape
     chans = relu_flat.shape[1]
@@ -159,7 +163,7 @@
     f32, bf16 = jnp.float32, jnp.bfloat16
     part = jax.ShapeDtypeStruct((lows, cells // lows // 2, width), bf16)
     return pl.pallas_call(
-        functools.partial(source_kernel, highs),
+        functools.partial(source_kernel, highs, tgt_devices),
         out_shape=(
             jax.ShapeDtypeStruct((sources, chans), bf16),
             jax.ShapeDtypeStruct((chans, width), f32),
@@ -193,16 +197,24 @@
     return left, wide, right
 
 
-def terms_kernel(at_ref, parts_ref, relu_ref, paired_ref, own_ref, linked_ref, out_ref, grad_ref, terms_ref):
+def neighbours(row_total, at_ref, paired_ref, linked_ref):
+    row = at_ref[0]
+    even = lax.rem(row, 2) == 0
+    paired, linked = paired_ref[...], linked_ref[...]
+    zero = jnp.zeros_like(paired)
+    before = jnp.where(row == 0, zero, jnp.where(even, linked, paired))
+    after = jnp.where(row == row_total - 1, zero, jnp.where(even, paired, linked))
+    return before, after
+
+
+def terms_kernel(row_total, at_ref, parts_ref, relu_ref, paired_ref, own_ref, linked_ref, out_ref, grad_ref, terms_ref):
     total = parts_ref[0].astype(jnp.float32)
     for k in range(1, parts_ref.shape[0]):
         total += parts_ref[k].astype(jnp.float32)
     grad = jnp.where(relu_ref[0].astype(jnp.float32) > 0, total, 0.0).astype(jnp.bfloat16)
     grad_ref[...] = grad
     near_grad = jnp.concatenate(shifted(grad.astype(jnp.float32)), axis=1).astype(jnp.bfloat16)
-    even = at_ref[1] == 0
-    before = jnp.where(even, linked_ref[...], paired_ref[...])
-    after = jnp.where(even, paired_ref[...], linked_ref[...])
+    before, after = neighbours(row_total, at_ref, paired_ref, linked_ref)
     near_input = jnp.concatenate([before, own_ref[...], after], axis=1)
     conv = lax.dot_general(
         near_input, near_grad, (((0,), (0,)), ((), ())), preferred_element_type=jnp.float32
@@ -212,13 +224,13 @@
     terms_ref[...] = jnp.concatenate([conv, out_ref[...]], axis=1).astype(jnp.bfloat16)
 
 
-def weight_terms(parts, post_relu, inputs, out_term, tgt_at, odd, near):
+def weight_terms(parts, post_relu, inputs, out_term, row_at, row_total, near):
     count, src_width, chans = parts.shape
     whole = lambda *shape: pl.BlockSpec(shape, lambda r, f: (0,) * len(shape))
     across = 3 * chans
     down = (across + chans) // near
     return pl.pallas_call(
-        terms_kernel,
+        functools.partial(terms_kernel, row_total),
         out_shape=(
             jax.ShapeDtypeStruct((src_width, chans), jnp.bfloat16),
             jax.ShapeDtypeStruct((near, down, across), jnp.bfloat16),
@@ -228,7 +240,7 @@
             grid=(1,),
             in_specs=[
                 whole(count, src_width, chans),
-                pl.BlockSpec((1, src_width, chans), lambda r, f: (f[0], 0, 0)),
+                pl.BlockSpec((1, src_width, chans), lambda r, f: (lax.rem(f[0], count), 0, 0)),
                 whole(src_width, chans),
                 whole(src_width, chans),
                 whole(src_width, chans),
@@ -238,7 +250,7 @@
         ),
         compiler_params=pltpu.CompilerParams(vmem_limit_bytes=8 * 2**20),
         name="weight_terms",
-    )(jnp.stack([tgt_at, odd]), parts, post_relu, *inputs, out_term)
+    )(row_at, parts, post_relu, *inputs, out_term)
 
 
 def near_sum_kernel(parts_ref, both_ref, joint_ref):
@@ -294,10 +306,8 @@
     )(parts)
 
 
-def act_kernel(at_ref, grad_ref, paired_ref, linked_ref, weight_ref, act_ref):
-    even = at_ref[0] == 0
-    before = jnp.where(even, linked_ref[...], paired_ref[...])
-    after = jnp.where(even, paired_ref[...], linked_ref[...])
+def act_kernel(row_total, at_ref, grad_ref, paired_ref, linked_ref, weight_ref, act_ref):
+    before, after = neighbours(row_total, at_ref, paired_ref, linked_ref)
     total = jnp.zeros(grad_ref.shape, jnp.float32)
     for p, row in enumerate((after, grad_ref[...], before)):
         for q, tap in enumerate(shifted(row.astype(jnp.float32))):
@@ -310,12 +320,12 @@
     act_ref[0] = total.astype(jnp.bfloat16)
 
 
-def act_rows(block_grad, paired, linked, conv_weight, odd):
+def act_rows(block_grad, paired, linked, conv_weight, row_at, row_total):
     whole = lambda *shape: pl.BlockSpec(shape, lambda r, f: (0,) * len(shape))
     cols, chans = block_grad.shape
     row = whole(cols, chans)
     return pl.pallas_call(
-        act_kernel,
+        functools.partial(act_kernel, row_total),
         out_shape=jax.ShapeDtypeStruct((1, cols, chans), jnp.bfloat16),
         grid_spec=pltpu.PrefetchScalarGridSpec(
             num_scalar_prefetch=1,
@@ -325,7 +335,7 @@
         ),
         compiler_params=pltpu.CompilerParams(vmem_limit_bytes=8 * 2**20),
         name="act_rows",
-    )(odd.reshape(1), block_grad, paired, linked, conv_weight)
+    )(row_at, block_grad, paired, linked, conv_weight)
 
 
 def far_sum_kernel(scale, parts_ref, tgt_ref, shared_ref, left, right):
@@ -391,15 +401,13 @@
     src_rows, src_width, _ = upstream.shape
     tgt_rows, tgt_width, width = target_feats.shape
     chans = post_relu.shape[2]
-    src_devices = lax.axis_size(SRC)
+    src_devices, tgt_devices = lax.axis_size(SRC), lax.axis_size(TGT)
     row_total = src_devices * src_rows
     near, highs, lows = lax.axis_size(NEAR), lax.axis_size("zh"), lax.axis_size("x")
-    tgt_at = lax.axis_index(TGT)
-    core_at = lax.axis_index("c")
-    odd = lax.axis_index("zl")
+    row_at = lax.axis_index(ALL).reshape(1)
 
     pairs = [(i, i ^ 1) for i in range(row_total)]
-    links = [(i, i + 1) for i in range(1, row_total - 1, 2)]
+    links = [(i, (i + 1) % row_total) for i in range(1, row_total, 2)]
     links += [(j, i) for i, j in links]
     own_input = conv_input[0]
     input_paired = lax.ppermute(own_input, ALL, pairs)
@@ -412,9 +420,10 @@
         target_feats,
         relu_flat,
         out_weight,
-        jnp.stack([tgt_at * tgt_rows, core_at]),
+        row_at,
         highs,
         lows,
+        tgt_devices,
     )
     hidden = lax.all_to_all(hidden.reshape(src_rows, src_width, chans), TGT, 0, 0)
 
@@ -425,7 +434,7 @@
     both = (kept.astype(jnp.float32) + taken.astype(jnp.float32)).astype(jnp.bfloat16)
 
     block_grad, terms = weight_terms(
-        hidden, post_relu, (input_paired, own_input, input_linked), out_term, tgt_at, odd, near
+        hidden, post_relu, (input_paired, own_input, input_linked), out_term, row_at, row_total, near
     )
     terms = lax.all_to_all(terms, NEAR, 0, 0)
     grad_paired = lax.ppermute(block_grad, ALL, pairs)
@@ -439,7 +448,9 @@
         joint, tgt_rows, cols, near, terms.shape[1], terms.shape[2], 1.0 / row_total
     )
     pieces = lax.all_to_all(pieces, NEAR, 0, 0)
-    act_grad = act_rows(block_grad, grad_paired, grad_linked, conv_weight, odd)
+    act_grad = act_rows(
+        block_grad, grad_paired, grad_linked, conv_weight, row_at, row_total
+    )
     conv_total, out_total = unpack(pieces, chans, width)
     return (tgt_grad, act_grad, out_total, conv_total)
 

time: 90.3 us -> 88.7 us (0.982)
  blocking collectives: 27.6 us -> 22.7 us
  waiting for transfers between devices: 14.1 us -> 17.4 us
  starting transfers between devices: 33.4 us -> 34.6 us
    all_to_all x1, starting transfers between devices: 4.87 us -> 10.2 us  [body(): terms = lax.all_to_all(terms, NEAR, 0, 0)]
    all_to_all x1, blocking collectives: 15.2 us -> 11.4 us  [body(): joint = lax.all_to_all(joint, 'zh', 0, 0)]
    ppermute x1, starting transfers between devices: 6.72 us -> 3.75 us  [body(): input_linked = lax.ppermute(own_input, ALL, links)]
    ppermute x1, waiting for transfers between devices: 1.28 us -> 3.78 us  [body(): input_linked = lax.ppermute(own_input, ALL, links)]
    ppermute x1, waiting for transfers between devices: 4.14 us -> 6.14 us  [body(): grad_linked = lax.ppermute(block_grad, ALL, links)]
    ppermute x1, starting transfers between devices: 5.64 us -> 3.74 us  [body(): grad_linked = lax.ppermute(block_grad, ALL, links)]
    ppermute x1, waiting for transfers between devices: 1.27 us -> 0.01 us  [body(): input_paired = lax.ppermute(own_input, ALL, pairs)]
    all_to_all x1, blocking collectives: 12.4 us -> 11.3 us  [body(): joint = lax.all_to_all(joint, 'x', 0, 0)]
  transfers between devices with their start and end apart: 8 -> 8, of which waited for: 4 -> 3; matrix products, arithmetic and copies ran while one was open for 0% -> 0% of each run, Pallas kernels for 3% -> 2%
where the time goes in v6:
time: 88.7 us; the launch traced here: 88.2 us
  starting transfers between devices  34.6 us (39%)
  blocking collectives  22.7 us (26%)
  waiting for transfers between devices  17.4 us (20%)
  Pallas kernels  12.7 us (14%)
    all_to_all x1, blocking collectives, body(): joint = lax.all_to_all(joint, 'zh', 0, 0)  11.4 us
    all_to_all x1, blocking collectives, body(): joint = lax.all_to_all(joint, 'x', 0, 0)  11.3 us
    all_to_all x1, starting transfers between devices, body(): terms = lax.all_to_all(terms, NEAR, 0, 0)  10.2 us
    all_to_all x1, starting transfers between devices, body(): pieces = lax.all_to_all(pieces, NEAR, 0, 0)  9.36 us
    pallas_call x1, Pallas kernels, source_pass(): pl.pallas_call(functools.partial(source_kernel, highs, tgt_devices), out_...  8.82 us
    all_to_all x1, waiting for transfers between devices, body(): terms = lax.all_to_all(terms, NEAR, 0, 0)  7.45 us
    all_to_all x1, starting transfers between devices, body(): lax.all_to_all(hidden.reshape(src_rows, src_width, chans), TGT, 0, 0)  6.49 us
    ppermute x1, waiting for transfers between devices, body(): grad_linked = lax.ppermute(block_grad, ALL, links)  6.14 us
  transfers between devices with their start and end apart: 8, of which 3 were waited for; matrix products, arithmetic and copies ran while one was open for 0% of the time, Pallas kernels for 2%

profile of v6, /device:TPU:1, one launch (start us, length us, event | category | flops | bytes accessed | tf_op | source)
XLA Modules:
  0.0 88.2 jit_solution(16587552810302427921)
XLA Ops:
  0.6 8.8 %source_pass.1 = (bf16[1024,128]{1,0:T(8,128)(2,1)}, f32[128,256]{1,0:T(8,128)}, bf16[4,256,256]{2,1,0:T(8,128)(2,1)}, bf16[4,256,256]{2,1,0:T(8,128)(2,1)}) custom-call(s32[1]{0:T(128)} %bitcast.at_ref, bf16[324,8,128]{2,1,0:T(8,128)(2,1)} %bitcast.12, s32[2,8,128]{2,1,0:T(8,128)} %cents_ref.1, bf16[8,256,256]{2,1,0:T(8,128)(2,1)} %targets_ref.1, ...), custom_call_target="tpu_custom_call" | custom-call | flops 4000000000 | bytes 4000000 | tf_op jit(solution)/shard_map/source_pass/pallas_call | solution.py:165
  9.5 0.0 copy-start.2
  9.5 6.5 %all-to-all-start = ((bf16[8,128,128]{2,1,0:T(8,128)(2,1)}), bf16[8,128,128]{2,1,0:T(8,128)(2,1)S(1)}, u32[]{:S(2)}, u32[]{:S(2)}) async-start(bf16[8,128,128]{2,1,0:T(8,128)(2,1)} %bitcast.10), calls=%async_computation | async-start | bytes 524288 | tf_op jit(solution)/shard_map/all_to_all | solution.py:428
  16.0 1.0 %collective-permute-start.2 = (bf16[4,256,256]{2,1,0:T(8,128)(2,1)}, bf16[4,256,256]{2,1,0:T(8,128)(2,1)S(1)}, u32[]{:S(2)}, u32[]{:S(2)}) collective-permute-start(bf16[4,256,256]{2,1,0:T(8,128)(2,1)} %get-tuple-element.18), channel_id=1, source_target_pairs={{0,8},{8,0},{1,9},{9,1},{2,10},{10,2},{3,11},{11,3},{4,12},{12,4},... | collective-permute-start | bytes 1572872 | tf_op jit(solution)/shard_map/ppermute | solution.py:433
  17.0 0.0 copy-done.2
  17.0 3.7 %collective-permute-start.1 = (bf16[128,128]{1,0:T(8,128)(2,1)S(1)}, bf16[128,128]{1,0:T(8,128)(2,1)S(1)}, u32[]{:S(2)}, u32[]{:S(2)}) collective-permute-start(bf16[128,128]{1,0:T(8,128)(2,1)S(1)} %bitcast.7), channel_id=1, source_target_pairs={{1,2},{3,4},{5,6},{7,8},{9,10},{11,12},{13,14},{15,16},{17,18},{19... | collective-permute-start | bytes 98312 | tf_op jit(solution)/shard_map/ppermute | solution.py:414
  20.8 0.0 collective-permute-start
  20.8 0.0 copy-done.4
  20.8 3.8 %collective-permute-done.1.linked_ref = bf16[128,128]{1,0:T(8,128)(2,1)S(1)} collective-permute-done((bf16[128,128]{1,0:T(8,128)(2,1)S(1)}, bf16[128,128]{1,0:T(8,128)(2,1)S(1)}, u32[]{:S(2)}, u32[]{:S(2)}) %collective-permute-start.1) | collective-permute-done | bytes 32800 | tf_op jit(solution)/shard_map/ppermute | solution.py:414
  24.6 0.0 collective-permute-done.paired_ref
  24.6 0.0 all-to-all-done.parts_ref
  24.6 0.0 copy-done.1
  24.6 1.0 %weight_terms.1 = (bf16[128,128]{1,0:T(8,128)(2,1)S(1)}, bf16[16,32,384]{2,1,0:T(8,128)(2,1)}) custom-call(s32[1]{0:T(128)} %bitcast.at_ref, bf16[8,128,128]{2,1,0:T(8,128)(2,1)S(1)} %all-to-all-done.parts_ref, bf16[8,128,128]{2,1,0:T(8,128)(2,1)S(1)} %copy-done.1, bf16[128,128]{1,0:T(8,128)(2,1)S(1)} %collective-permute-done.paired_ref, ...), custom_call_target="tpu_custom_call" | custom-call | tf_op jit(solution)/shard_map/weight_terms/pallas_call | solution.py:232
  25.6 10.2 %all-to-all-start.1 = ((bf16[16,32,384]{2,1,0:T(8,128)(2,1)}), bf16[16,32,384]{2,1,0:T(8,128)(2,1)S(1)}, u32[]{:S(2)}, u32[]{:S(2)}) async-start(bf16[16,32,384]{2,1,0:T(8,128)(2,1)} %get-tuple-element.16), calls=%async_computation.1 | async-start | bytes 786432 | tf_op jit(solution)/shard_map/all_to_all | solution.py:439
  35.8 0.0 collective-permute-done.2
  35.8 0.0 copy-done.3
  35.8 0.1 add_convert_fusion.both_ref
  35.9 7.5 %all-to-all-done.1.parts_ref = bf16[16,32,384]{2,1,0:T(8,128)(2,1)S(1)} async-done(((bf16[16,32,384]{2,1,0:T(8,128)(2,1)}), bf16[16,32,384]{2,1,0:T(8,128)(2,1)S(1)}, u32[]{:S(2)}, u32[]{:S(2)}) %all-to-all-start.1) | async-done | bytes 393248 | tf_op jit(solution)/shard_map/all_to_all | solution.py:439
  43.4 0.1 near_sum.1
  43.4 11.3 %all_to_all.25.parts_ref = bf16[4,304,256]{2,1,0:T(8,128)(2,1)S(1)} all-to-all(bf16[4,304,256]{2,1,0:T(8,128)(2,1)S(1)} %near_sum.1), channel_id=1, replica_groups=mesh['zh'=4,'x'=4,'c'=2,'y'=4,'zl'=2] {'x'}, dimensions={0} | all-to-all | bytes 1245184 | tf_op jit(solution)/shard_map/all_to_all | solution.py:443
  54.8 0.1 x_sum.1
  54.8 11.4 %all_to_all.26.parts_ref = bf16[4,112,256]{2,1,0:T(8,128)(2,1)S(1)} all-to-all(bf16[4,112,256]{2,1,0:T(8,128)(2,1)S(1)} %x_sum.1), channel_id=1, replica_groups=mesh['zh'=4,'x'=4,'c'=2,'y'=4,'zl'=2] {'zh'}, dimensions={0} | all-to-all | bytes 458752 | tf_op jit(solution)/shard_map/all_to_all | solution.py:446
  66.3 0.8 far_sum.1
  67.1 9.4 %all-to-all-start.4 = ((bf16[16,32,384]{2,1,0:T(8,128)(2,1)}), bf16[16,32,384]{2,1,0:T(8,128)(2,1)S(1)}, u32[]{:S(2)}, u32[]{:S(2)}) async-start(bf16[16,32,384]{2,1,0:T(8,128)(2,1)} %get-tuple-element.21), calls=%async_computation.4 | async-start | bytes 786432 | tf_op jit(solution)/shard_map/all_to_all | solution.py:450
  76.4 3.7 %collective-permute-start.4 = (bf16[128,128]{1,0:T(8,128)(2,1)S(1)}, bf16[128,128]{1,0:T(8,128)(2,1)S(1)}, u32[]{:S(2)}, u32[]{:S(2)}) collective-permute-start(bf16[128,128]{1,0:T(8,128)(2,1)S(1)} %get-tuple-element.20.grad_ref), channel_id=1, source_target_pairs={{1,2},{3,4},{5,6},{7,8},{9,10},{11,12},{13,14},{15,16},{17,18},{19... | collective-permute-start | bytes 98312 | tf_op jit(solution)/shard_map/ppermute | solution.py:441
  80.2 0.0 collective-permute-start.3
  80.2 6.1 %collective-permute-done.4.linked_ref = bf16[128,128]{1,0:T(8,128)(2,1)S(1)} collective-permute-done((bf16[128,128]{1,0:T(8,128)(2,1)S(1)}, bf16[128,128]{1,0:T(8,128)(2,1)S(1)}, u32[]{:S(2)}, u32[]{:S(2)}) %collective-permute-start.4) | collective-permute-done | bytes 32800 | tf_op jit(solution)/shard_map/ppermute | solution.py:441
  86.3 0.0 collective-permute-done.3.paired_ref
  86.3 0.0 copy-done
  86.3 1.0 %act_rows.1 = bf16[1,128,128]{2,1,0:T(8,128)(2,1)} custom-call(s32[1]{0:T(128)} %bitcast.at_ref, bf16[128,128]{1,0:T(8,128)(2,1)S(1)} %get-tuple-element.20.grad_ref, bf16[128,128]{1,0:T(8,128)(2,1)S(1)} %collective-permute-done.3.paired_ref, bf16[128,128]{1,0:T(8,128)(2,1)S(1)} %collective-permute-done.4.linked_ref, bf16[3,3,128,128]{3,2,1,0:T(8,128)(2,1)S(1)} %copy-done), custom_call_target="tpu_custom_call" | custom-call | tf_op jit(solution)/shard_map/act_rows/pallas_call | solution.py:327
  87.3 0.0 all-to-all-done.4.totals_ref
  87.3 0.9 %unpack.1 = (f32[3,3,128,128]{3,2,1,0:T(8,128)}, f32[128,256]{1,0:T(8,128)}) custom-call(bf16[16,32,384]{2,1,0:T(8,128)(2,1)S(1)} %all-to-all-done.4.totals_ref), custom_call_target="tpu_custom_call" | custom-call | tf_op jit(solution)/shard_map/unpack/pallas_call | solution.py:389
  (5 shorter events, 0.0 us)
Async XLA Ops:
  9.5 7.5 %copy-start.2 = (bf16[1,128,128]{2,1,0:T(8,128)(2,1)S(1)}, bf16[1,128,128]{2,1,0:T(8,128)(2,1)}, u32[]{:S(2)}) copy-start(bf16[1,128,128]{2,1,0:T(8,128)(2,1)} %param.10) | copy-start | bytes 98308
  9.5 11.3 %copy-start.4 = (f32[128,256]{1,0:T(8,128)S(1)}, f32[128,256]{1,0:T(8,128)}, u32[]{:S(2)}) copy-start(f32[128,256]{1,0:T(8,128)} %get-tuple-element.15) | copy-start | bytes 393220
  9.5 15.1 %all-to-all-start = ((bf16[8,128,128]{2,1,0:T(8,128)(2,1)}), bf16[8,128,128]{2,1,0:T(8,128)(2,1)S(1)}, u32[]{:S(2)}, u32[]{:S(2)}) async-start(bf16[8,128,128]{2,1,0:T(8,128)(2,1)} %bitcast.10), calls=%async_computation | async-start | bytes 524288 | tf_op jit(solution)/shard_map/all_to_all | solution.py:428
  16.0 8.6 %copy-start.1 = (bf16[8,128,128]{2,1,0:T(8,128)(2,1)S(1)}, bf16[8,128,128]{2,1,0:T(8,128)(2,1)}, u32[]{:S(2)}) copy-start(bf16[8,128,128]{2,1,0:T(8,128)(2,1)} %relu_ref.1) | copy-start | bytes 786436
  16.0 19.8 %collective-permute-start.2 = (bf16[4,256,256]{2,1,0:T(8,128)(2,1)}, bf16[4,256,256]{2,1,0:T(8,128)(2,1)S(1)}, u32[]{:S(2)}, u32[]{:S(2)}) collective-permute-start(bf16[4,256,256]{2,1,0:T(8,128)(2,1)} %get-tuple-element.18), channel_id=1, source_target_pairs={{0,8},{8,0},{1,9},{9,1},{2,10},{10,2},{3,11},{11,3},{4,12},{12,4},... | collective-permute-start | bytes 1572872 | tf_op jit(solution)/shard_map/ppermute | solution.py:433
  17.0 7.6 %collective-permute-start.1 = (bf16[128,128]{1,0:T(8,128)(2,1)S(1)}, bf16[128,128]{1,0:T(8,128)(2,1)S(1)}, u32[]{:S(2)}, u32[]{:S(2)}) collective-permute-start(bf16[128,128]{1,0:T(8,128)(2,1)S(1)} %bitcast.7), channel_id=1, source_target_pairs={{1,2},{3,4},{5,6},{7,8},{9,10},{11,12},{13,14},{15,16},{17,18},{19... | collective-permute-start | bytes 98312 | tf_op jit(solution)/shard_map/ppermute | solution.py:414
  20.8 3.8 %collective-permute-start = (bf16[128,128]{1,0:T(8,128)(2,1)S(1)}, bf16[128,128]{1,0:T(8,128)(2,1)S(1)}, u32[]{:S(2)}, u32[]{:S(2)}) collective-permute-start(bf16[128,128]{1,0:T(8,128)(2,1)S(1)} %bitcast.8), channel_id=1, source_target_pairs={{0,1},{1,0},{2,3},{3,2},{4,5},{5,4},{6,7},{7,6},{8,9},{9,8},{10,11... | collective-permute-start | bytes 98312 | tf_op jit(solution)/shard_map/ppermute | solution.py:413
  25.6 10.2 %copy-start.3 = (bf16[4,256,256]{2,1,0:T(8,128)(2,1)S(1)}, bf16[4,256,256]{2,1,0:T(8,128)(2,1)}, u32[]{:S(2)}) copy-start(bf16[4,256,256]{2,1,0:T(8,128)(2,1)} %get-tuple-element.17) | copy-start | bytes 1572868
  25.6 17.8 %all-to-all-start.1 = ((bf16[16,32,384]{2,1,0:T(8,128)(2,1)}), bf16[16,32,384]{2,1,0:T(8,128)(2,1)S(1)}, u32[]{:S(2)}, u32[]{:S(2)}) async-start(bf16[16,32,384]{2,1,0:T(8,128)(2,1)} %get-tuple-element.16), calls=%async_computation.1 | async-start | bytes 786432 | tf_op jit(solution)/shard_map/all_to_all | solution.py:439
  67.1 19.3 %copy-start = (bf16[3,3,128,128]{3,2,1,0:T(8,128)(2,1)S(1)}, bf16[3,3,128,128]{3,2,1,0:T(8,128)(2,1)}, u32[]{:S(2)}) copy-start(bf16[3,3,128,128]{3,2,1,0:T(8,128)(2,1)} %weight_ref.3) | copy-start | bytes 884740
  67.1 20.2 %all-to-all-start.4 = ((bf16[16,32,384]{2,1,0:T(8,128)(2,1)}), bf16[16,32,384]{2,1,0:T(8,128)(2,1)S(1)}, u32[]{:S(2)}, u32[]{:S(2)}) async-start(bf16[16,32,384]{2,1,0:T(8,128)(2,1)} %get-tuple-element.21), calls=%async_computation.4 | async-start | bytes 786432 | tf_op jit(solution)/shard_map/all_to_all | solution.py:450
  76.4 9.9 %collective-permute-start.4 = (bf16[128,128]{1,0:T(8,128)(2,1)S(1)}, bf16[128,128]{1,0:T(8,128)(2,1)S(1)}, u32[]{:S(2)}, u32[]{:S(2)}) collective-permute-start(bf16[128,128]{1,0:T(8,128)(2,1)S(1)} %get-tuple-element.20.grad_ref), channel_id=1, source_target_pairs={{1,2},{3,4},{5,6},{7,8},{9,10},{11,12},{13,14},{15,16},{17,18},{19... | collective-permute-start | bytes 98312 | tf_op jit(solution)/shard_map/ppermute | solution.py:441
  80.2 6.1 %collective-permute-start.3 = (bf16[128,128]{1,0:T(8,128)(2,1)S(1)}, bf16[128,128]{1,0:T(8,128)(2,1)S(1)}, u32[]{:S(2)}, u32[]{:S(2)}) collective-permute-start(bf16[128,128]{1,0:T(8,128)(2,1)S(1)} %get-tuple-element.20.grad_ref), channel_id=1, source_target_pairs={{0,1},{1,0},{2,3},{3,2},{4,5},{5,4},{6,7},{7,6},{8,9},{9,8},{10,11... | collective-permute-start | bytes 98312 | tf_op jit(solution)/shard_map/ppermute | solution.py:440
